TPU v7x, 32 devices: a whole 2x2x4 slice. The times are simulated.
32 devices in a mesh: grp: 2 (over y), ctx: 4 (over z), head: 2 (over x), rep: 2 (over core).
Axes of the slice: x: 2, y: 2, z: 4, core: 2. Of those that a mesh axis runs over, the one named last changes fastest.
Arguments:
- tokens: bfloat16 [4096, 2048], P(('grp', 'ctx', 'rep')), parts along dimension 0, may hold values from -6 to 6
- doc_ids: int32 [4096], P(('grp', 'ctx', 'rep')), parts along dimension 0, may hold values from 0 to 3, never falling along the last dimension, each value on 1 to 1024 neighbouring positions
- dest_rows: int32 [4096], P(('grp', 'ctx', 'rep')), parts along dimension 0, may hold values from 0 to 2047, as said below
- w_query: bfloat16 [2048, 4096], P(None, 'head'), may hold values from -0.125 to 0.125
- w_key: bfloat16 [2048, 512], P(None, 'head'), may hold values from -0.125 to 0.125
- w_value: bfloat16 [2048, 512], P(None, 'head'), may hold values from -0.125 to 0.125
- w_out: bfloat16 [4096, 2048], P('head'), may hold values from -0.09375 to 0.09375
Outputs:
- layer_out: bfloat16 [4096, 2048], P(('grp', 'ctx', 'rep'), 'head'), parts along dimension 0
There are 2 independent parts, one for each index of `grp`. A program takes and returns all parts, laid end to end along the dimension named above; an argument that names none is the same for every part. Nothing has to cross between parts.
Inputs may be any that keep to these rules, and one draw needn't show every extreme that they name: dest_rows is a permutation of the 2048 rows; owner o holds rows o * 256 to (o + 1) * 256 - 1. The 256 tokens of one device go in runs of 16 consecutive tokens, a run to one owner; each device sends 3 * 16 = 48 tokens to half of the owners and 16 to each of the others. `doc_ids`: document number of each token, never falling along the sequence.
All inputs are finite; a program needn't handle non-finite values.
Results may differ from a plain program's by a relative error of at most 0.0078.
Values may be sent and summed in bfloat16 or wider, within the bound.
No kernel may reach another device: no remote copies, remote signals or barrier semaphores. Data moves between devices by JAX's collectives and lax.ppermute only.
A program may use at most 128 MiB of HBM per device.

v0:
```python
import math

import jax
import jax.numpy as jnp
from jax import lax
from jax.sharding import PartitionSpec as P

HD = 128


THETA = 1000000.0
EPSILON = 1e-06


def rope_tables(positions, head_dim):
    inverse = jnp.power(THETA, -(jnp.arange(0, head_dim, 2, dtype=jnp.float32) / head_dim))
    angles = positions.astype(jnp.float32)[:, None] * inverse[None, :]
    cosine = jnp.cos(angles)
    sine = jnp.sin(angles)
    return (jnp.concatenate([cosine, cosine], -1), jnp.concatenate([sine, sine], -1))


def project_heads(tokens, weight, positions, head_dim):
    flat = jnp.dot(tokens, weight, preferred_element_type=jnp.float32)
    heads = flat.reshape(flat.shape[0], -1, head_dim)
    normed = heads * lax.rsqrt(jnp.mean(heads * heads, axis=-1, keepdims=True) + EPSILON)
    cosine, sine = rope_tables(positions, head_dim)
    half_dim = head_dim // 2
    rotated = jnp.concatenate([-normed[..., half_dim:], normed[..., :half_dim]], -1)
    return (normed * cosine[:, None, :] + rotated * sine[:, None, :]).astype(jnp.bfloat16)


def route_rows(dest_rows, tok_rows):
    owners = lax.axis_size(("ctx", "rep"))
    capacity = 3 * (tok_rows // (2 * owners))
    owner_of = dest_rows // tok_rows
    slot_in = dest_rows - owner_of * tok_rows
    onehot = (owner_of[:, None] == jnp.arange(owners, dtype=jnp.int32)[None, :]).astype(jnp.int32)
    order_in = jnp.sum((jnp.cumsum(onehot, axis=0) - onehot) * onehot, axis=1)
    return (owner_of * capacity + order_in, slot_in, owners * capacity)


def scatter_rows(values, buffer_pos, buffer_len, filler):
    empty = jnp.full((buffer_len,) + values.shape[1:], filler, values.dtype)
    return empty.at[buffer_pos].set(values)


def place_rows(values, slots, tok_rows):
    target = jnp.where(slots >= 0, slots, tok_rows)
    empty = jnp.zeros((tok_rows,) + values.shape[1:], values.dtype)
    return empty.at[target].set(values, mode="drop")


def attend(queries, query_pos, query_seg, keys_in, values_in, key_seg):
    rows_all, kv_heads, groups, head_dim = queries.shape
    score_scale = 1.0 / math.sqrt(head_dim)

    def add_block(totals, key_blk, value_blk, seg_blk, offset):
        key_pos = offset + jnp.arange(key_blk.shape[0], dtype=jnp.int32)
        visible = (seg_blk[None, :] == query_seg[:, None]) & (
            key_pos[None, :] <= query_pos[:, None]
        )

        def compute(current):
            scores = (
                jnp.einsum("rkgd,nkd->rkgn", queries, key_blk, preferred_element_type=jnp.float32)
                * score_scale
            )
            weights = jnp.where(visible[:, None, None, :], jnp.exp(scores), 0.0)
            numer = current[0] + jnp.einsum(
                "rkgn,nkd->rkgd",
                weights.astype(jnp.bfloat16),
                value_blk,
                preferred_element_type=jnp.float32,
            )
            return (numer, current[1] + jnp.sum(weights, axis=-1))

        return lax.cond(jnp.any(visible), compute, lambda current: current, totals)

    initial = (
        jnp.zeros((rows_all, kv_heads, groups, head_dim), jnp.float32),
        jnp.zeros((rows_all, kv_heads, groups), jnp.float32),
    )
    paired = (
        lax.all_gather(keys_in, "rep", axis=0, tiled=True),
        lax.all_gather(values_in, "rep", axis=0, tiled=True),
        lax.all_gather(key_seg, "rep", axis=0, tiled=True),
    )
    key_part = lax.all_gather(paired[0], "ctx", axis=0, tiled=True)
    value_part = lax.all_gather(paired[1], "ctx", axis=0, tiled=True)
    seg_part = lax.all_gather(paired[2], "ctx", axis=0, tiled=True)
    length = key_part.shape[0]
    block_rows = 512
    blocks = length // block_rows

    def loop_body(counter, current):
        first_row = counter * block_rows
        return add_block(
            current,
            lax.dynamic_slice_in_dim(key_part, first_row, block_rows, 0),
            lax.dynamic_slice_in_dim(value_part, first_row, block_rows, 0),
            lax.dynamic_slice_in_dim(seg_part, first_row, block_rows, 0),
            first_row,
        )

    numer, total = lax.fori_loop(0, blocks, loop_body, initial)
    result = numer / total[..., None]
    return result.astype(jnp.bfloat16).reshape(rows_all, kv_heads * groups * head_dim)


def local(tokens, doc_ids, dest_rows, w_query, w_key, w_value, w_out):
    tok_rows = tokens.shape[0]
    head_dim = HD
    positions = lax.axis_index(("ctx", "rep")) * tok_rows + jnp.arange(tok_rows, dtype=jnp.int32)
    queries = project_heads(tokens, w_query, positions, head_dim)
    keys_local = project_heads(tokens, w_key, positions, head_dim)
    kv_heads = keys_local.shape[1]
    groups = queries.shape[1] // kv_heads
    values_local = jnp.dot(tokens, w_value, preferred_element_type=jnp.float32).astype(jnp.bfloat16)
    values_local = values_local.reshape(tok_rows, kv_heads, head_dim)
    buffer_pos, slot_in, buffer_len = route_rows(dest_rows, tok_rows)
    query_flat = queries.reshape(tok_rows, kv_heads * groups * head_dim)
    outgoing = (
        scatter_rows(query_flat, buffer_pos, buffer_len, 0),
        scatter_rows(slot_in, buffer_pos, buffer_len, -1),
        scatter_rows(positions, buffer_pos, buffer_len, 0),
        scatter_rows(doc_ids, buffer_pos, buffer_len, 0),
    )
    got_query, got_slot, got_pos, got_seg = (
        lax.all_to_all(outgoing[0], ("ctx", "rep"), split_axis=0, concat_axis=0, tiled=True),
        lax.all_to_all(outgoing[1], ("ctx", "rep"), split_axis=0, concat_axis=0, tiled=True),
        lax.all_to_all(outgoing[2], ("ctx", "rep"), split_axis=0, concat_axis=0, tiled=True),
        lax.all_to_all(outgoing[3], ("ctx", "rep"), split_axis=0, concat_axis=0, tiled=True),
    )
    own_query = place_rows(got_query, got_slot, tok_rows).reshape(
        tok_rows, kv_heads, groups, head_dim
    )
    own_pos = place_rows(got_pos, got_slot, tok_rows)
    own_seg = place_rows(got_seg, got_slot, tok_rows)
    attended = attend(own_query, own_pos, own_seg, keys_local, values_local, doc_ids)
    partial_out = jnp.dot(attended, w_out, preferred_element_type=jnp.float32).astype(jnp.bfloat16)
    return (
        lax.psum_scatter(partial_out, "head", scatter_dimension=1, tiled=True)
        .astype(jnp.float32)
        .astype(jnp.bfloat16)
    )


def solution(mesh):
    return jax.shard_map(
        local,
        mesh=mesh,
        in_specs=(
            P(("grp", "ctx", "rep"), None),
            P(("grp", "ctx", "rep")),
            P(("grp", "ctx", "rep")),
            P(None, "head"),
            P(None, "head"),
            P(None, "head"),
            P("head", None),
        ),
        out_specs=P(("grp", "ctx", "rep"), "head"),
        check_vma=False,
    )
```

profile of v0, /device:TPU:0, one launch (start us, length us, event | category | flops | bytes accessed | tf_op | source)
XLA Modules:
  0.0 215.8 jit_solution(6226166310934283381)
XLA Ops:
  10.4 6.3 %all-to-all-start = ((s32[8,48,1]{1,2,0:T(1,128)}), s32[8,48,1]{1,2,0:T(1,128)S(1)}, u32[]{:S(2)}, u32[]{:S(2)}) async-start(s32[8,48,1]{1,2,0:T(1,128)} %bitcast.12), calls=%async_computation | async-start | bytes 8192 | tf_op jit(solution)/shard_map/all_to_all | solution.py:131
  19.9 2.2 %all_gather.20 = bf16[512,2,128]{2,0,1:T(8,128)(2,1)} all-gather(bf16[256,2,128]{2,0,1:T(8,128)(2,1)S(1)} %fusion.25), channel_id=1, replica_groups=mesh['grp'=2,'ctx'=4,'head'=2,'rep'=2] {'rep'}, dimensions={0}, use_global_device_ids=true | all-gather | bytes 393216 | tf_op jit(solution)/shard_map/all_gather | solution.py:85
  22.2 5.7 %fusion.42 = f32[256,2048]{1,0:T(8,128)S(1)} fusion(bf16[256,2048]{1,0:T(8,128)(2,1)S(1)} %copy-done, bf16[2048,2048]{1,0:T(8,128)(2,1)} %param.14), kind=kOutput, calls=%fused_computation.83 | convolution fusion | flops 2147483648 | bytes 11534336 | tf_op jit(solution)/shard_map/dot_general | solution.py:24
  31.3 2.2 %broadcast_multiply_fusion = f32[256,16,128]{2,1,0:T(8,128)S(1)} fusion(f32[256,16]{1,0:T(8,128)S(1)} %copy.47, f32[32,8,16,128]{3,2,1,0:T(8,128)} %copy-done.1), kind=kLoop, calls=%fused_computation.37 | loop fusion | flops 524288 | bytes 4210688 | tf_op jit(solution)/shard_map/mul | solution.py:26
  35.7 5.0 %all-to-all-start.2 = ((s32[8,48,1]{1,2,0:T(1,128)}), s32[8,48,1]{1,2,0:T(1,128)S(1)}, u32[]{:S(2)}, u32[]{:S(2)}) async-start(s32[8,48,1]{1,2,0:T(1,128)} %bitcast.14), calls=%async_computation.2 | async-start | bytes 8192 | tf_op jit(solution)/shard_map/all_to_all | solution.py:132
  40.6 2.7 %slice_negate_fusion = (f32[256,16,64]{2,1,0:T(8,128)}, f32[256,16,64]{2,1,0:T(8,128)}) fusion(f32[256,16,128]{2,1,0:T(8,128)S(1)} %broadcast_multiply_fusion), kind=kLoop, calls=%fused_computation.31 | loop fusion | flops 262144 | bytes 4194304 | tf_op jit(solution)/shard_map/neg | solution.py:29
  46.2 4.3 %all-to-all-start.1 = ((s32[8,48,1]{1,2,0:T(1,128)}), s32[8,48,1]{1,2,0:T(1,128)S(1)}, u32[]{:S(2)}, u32[]{:S(2)}) async-start(s32[8,48,1]{1,2,0:T(1,128)} %bitcast.13), calls=%async_computation.1 | async-start | bytes 8192 | tf_op jit(solution)/shard_map/all_to_all | solution.py:133
  50.5 2.8 %maximum_multiply_fusion = f32[256,16,128]{2,1,0:T(8,128)S(1)} fusion(f32[256,16,64]{2,1,0:T(8,128)} %get-tuple-element.300, f32[256,16,64]{2,1,0:T(8,128)} %get-tuple-element.299, f32[256,128]{1,0:T(8,128)S(1)} %pad_maximum_fusion.1), kind=kLoop, calls=%fused_computation.32 | loop fusion | flops 1048576 | bytes 4325376 | tf_op jit(solution)/shard_map/mul | solution.py:30
  54.8 1.9 mul.138
  56.7 7.4 %scatter_custom_fusion.5 = bf16[384,2048]{1,0:T(8,128)(2,1)} fusion(s32[256]{0:T(256)} %copy-done.5, f32[32,8,16,128]{3,2,1,0:T(8,128)S(1)} %bitcast.79, f32[32,8,16,128]{3,2,1,0:T(8,128)} %bitcast.81, f32[256,2048]{1,0:T(8,128)} %copy-done.2, f32[32,8,16,128]{3,2,1,0:T(8,128)} %bitcast.82, bf16[]{:T(256)} %constant.112.clone.1), kind=kCustom, calls=%fused_computation.36 | custom fusion | flops 2097152 | bytes 9961984 | tf_op jit(solution)/shard_map/scatter | solution.py:45
  64.1 5.1 %all-to-all-start.3 = ((bf16[8,48,2048]{2,1,0:T(8,128)(2,1)}), bf16[8,48,2048]{2,1,0:T(8,128)(2,1)S(1)}, u32[]{:S(2)}, u32[]{:S(2)}) async-start(bf16[8,48,2048]{2,1,0:T(8,128)(2,1)} %bitcast.84), calls=%async_computation.3 | async-start | bytes 3145728 | tf_op jit(solution)/shard_map/all_to_all | solution.py:130
  71.1 2.2 %all_gather.22 = bf16[512,2,128]{2,0,1:T(8,128)(2,1)} all-gather(bf16[256,2,128]{2,0,1:T(8,128)(2,1)S(1)} %copy.49), channel_id=1, replica_groups=mesh['grp'=2,'ctx'=4,'head'=2,'rep'=2] {'rep'}, dimensions={0}, use_global_device_ids=true | all-gather | bytes 393216 | tf_op jit(solution)/shard_map/all_gather | solution.py:86
  75.3 53.8 %all-gather.1 = s32[4,1,512]{2,1,0:T(1,128)S(1)} all-gather(s32[1,1,512]{2,1,0:T(1,128)S(1)} %bitcast.91), channel_id=1, replica_groups=mesh['grp'=2,'ctx'=4,'head'=2,'rep'=2] {'ctx'}, dimensions={0}, use_global_device_ids=true | all-gather | bytes 10240 | tf_op jit(solution)/shard_map/all_gather | solution.py:91
  132.0 2.9 %scatter_custom_fusion.4 = s32[256]{0:T(256)S(1)} fusion(s32[384]{0:T(512)S(1)} %fusion.29, s32[384]{0:T(512)S(1)} %reshape.153, s32[]{:T(128)} %constant.95.clone.1), kind=kCustom, calls=%fused_computation.79 | custom fusion | bytes 1028 | tf_op jit(solution)/shard_map/scatter | solution.py:51
  134.9 2.9 %scatter_custom_fusion.2 = s32[256]{0:T(256)S(1)} fusion(s32[384]{0:T(512)S(1)} %fusion.29, s32[384]{0:T(512)S(1)} %reshape.137, s32[]{:T(128)} %constant.95.clone.1), kind=kCustom, calls=%fused_computation.77 | custom fusion | bytes 1028 | tf_op jit(solution)/shard_map/scatter | solution.py:51
  139.0 4.2 %scatter_custom_fusion.6 = bf16[256,2048]{1,0:T(8,128)(2,1)S(1)} fusion(s32[384]{0:T(512)S(1)} %fusion.29, bf16[384,2048]{1,0:T(8,128)(2,1)} %bitcast.86, bf16[]{:T(256)} %constant.112.clone.1), kind=kCustom, calls=%fused_computation.39 | custom fusion | bytes 1049088 | tf_op jit(solution)/shard_map/scatter | solution.py:51
  145.3 34.9 %while.15 = (s32[]{:T(128)}, f32[256,2,8,128]{3,0,2,1:T(8,128)S(1)}, f32[256,2,8]{0,2,1:T(8,128)S(1)}, s32[2048]{0:T(1024)S(1)}, s32[256]{0:T(256)S(1)}, /*index...) while((s32[]{:T(128)}, ...), condition=%wide.region_17.18_spmd, body=%wide.region_12.0_spmd.sunk | while | flops 1087373824 | bytes 23016728 | solution.py:106
  146.9 7.1 %conditional.2 = ((f32[256,2,8,128]{3,0,2,1:T(8,128)S(1)}, f32[256,2,8]{0,2,1:T(8,128)S(1)})) conditional(s32[]{:T(128)} %convert_element_type.67, (f32[256,2,8,128]{3,0,2,1:T(8,128)S(1)}, f32[256,2,8]{0,2,1:T(8,128)S(1)}) %tuple.56, (pred[256,512]{0,1:T(8,128)(4,1)S(1)}, bf16[2048,2,128]{2,0,1:T(8,128)(2,1)}, s32[]{:T(128)}, ...), branch_computations={%region_14.14_spmd, %region_15.16_spmd} | conditional | flops 1086849024 | bytes 22873112 | solution.py:78
  146.9 3.3 %fusion = (f32[256,2,8]{0,2,1:T(8,128)S(1)}, f32[2,512,256,8]{2,1,3,0:T(8,128)S(1)}) fusion(pred[256,512]{0,1:T(8,128)(4,1)S(1)} %get-tuple-element.208, bf16[256,2,8,128]{3,0,2,1:T(8,128)(2,1)} %get-tuple-element.211, bf16[2048,2,128]{2,0,1:T(8,128)(2,1)} %get-tuple-element.209, s32[]{:T(128)} %get-tuple-element.210), kind=kOutput, calls=%fused_computation.8 | convolution fusion | flops 543158272 | bytes 9847296 | tf_op jit(solution)/shard_map/while/body/eval_jaxpr/cond/branch_1_fun/rkgd,nkd->rkgn/dot_general | solution.py:66
  150.2 3.8 %bitcast_add_fusion = f32[256,2,8,128]{3,0,2,1:T(8,128)S(1)} fusion(f32[256,2,8,128]{3,0,2,1:T(8,128)S(1)} %get-tuple-element.207, f32[2,512,256,8]{2,1,3,0:T(8,128)S(1)} %get-tuple-element.298, pred[256,512]{0,1:T(8,128)(4,1)S(1)} %get-tuple-element.208, bf16[2048,2,128]{2,0,1:T(8,128)(2,1)} %get-tuple-element.212, s32[]{:T(128)} %get-tuple-element.210), kind=kOutput, calls=%fused_computation.14 | convolution fusion | flops 543686656 | bytes 12976640 | tf_op jit(solution)/shard_map/while/body/eval_jaxpr/cond/branch_1_fun/rkgn,nkd->rkgd/dot_general | solution.py:70
  155.6 7.1 %conditional.2 = ((f32[256,2,8,128]{3,0,2,1:T(8,128)S(1)}, f32[256,2,8]{0,2,1:T(8,128)S(1)})) conditional(s32[]{:T(128)} %convert_element_type.67, (f32[256,2,8,128]{3,0,2,1:T(8,128)S(1)}, f32[256,2,8]{0,2,1:T(8,128)S(1)}) %tuple.56, (pred[256,512]{0,1:T(8,128)(4,1)S(1)}, bf16[2048,2,128]{2,0,1:T(8,128)(2,1)}, s32[]{:T(128)}, ...), branch_computations={%region_14.14_spmd, %region_15.16_spmd} | conditional | flops 1086849024 | bytes 22873112 | solution.py:78
  155.6 3.3 %fusion = (f32[256,2,8]{0,2,1:T(8,128)S(1)}, f32[2,512,256,8]{2,1,3,0:T(8,128)S(1)}) fusion(pred[256,512]{0,1:T(8,128)(4,1)S(1)} %get-tuple-element.208, bf16[256,2,8,128]{3,0,2,1:T(8,128)(2,1)} %get-tuple-element.211, bf16[2048,2,128]{2,0,1:T(8,128)(2,1)} %get-tuple-element.209, s32[]{:T(128)} %get-tuple-element.210), kind=kOutput, calls=%fused_computation.8 | convolution fusion | flops 543158272 | bytes 9847296 | tf_op jit(solution)/shard_map/while/body/eval_jaxpr/cond/branch_1_fun/rkgd,nkd->rkgn/dot_general | solution.py:66
  158.9 3.8 %bitcast_add_fusion = f32[256,2,8,128]{3,0,2,1:T(8,128)S(1)} fusion(f32[256,2,8,128]{3,0,2,1:T(8,128)S(1)} %get-tuple-element.207, f32[2,512,256,8]{2,1,3,0:T(8,128)S(1)} %get-tuple-element.298, pred[256,512]{0,1:T(8,128)(4,1)S(1)} %get-tuple-element.208, bf16[2048,2,128]{2,0,1:T(8,128)(2,1)} %get-tuple-element.212, s32[]{:T(128)} %get-tuple-element.210), kind=kOutput, calls=%fused_computation.14 | convolution fusion | flops 543686656 | bytes 12976640 | tf_op jit(solution)/shard_map/while/body/eval_jaxpr/cond/branch_1_fun/rkgn,nkd->rkgd/dot_general | solution.py:70
  164.3 7.1 %conditional.2 = ((f32[256,2,8,128]{3,0,2,1:T(8,128)S(1)}, f32[256,2,8]{0,2,1:T(8,128)S(1)})) conditional(s32[]{:T(128)} %convert_element_type.67, (f32[256,2,8,128]{3,0,2,1:T(8,128)S(1)}, f32[256,2,8]{0,2,1:T(8,128)S(1)}) %tuple.56, (pred[256,512]{0,1:T(8,128)(4,1)S(1)}, bf16[2048,2,128]{2,0,1:T(8,128)(2,1)}, s32[]{:T(128)}, ...), branch_computations={%region_14.14_spmd, %region_15.16_spmd} | conditional | flops 1086849024 | bytes 22873112 | solution.py:78
  164.4 3.3 %fusion = (f32[256,2,8]{0,2,1:T(8,128)S(1)}, f32[2,512,256,8]{2,1,3,0:T(8,128)S(1)}) fusion(pred[256,512]{0,1:T(8,128)(4,1)S(1)} %get-tuple-element.208, bf16[256,2,8,128]{3,0,2,1:T(8,128)(2,1)} %get-tuple-element.211, bf16[2048,2,128]{2,0,1:T(8,128)(2,1)} %get-tuple-element.209, s32[]{:T(128)} %get-tuple-element.210), kind=kOutput, calls=%fused_computation.8 | convolution fusion | flops 543158272 | bytes 9847296 | tf_op jit(solution)/shard_map/while/body/eval_jaxpr/cond/branch_1_fun/rkgd,nkd->rkgn/dot_general | solution.py:66
  167.7 3.8 %bitcast_add_fusion = f32[256,2,8,128]{3,0,2,1:T(8,128)S(1)} fusion(f32[256,2,8,128]{3,0,2,1:T(8,128)S(1)} %get-tuple-element.207, f32[2,512,256,8]{2,1,3,0:T(8,128)S(1)} %get-tuple-element.298, pred[256,512]{0,1:T(8,128)(4,1)S(1)} %get-tuple-element.208, bf16[2048,2,128]{2,0,1:T(8,128)(2,1)} %get-tuple-element.212, s32[]{:T(128)} %get-tuple-element.210), kind=kOutput, calls=%fused_computation.14 | convolution fusion | flops 543686656 | bytes 12976640 | tf_op jit(solution)/shard_map/while/body/eval_jaxpr/cond/branch_1_fun/rkgn,nkd->rkgd/dot_general | solution.py:70
  173.1 7.1 %conditional.2 = ((f32[256,2,8,128]{3,0,2,1:T(8,128)S(1)}, f32[256,2,8]{0,2,1:T(8,128)S(1)})) conditional(s32[]{:T(128)} %convert_element_type.67, (f32[256,2,8,128]{3,0,2,1:T(8,128)S(1)}, f32[256,2,8]{0,2,1:T(8,128)S(1)}) %tuple.56, (pred[256,512]{0,1:T(8,128)(4,1)S(1)}, bf16[2048,2,128]{2,0,1:T(8,128)(2,1)}, s32[]{:T(128)}, ...), branch_computations={%region_14.14_spmd, %region_15.16_spmd} | conditional | flops 1086849024 | bytes 22873112 | solution.py:78
  173.1 3.3 %fusion = (f32[256,2,8]{0,2,1:T(8,128)S(1)}, f32[2,512,256,8]{2,1,3,0:T(8,128)S(1)}) fusion(pred[256,512]{0,1:T(8,128)(4,1)S(1)} %get-tuple-element.208, bf16[256,2,8,128]{3,0,2,1:T(8,128)(2,1)} %get-tuple-element.211, bf16[2048,2,128]{2,0,1:T(8,128)(2,1)} %get-tuple-element.209, s32[]{:T(128)} %get-tuple-element.210), kind=kOutput, calls=%fused_computation.8 | convolution fusion | flops 543158272 | bytes 9847296 | tf_op jit(solution)/shard_map/while/body/eval_jaxpr/cond/branch_1_fun/rkgd,nkd->rkgn/dot_general | solution.py:66
  176.4 3.8 %bitcast_add_fusion = f32[256,2,8,128]{3,0,2,1:T(8,128)S(1)} fusion(f32[256,2,8,128]{3,0,2,1:T(8,128)S(1)} %get-tuple-element.207, f32[2,512,256,8]{2,1,3,0:T(8,128)S(1)} %get-tuple-element.298, pred[256,512]{0,1:T(8,128)(4,1)S(1)} %get-tuple-element.208, bf16[2048,2,128]{2,0,1:T(8,128)(2,1)} %get-tuple-element.212, s32[]{:T(128)} %get-tuple-element.210), kind=kOutput, calls=%fused_computation.14 | convolution fusion | flops 543686656 | bytes 12976640 | tf_op jit(solution)/shard_map/while/body/eval_jaxpr/cond/branch_1_fun/rkgn,nkd->rkgd/dot_general | solution.py:70
  180.2 1.9 copy.51
  183.9 6.7 %convolution_convert_fusion = bf16[256,2048]{1,0:T(8,128)(2,1)} fusion(bf16[256,2048]{0,1:T(8,128)(2,1)S(1)} %bitcast.83, bf16[2048,2048]{1,0:T(8,128)(2,1)} %param.17), kind=kOutput, calls=%fused_computation.26 | convolution fusion | flops 2148007936 | bytes 10485760 | tf_op jit(solution)/shard_map/dot_general | solution.py:141
  190.6 18.6 %reduce-scatter.2.cloned.1.call-done = bf16[256,1024]{1,0:T(8,128)(2,1)} async-done(((bf16[256,2048]{1,0:T(8,128)(2,1)}), bf16[256,1024]{1,0:T(8,128)(2,1)}) %reduce-scatter.2.cloned.1.call-update) | async-done | bytes 524304 | tf_op jit(solution)/shard_map/reduce_scatter | solution.py:143
  (87 shorter events, 32.3 us)
Async XLA Ops:
  6.5 11.0 %copy-start = (bf16[256,2048]{1,0:T(8,128)(2,1)S(1)}, bf16[256,2048]{1,0:T(8,128)(2,1)}, u32[]{:S(2)}) copy-start(bf16[256,2048]{1,0:T(8,128)(2,1)} %param.11) | copy-start | bytes 3145732
  8.3 35.1 %copy-start.5 = (s32[256]{0:T(256)}, s32[256]{0:T(256)S(1)}, u32[]{:S(2)}) copy-start(s32[256]{0:T(256)S(1)} %compare_select_fusion.2) | copy-start | bytes 3076
  10.4 25.3 %all-to-all-start = ((s32[8,48,1]{1,2,0:T(1,128)}), s32[8,48,1]{1,2,0:T(1,128)S(1)}, u32[]{:S(2)}, u32[]{:S(2)}) async-start(s32[8,48,1]{1,2,0:T(1,128)} %bitcast.12), calls=%async_computation | async-start | bytes 8192 | tf_op jit(solution)/shard_map/all_to_all | solution.py:131
  16.7 128.4 %all-gather.5.cloned.1.call-start = ((), (), s32[]{:S(2)}) async-start(), calls=%async_computation.5 | async-start | bytes 1310720 | tf_op jit(solution)/shard_map/all_gather | solution.py:89
  27.9 1.4 copy-start.2
  29.2 1.3 copy-start.1
  35.7 10.5 %all-to-all-start.2 = ((s32[8,48,1]{1,2,0:T(1,128)}), s32[8,48,1]{1,2,0:T(1,128)S(1)}, u32[]{:S(2)}, u32[]{:S(2)}) async-start(s32[8,48,1]{1,2,0:T(1,128)} %bitcast.14), calls=%async_computation.2 | async-start | bytes 8192 | tf_op jit(solution)/shard_map/all_to_all | solution.py:132
  40.6 2.7 %copy-start.4 = (s32[256]{0:T(256)S(1)}, s32[256]{0:T(256)}, u32[]{:S(2)}) copy-start(s32[256]{0:T(256)} %param.12) | copy-start | bytes 3076
  46.2 17.9 %all-to-all-start.1 = ((s32[8,48,1]{1,2,0:T(1,128)}), s32[8,48,1]{1,2,0:T(1,128)S(1)}, u32[]{:S(2)}, u32[]{:S(2)}) async-start(s32[8,48,1]{1,2,0:T(1,128)} %bitcast.13), calls=%async_computation.1 | async-start | bytes 8192 | tf_op jit(solution)/shard_map/all_to_all | solution.py:133
  64.1 73.7 %all-to-all-start.3 = ((bf16[8,48,2048]{2,1,0:T(8,128)(2,1)}), bf16[8,48,2048]{2,1,0:T(8,128)(2,1)S(1)}, u32[]{:S(2)}, u32[]{:S(2)}) async-start(bf16[8,48,2048]{2,1,0:T(8,128)(2,1)} %bitcast.84), calls=%async_computation.3 | async-start | bytes 3145728 | tf_op jit(solution)/shard_map/all_to_all | solution.py:130
  69.2 75.8 %all-gather.7.cloned.1.call-start = ((), (), s32[]{:S(2)}) async-start(), calls=%async_computation.6 | async-start | bytes 1310720 | tf_op jit(solution)/shard_map/all_gather | solution.py:90
  73.4 135.9 %reduce-scatter.2.cloned.1.call-start = ((), (), s32[]{:S(2)}) async-start(), calls=%async_computation.7 | async-start | bytes 1572864 | tf_op jit(solution)/shard_map/reduce_scatter | solution.py:143
  137.9 1.2 copy-start.3
Sparse Core Ops, SparseCore 0:
  22.3 29.3 all-gather.4
  73.5 49.1 all-gather.6
  190.8 18.4 reduce-scatter.1
where the time goes:
time: 217 us; the launch traced here: 216 us
  blocking collectives  60 us (28%)
  matrix products  44.3 us (20%)
  local copies, waits for them, and re-layouts  29 us (13%)
  other arithmetic  25.9 us (12%)
  starting transfers between devices  20.8 us (10%)
  waiting for transfers between devices  19.4 us (9%)
  between operations  13.4 us (6%)
  loops' own time  2.83 us (1%)
    all_gather x1, blocking collectives, attend(): seg_part = lax.all_gather(paired[2], 'ctx', axis=0, tiled=True)  53.8 us
    reduce_scatter x1, waiting for transfers between devices, local(): lax.psum_scatter(partial_out, 'head', scatter_dimension=1, tiled=True)  18.6 us
    dot_general x4, matrix products, compute(): jnp.einsum('rkgn,nkd->rkgd', weights.astype(jnp.bfloat16), value_blk, pre...  15.1 us
    dot_general x4, matrix products, compute(): jnp.einsum('rkgd,nkd->rkgn', queries, key_blk, preferred_element_type=jnp...  13.2 us
    scatter x4, local copies, waits for them, and re-layouts, place_rows(): return empty.at[target].set(values, mode='drop')  10.5 us
    dot_general x2, matrix products, project_heads(): flat = jnp.dot(tokens, weight, preferred_element_type=jnp.float32)  7.48 us
    scatter x1, other arithmetic, scatter_rows(): return empty.at[buffer_pos].set(values)  7.38 us
    dot_general x1, matrix products, local(): jnp.dot(attended, w_out, preferred_element_type=jnp.float32)  6.74 us
  transfers between devices with their start and end apart: 7, of which 2 were waited for; matrix products, arithmetic and copies ran while one was open for 22% of the time, Pallas kernels for 0%

commit v1 on v0

v1 whole, which is shorter than its diff:
```python
import functools
import math

import jax
import jax.numpy as jnp
from jax import lax
from jax.experimental import pallas as pl
from jax.experimental.pallas import tpu as pltpu
from jax.sharding import PartitionSpec as P

HD = 128
THETA = 1000000.0
EPSILON = 1e-06
HIDE = -1e30
F32 = jnp.float32
BF16 = jnp.bfloat16
VMEM = pl.BlockSpec(memory_space=pltpu.VMEM)
ANY = pl.BlockSpec(memory_space=pl.ANY)
MIB = 1 << 20


def params(mib):
    return pltpu.CompilerParams(vmem_limit_bytes=mib * MIB)


def cost(flops, nbytes, trans=0):
    return pl.CostEstimate(flops=int(flops), bytes_accessed=int(nbytes), transcendentals=int(trans))


def column_of(row):
    n = row.shape[1]
    at = lax.broadcasted_iota(jnp.int32, (n, n), 0) == lax.broadcasted_iota(jnp.int32, (n, n), 1)
    return jnp.sum(jnp.where(at, row, 0.0), axis=1, keepdims=True)


def norm_rope(heads, cosine, sine, factor):
    scale = lax.rsqrt(jnp.mean(heads * heads, axis=-1, keepdims=True) + EPSILON)
    if factor != 1.0:
        scale = scale * factor
    turned = pltpu.roll(heads, HD // 2, 1)
    return ((heads * cosine + turned * sine) * scale).astype(BF16)


def kv_kernel(x_ref, wk_ref, wv_ref, seg_ref, k_ref, v_ref, tab_ref, acc_k, acc_v):
    step = pl.program_id(0)
    rows = x_ref.shape[0]
    first = (lax.axis_index("ctx") * 2 + lax.axis_index("rep")) * rows

    @pl.when(step == 0)
    def _():
        lane = lax.broadcasted_iota(jnp.int32, (1, HD), 1)
        freq = jnp.exp(lax.rem(lane, HD // 2).astype(F32) * (-2.0 * math.log(THETA) / HD))
        pos = (first + lax.broadcasted_iota(jnp.int32, (rows, HD), 0)).astype(F32)
        angle = pos * freq
        tab_ref[:, :HD] = jnp.cos(angle)
        tab_ref[:, HD:] = jnp.where(lane < HD // 2, -jnp.sin(angle), jnp.sin(angle))
        acc_k[...] = jnp.zeros_like(acc_k)
        acc_v[...] = jnp.zeros_like(acc_v)

    acc_k[...] += jnp.dot(x_ref[...], wk_ref[...], preferred_element_type=F32)
    acc_v[...] += jnp.dot(x_ref[...], wv_ref[...], preferred_element_type=F32)

    @pl.when(step == pl.num_programs(0) - 1)
    def _():
        for g in range(acc_k.shape[1] // HD):
            at = pl.ds(g * HD, HD)
            k_ref[0:rows, at] = norm_rope(acc_k[:, at], tab_ref[:, :HD], tab_ref[:, HD:], 1.0)
        wide = k_ref.shape[1]
        line = lax.broadcasted_iota(jnp.int32, (16, wide), 0)
        segs = jnp.zeros((16, wide), F32)
        for i in range(rows // wide):
            segs = jnp.where(line == i, seg_ref[:, i * wide:(i + 1) * wide].astype(F32), segs)
        k_ref[rows:, :] = segs.astype(BF16)
        v_ref[...] = acc_v[...].astype(BF16)


def q_kernel(x_ref, w_ref, tab_ref, q_ref):
    flat = jnp.dot(x_ref[...], w_ref[...], preferred_element_type=F32)
    factor = math.log2(math.e) / math.sqrt(HD)
    for j in range(q_ref.shape[0]):
        q_ref[j] = norm_rope(flat[:, j * HD:(j + 1) * HD], tab_ref[:, :HD], tab_ref[:, HD:], factor)


def route_kernel(ctx, cap, dest_ref, pos_ref, *slot_refs):
    rows = dest_ref.shape[1]
    mine_c, mine_r = lax.axis_index("ctx"), lax.axis_index("rep")
    dest = dest_ref[...]
    owner = lax.div(dest, rows)
    slot = dest - owner * rows
    owner_col = column_of(owner.astype(F32))
    ii = lax.broadcasted_iota(jnp.int32, (rows, rows), 0)
    jj = lax.broadcasted_iota(jnp.int32, (rows, rows), 1)
    before = (owner_col == owner.astype(F32)) & (ii < jj)
    rank = jnp.sum(jnp.where(before, 1.0, 0.0), axis=0, keepdims=True).astype(jnp.int32)
    near_c = jnp.bitwise_xor(lax.div(owner, 2), mine_c)
    near_r = jnp.bitwise_xor(lax.rem(owner, 2), mine_r)
    pos = (near_c * 2 + near_r) * cap + rank
    pos_ref[...] = jnp.broadcast_to(pos, pos_ref.shape)
    pos_col = column_of(pos.astype(F32))
    target_col = column_of((near_r * rows + slot).astype(F32)) + 1.0
    lanes = slot_refs[0].shape[1]
    for k in range(ctx):
        lane = lax.broadcasted_iota(jnp.int32, (rows, lanes), 1)
        hit = (pos_col == (lane + k * 2 * cap).astype(F32)) & (lane < 2 * cap)
        got = jnp.sum(jnp.where(hit, target_col, 0.0), axis=0, keepdims=True) - 1.0
        slot_refs[k][...] = jnp.broadcast_to(got.astype(jnp.int32), slot_refs[k].shape)


def documents(k_ref, rows):
    wide = k_ref.shape[1]
    lines = k_ref[rows:rows + 16, :].astype(F32)
    return jnp.concatenate([lines[i:i + 1] for i in range(rows // wide)], 1)


def add_block(q_ref, k_ref, v_ref, acc_ref, seg_col, lowest, valid, own, fresh):
    heads, rows = q_ref.shape[0], q_ref.shape[1]
    kv_heads = v_ref.shape[1] // HD
    groups = heads // kv_heads
    seg = documents(k_ref, rows)
    seen = valid & (jnp.max(seg) == lowest) if not own else True

    def compute():
        visible = seg == seg_col
        if own:
            ii = lax.broadcasted_iota(jnp.int32, (rows, rows), 0)
            jj = lax.broadcasted_iota(jnp.int32, (rows, rows), 1)
            visible = visible & (jj <= ii)
        bias = jnp.where(visible, 0.0, HIDE)
        for g in range(kv_heads):
            keys = k_ref[0:rows, g * HD:(g + 1) * HD]
            vals = jnp.concatenate([v_ref[:, g * HD:(g + 1) * HD], jnp.ones((rows, HD), BF16)], 1)

            def head(j, _):
                s = lax.dot_general(q_ref[j], keys, (((1,), (1,)), ((), ())), preferred_element_type=F32)
                p = jnp.exp2(s + bias).astype(BF16)
                new = jnp.dot(p, vals, preferred_element_type=F32)
                if fresh:
                    acc_ref[j] = new
                else:
                    acc_ref[j] += new
                return 0

            lax.fori_loop(g * groups, (g + 1) * groups, head, 0, unroll=2)

    if own:
        compute()
    else:
        pl.when(seen)(compute)


def near_kernel(n_hops, q_ref, *refs):
    acc_ref = refs[-1]
    blocks = [(refs[2 * i], refs[2 * i + 1]) for i in range(len(refs) // 2)]
    rows = q_ref.shape[1]
    c, r = lax.axis_index("ctx"), lax.axis_index("rep")
    seg = documents(blocks[0][0], rows)
    seg_col = column_of(seg)
    lowest = jnp.min(seg)
    add_block(q_ref, *blocks[0], acc_ref, seg_col, lowest, True, True, True)
    add_block(q_ref, *blocks[1], acc_ref, seg_col, lowest, r == 1, False, False)
    for i, (k_ref, v_ref) in enumerate(blocks[2:]):
        add_block(q_ref, k_ref, v_ref, acc_ref, seg_col, lowest, c >= i // 2 + 1, False, False)


def far_kernel(hop, q_ref, seg_ref, k0, v0, k1, v1, near_ref, w_ref, att_ref, *rest):
    n_out = len(rest) - 5
    outs, (acc, held, w_buf, sem_a, sem_w) = rest[:n_out], rest[n_out:]
    rows = q_ref.shape[1]
    heads = q_ref.shape[0]
    n_other = lax.axis_size("head") - 1
    half = w_buf.shape[1] // n_other
    c, r, h = lax.axis_index("ctx"), lax.axis_index("rep"), lax.axis_index("head")
    load = pltpu.make_async_copy(near_ref, held, sem_a)
    load.start()
    wide = []
    for d in range(n_other):
        from_ = pl.multiple_of(jnp.bitwise_xor(h, d + 1) * half, half)
        wide.append(pltpu.make_async_copy(w_ref.at[:, pl.ds(from_, half)], w_buf.at[:, pl.ds(d * half, half)], sem_w.at[d]))
        wide[-1].start()
    seg = seg_ref[...].astype(F32)
    seg_col = column_of(seg)
    lowest = jnp.min(seg)
    acc[...] = jnp.zeros_like(acc)
    add_block(q_ref, k0, v0, acc, seg_col, lowest, c >= hop, False, False)
    add_block(q_ref, k1, v1, acc, seg_col, lowest, (c >= hop) & (r == 0), False, False)
    load.wait()
    for j in range(heads):
        both = acc[j] + held[j]
        att_ref[:, j * HD:(j + 1) * HD] = (both[:, :HD] / both[:, HD:]).astype(BF16)
    for copy in wide:
        copy.wait()
    at = 0
    for out in outs:
        width = out.shape[1]
        out[...] = jnp.dot(att_ref[...], w_buf[:, at:at + width], preferred_element_type=F32).astype(BF16)
        at += width


def own_kernel(att_ref, w_ref, *rest):
    n_out = len(rest) - 2
    outs, (w_buf, sem) = rest[:n_out], rest[n_out:]
    half = w_buf.shape[1]
    h = lax.axis_index("head")
    copies, at = [], 0
    for i, out in enumerate(outs):
        width = out.shape[1]
        from_ = pl.multiple_of(h * half + at, 128)
        copies.append(pltpu.make_async_copy(w_ref.at[:, pl.ds(from_, width)], w_buf.at[:, pl.ds(at, width)], sem.at[i]))
        copies[-1].start()
        at += width
    at = 0
    for i, out in enumerate(outs):
        width = out.shape[1]
        copies[i].wait()
        out[...] = jnp.dot(att_ref[...], w_buf[:, at:at + width], preferred_element_type=F32).astype(BF16)
        at += width


def pick_kernel(n_head, pos_ref, *refs):
    shares, outs = refs[:n_head], refs[n_head:]
    rows = shares[0].shape[0]
    span = outs[0].shape[0]
    total = shares[0][...].astype(F32)
    for share in shares[1:]:
        total = total + share[...].astype(F32)
    total = total.astype(BF16)
    pos = pos_ref[0:1, :]
    every = span * len(outs)
    pick = jnp.where(lax.broadcasted_iota(jnp.int32, (every, rows), 0) == pos, 1.0, 0.0).astype(BF16)
    moved = jnp.dot(pick, total, preferred_element_type=F32).astype(BF16)
    for k, out in enumerate(outs):
        out[...] = moved[k * span:(k + 1) * span]


def place_kernel(ctx, rows, *refs):
    blocks, slots, (mine_ref, pair_ref) = refs[:ctx], refs[ctx:2 * ctx], refs[2 * ctx:]
    span = blocks[0].shape[0]
    total = None
    for block, slot in zip(blocks, slots, strict=True):
        at = lax.broadcasted_iota(jnp.int32, (2 * rows, span), 0) == slot[0:1, 0:span]
        put = jnp.dot(jnp.where(at, 1.0, 0.0).astype(BF16), block[...], preferred_element_type=F32)
        total = put if total is None else total + put
    mine_ref[...] = total[:rows].astype(BF16)
    pair_ref[...] = total[rows:].astype(BF16)


def join_kernel(n, *refs):
    out = refs[-1]
    at = 0
    for mine, other in zip(refs[:n], refs[n:2 * n], strict=True):
        width = mine.shape[1]
        out[:, at:at + width] = (mine[...].astype(F32) + other[...].astype(F32)).astype(BF16)
        at += width


def local(tokens, doc_ids, dest_rows, w_query, w_key, w_value, w_out):
    ctx, rep, n_head = lax.axis_size("ctx"), lax.axis_size("rep"), lax.axis_size("head")
    rows, width = tokens.shape
    kv_cols, q_cols = w_key.shape[1], w_query.shape[1]
    heads = q_cols // HD
    out_cols = w_out.shape[1]
    half = out_cols // n_head
    others = n_head - 1
    hops = ctx // 2
    cap = 3 * (rows // (2 * ctx * rep))
    span = 2 * cap
    lanes = -(-span // 128) * 128
    every = ctx * span
    sds = jax.ShapeDtypeStruct
    chunks = (half // 4, half - half // 4)

    up = [(i, i + 1) for i in range(ctx - 1)]
    swap = [(0, 1), (1, 0)]
    seg_row = doc_ids.reshape(1, rows)

    parts = 4
    depth = width // parts
    key0, val0, table = pl.pallas_call(
        kv_kernel,
        grid=(parts,),
        in_specs=[
            pl.BlockSpec((rows, depth), lambda i: (0, i)),
            pl.BlockSpec((depth, kv_cols), lambda i: (i, 0)),
            pl.BlockSpec((depth, kv_cols), lambda i: (i, 0)),
            pl.BlockSpec((1, rows), lambda i: (0, 0)),
        ],
        out_specs=[
            pl.BlockSpec((rows + 16, kv_cols), lambda i: (0, 0)),
            pl.BlockSpec((rows, kv_cols), lambda i: (0, 0)),
            pl.BlockSpec((rows, 2 * HD), lambda i: (0, 0)),
        ],
        out_shape=[sds((rows + 16, kv_cols), BF16), sds((rows, kv_cols), BF16), sds((rows, 2 * HD), F32)],
        scratch_shapes=[pltpu.VMEM((rows, kv_cols), F32), pltpu.VMEM((rows, kv_cols), F32)],
        compiler_params=params(12),
        cost_estimate=cost(4 * rows * width * kv_cols, 2 * width * (rows + 2 * kv_cols)),
        name="keys_values",
    )(tokens, w_key, w_value, seg_row)

    hop_k, hop_v = [key0], [val0]
    for _ in range(hops):
        hop_k.append(lax.ppermute(hop_k[-1], "ctx", up))
        hop_v.append(lax.ppermute(hop_v[-1], "ctx", up))

    step = 2
    queries = pl.pallas_call(
        q_kernel,
        grid=(heads // step,),
        in_specs=[
            pl.BlockSpec((rows, width), lambda i: (0, 0)),
            pl.BlockSpec((width, step * HD), lambda i: (0, i)),
            pl.BlockSpec((rows, 2 * HD), lambda i: (0, 0)),
        ],
        out_specs=pl.BlockSpec((step, rows, HD), lambda i: (i, 0, 0)),
        out_shape=sds((heads, rows, HD), BF16),
        compiler_params=params(16),
        cost_estimate=cost(2 * rows * width * q_cols, 2 * width * (rows + q_cols)),
        name="queries",
    )(tokens, w_query, table)

    route = pl.pallas_call(
        functools.partial(route_kernel, ctx, cap),
        in_specs=[VMEM],
        out_specs=[VMEM] * (1 + ctx),
        out_shape=[sds((8, rows), jnp.int32)] + [sds((8, lanes), jnp.int32)] * ctx,
        compiler_params=params(8),
        cost_estimate=cost(4 * rows * rows, 8 * rows * 4),
        name="routes",
    )
    dest_row, _ = lax.optimization_barrier((dest_rows.reshape(1, rows), val0))
    buffer_pos, *slots = route(dest_row)

    def across(k):
        return [(i, i ^ k) for i in range(ctx)]

    slots = [slots[0]] + [lax.ppermute(slots[k], "ctx", across(k)) for k in range(1, ctx)]

    pair_k, pair_v = [], []
    for i in range(hops + 1):
        perm = [(0, 1)] if i == 0 else [(1, 0)] if i == hops else swap
        pair_k.append(lax.ppermute(hop_k[i], "rep", perm))
        pair_v.append(lax.ppermute(hop_v[i], "rep", perm))

    blocks = []
    for i in range(hops):
        blocks += [hop_k[i], hop_v[i], pair_k[i], pair_v[i]]
    work = heads * rows * rows
    near = pl.pallas_call(
        functools.partial(near_kernel, hops),
        in_specs=[VMEM] * (1 + len(blocks)),
        out_specs=VMEM,
        out_shape=sds((heads, rows, 2 * HD), F32),
        compiler_params=params(16),
        cost_estimate=cost(8 * work * HD * hops, 8 * MIB, 2 * work * hops),
        name="near_attention",
    )(queries, *blocks)

    attended, *far = pl.pallas_call(
        functools.partial(far_kernel, hops),
        in_specs=[VMEM] * 6 + [ANY, ANY],
        out_specs=[VMEM] * (1 + others * len(chunks)),
        out_shape=[sds((rows, heads * HD), BF16)] + [sds((rows, n), BF16) for n in chunks] * others,
        scratch_shapes=[
            pltpu.VMEM((heads, rows, 2 * HD), F32),
            pltpu.VMEM((heads, rows, 2 * HD), F32),
            pltpu.VMEM((heads * HD, others * half), BF16),
            pltpu.SemaphoreType.DMA,
            pltpu.SemaphoreType.DMA((others,)),
        ],
        compiler_params=params(28),
        cost_estimate=cost(8 * work * HD + 2 * rows * heads * HD * half, 10 * MIB, 2 * work),
        name="far_attention_project",
    )(queries, seg_row, hop_k[hops], hop_v[hops], pair_k[hops], pair_v[hops], near, w_out)

    theirs = []
    for j in range(len(chunks)):
        flips = [[(i, i ^ (d + 1)) for i in range(n_head)] for d in range(others)]
        theirs.append([lax.ppermute(far[d * len(chunks) + j], "head", flips[d]) for d in range(others)])

    ours = pl.pallas_call(
        own_kernel,
        in_specs=[VMEM, ANY],
        out_specs=[VMEM] * len(chunks),
        out_shape=[sds((rows, n), BF16) for n in chunks],
        scratch_shapes=[pltpu.VMEM((heads * HD, half), BF16), pltpu.SemaphoreType.DMA((len(chunks),))],
        compiler_params=params(12),
        cost_estimate=cost(2 * rows * heads * HD * half, 5 * MIB),
        name="project_own",
    )(attended, w_out)

    kept, gone = [], []
    for mine, other in zip(ours, theirs, strict=True):
        n = mine.shape[1]
        moved = pl.pallas_call(
            functools.partial(pick_kernel, n_head),
            in_specs=[VMEM] * (1 + n_head),
            out_specs=[VMEM] * ctx,
            out_shape=[sds((span, n), BF16)] * ctx,
            compiler_params=params(8),
            cost_estimate=cost(2 * every * rows * n, 2 * n * (2 * rows + every)),
            name="add_pick",
        )(buffer_pos, mine, *other)
        got = [moved[0]] + [lax.ppermute(moved[k], "ctx", across(k)) for k in range(1, ctx)]
        stay, leave = pl.pallas_call(
            functools.partial(place_kernel, ctx, rows),
            in_specs=[VMEM] * (2 * ctx),
            out_specs=[VMEM] * 2,
            out_shape=[sds((rows, n), BF16)] * 2,
            compiler_params=params(8),
            cost_estimate=cost(4 * every * rows * n, 2 * n * (2 * rows + every)),
            name="place",
        )(*got, *slots)
        kept.append(stay)
        gone.append(lax.ppermute(leave, "rep", swap))

    return pl.pallas_call(
        functools.partial(join_kernel, len(chunks)),
        in_specs=[VMEM] * (2 * len(chunks)),
        out_specs=VMEM,
        out_shape=sds((rows, half), BF16),
        compiler_params=params(8),
        cost_estimate=cost(rows * half, 6 * rows * half),
        name="join",
    )(*kept, *gone)


def solution(mesh):
    return jax.shard_map(
        local,
        mesh=mesh,
        in_specs=(
            P(("grp", "ctx", "rep"), None),
            P(("grp", "ctx", "rep")),
            P(("grp", "ctx", "rep")),
            P(None, "head"),
            P(None, "head"),
            P(None, "head"),
            P("head", None),
        ),
        out_specs=P(("grp", "ctx", "rep"), "head"),
        check_vma=False,
    )
```

time: 217 us -> 103 us (0.47)
  blocking collectives: 60 us -> 0 us
  matrix products: 44.3 us -> 0 us
  starting transfers between devices: 20.8 us -> 49.6 us
  other arithmetic: 25.9 us -> 0.01 us
  Pallas kernels: 0 us -> 23.9 us
  local copies, waits for them, and re-layouts: 29 us -> 9.23 us
  between operations: 13.4 us -> 0.32 us
  loops' own time: 2.83 us -> 0 us
    all_gather x4 -> x0, blocking collectives: 60 us -> none  [the longest x1 53.8 us: attend(): seg_part = lax.all_gather(paired[2], 'ctx', axis=0, tiled=True)]
    ppermute x0 -> x23, starting transfers between devices: none -> 49.6 us  [the longest x6 19.5 us: local(): lax.ppermute(moved[k], 'ctx', across(k))]
    dot_general x12 -> x0, matrix products: 44.3 us -> none  [the longest x4 15.1 us: compute(): jnp.einsum('rkgn,nkd->rkgd', weights.astype(jnp.bfloat16), value_blk, pre...]
    pallas_call x0 -> x11, Pallas kernels: none -> 23.9 us  [the longest x1 9.2 us: local(): pl.pallas_call(q_kernel, grid=(heads // step,), in_specs=[pl.BlockSpec((r...]
    all_to_all x4 -> x0, starting transfers between devices: 20.7 us -> none  [the longest x1 6.33 us: local(): lax.all_to_all(outgoing[1], ('ctx', 'rep'), split_axis=0, concat_axis=0,...]
    ppermute x0 -> x23, waiting for transfers between devices: none -> 20.2 us  [the longest x2 8.5 us: local(): lax.ppermute(far[d * len(chunks) + j], 'head', flips[d])]
    reduce_scatter x1 -> x0, waiting for transfers between devices: 18.6 us -> none  [local(): lax.psum_scatter(partial_out, 'head', scatter_dimension=1, tiled=True)]
    scatter x7 -> x0, local copies, waits for them, and re-layouts: 14.7 us -> none  [the longest x4 10.5 us: place_rows(): return empty.at[target].set(values, mode='drop')]
  transfers between devices with their start and end apart: 7 -> 23, of which waited for: 2 -> 8; matrix products, arithmetic and copies ran while one was open for 22% -> 0% of each run, Pallas kernels for 0% -> 16%
where the time goes in v1:
time: 103 us
  starting transfers between devices  49.6 us (48%)
  Pallas kernels  23.9 us (23%)
  waiting for transfers between devices  20.2 us (20%)
  local copies, waits for them, and re-layouts  9.23 us (9%)
    ppermute x6, starting transfers between devices, local(): lax.ppermute(moved[k], 'ctx', across(k))  19.5 us
    unnamed x20, local copies, waits for them, and re-layouts  9.23 us
    pallas_call x1, Pallas kernels, local(): pl.pallas_call(q_kernel, grid=(heads // step,), in_specs=[pl.BlockSpec((r...  9.2 us
    ppermute x2, waiting for transfers between devices, local(): lax.ppermute(far[d * len(chunks) + j], 'head', flips[d])  8.5 us
    ppermute x2, starting transfers between devices, local(): hop_k.append(lax.ppermute(hop_k[-1], 'ctx', up))  8.41 us
    ppermute x2, starting transfers between devices, local(): hop_v.append(lax.ppermute(hop_v[-1], 'ctx', up))  7.63 us
    ppermute x3, waiting for transfers between devices, local(): lax.ppermute(slots[k], 'ctx', across(k))  7.03 us
    ppermute x3, starting transfers between devices, local(): lax.ppermute(slots[k], 'ctx', across(k))  5.39 us
  transfers between devices with their start and end apart: 23, of which 8 were waited for; matrix products, arithmetic and copies ran while one was open for 0% of the time, Pallas kernels for 16%

profile of v1, /device:TPU:0, one launch (start us, length us, event | category | flops | bytes accessed | tf_op | source)
XLA Modules:
  0.0 103.3 jit_solution(4882054724831784099)
XLA Ops:
  0.0 1.2 %copy-done.1 = bf16[256,2048]{1,0:T(8,128)(2,1)S(1)} copy-done((bf16[256,2048]{1,0:T(8,128)(2,1)S(1)}, bf16[256,2048]{1,0:T(8,128)(2,1)}, u32[]{:S(2)}) %copy-start.1) | copy-done | bytes 1048600
  1.2 1.2 %copy-done.3 = bf16[2048,256]{1,0:T(8,128)(2,1)S(1)} copy-done((bf16[2048,256]{1,0:T(8,128)(2,1)S(1)}, bf16[2048,256]{1,0:T(8,128)(2,1)}, u32[]{:S(2)}) %copy-start.3) | copy-done | bytes 1048600
  4.4 2.1 %keys_values.1 = (bf16[272,256]{1,0:T(8,128)(2,1)S(1)}, bf16[256,256]{1,0:T(8,128)(2,1)S(1)}, f32[256,256]{1,0:T(8,128)S(1)}) custom-call(bf16[256,2048]{1,0:T(8,128)(2,1)S(1)} %copy-done.1, bf16[2048,256]{1,0:T(8,128)(2,1)S(1)} %copy-done.3, bf16[2048,256]{1,0:T(8,128)(2,1)S(1)} %copy-done.4, s32[1,256]{1,0:T(1,128)S(1)} %bitcast.4), custom_call_target="tpu_custom_call" | custom-call | flops 536870912 | bytes 3145728 | tf_op jit(solution)/shard_map/keys_values/pallas_call | solution.py:278
  6.5 4.9 %collective-permute-start = (bf16[272,256]{1,0:T(8,128)(2,1)S(1)}, bf16[272,256]{1,0:T(8,128)(2,1)S(1)}, u32[]{:S(2)}, u32[]{:S(2)}) collective-permute-start(bf16[272,256]{1,0:T(8,128)(2,1)S(1)} %get-tuple-element.35.refs_0_), channel_id=1, source_target_pairs={{0,4},{4,8},{8,12},{1,5},{5,9},{9,13},{2,6},{6,10},{10,14},{3,7},{... | collective-permute-start | bytes 417800 | tf_op jit(solution)/shard_map/ppermute | solution.py:301
  11.5 3.5 %collective-permute-start.2 = (bf16[256,256]{1,0:T(8,128)(2,1)S(1)}, bf16[256,256]{1,0:T(8,128)(2,1)S(1)}, u32[]{:S(2)}, u32[]{:S(2)}) collective-permute-start(bf16[256,256]{1,0:T(8,128)(2,1)S(1)} %get-tuple-element.31.refs_1_), channel_id=1, source_target_pairs={{0,4},{4,8},{8,12},{1,5},{5,9},{9,13},{2,6},{6,10},{10,14},{3,7},{... | collective-permute-start | bytes 393224 | tf_op jit(solution)/shard_map/ppermute | solution.py:302
  14.9 1.3 %collective-permute-start.7 = (bf16[256,256]{1,0:T(8,128)(2,1)S(1)}, bf16[256,256]{1,0:T(8,128)(2,1)S(1)}, u32[]{:S(2)}, u32[]{:S(2)}) collective-permute-start(bf16[256,256]{1,0:T(8,128)(2,1)S(1)} %get-tuple-element.31.refs_1_), channel_id=1, source_target_pairs={{0,1},{2,3},{4,5},{6,7},{8,9},{10,11},{12,13},{14,15},{16,17},{18,... | collective-permute-start | bytes 393224 | tf_op jit(solution)/shard_map/ppermute | solution.py:341
  16.2 1.3 %collective-permute-start.6 = (bf16[272,256]{1,0:T(8,128)(2,1)S(1)}, bf16[272,256]{1,0:T(8,128)(2,1)S(1)}, u32[]{:S(2)}, u32[]{:S(2)}) collective-permute-start(bf16[272,256]{1,0:T(8,128)(2,1)S(1)} %get-tuple-element.35.refs_0_), channel_id=1, source_target_pairs={{0,1},{2,3},{4,5},{6,7},{8,9},{10,11},{12,13},{14,15},{16,17},{18,... | collective-permute-start | bytes 417800 | tf_op jit(solution)/shard_map/ppermute | solution.py:340
  17.6 4.1 %collective-permute-start.3 = (bf16[256,256]{1,0:T(8,128)(2,1)S(1)}, bf16[256,256]{1,0:T(8,128)(2,1)S(1)}, u32[]{:S(2)}, u32[]{:S(2)}) collective-permute-start(bf16[256,256]{1,0:T(8,128)(2,1)S(1)} %collective-permute-done.2.refs_5_), channel_id=1, source_target_pairs={{0,4},{4,8},{8,12},{1,5},{5,9},{9,13},{2,6},{6,10},{10,14},{3,7},{... | collective-permute-start | bytes 393224 | tf_op jit(solution)/shard_map/ppermute | solution.py:302
  22.1 3.5 %collective-permute-start.1 = (bf16[272,256]{1,0:T(8,128)(2,1)S(1)}, bf16[272,256]{1,0:T(8,128)(2,1)S(1)}, u32[]{:S(2)}, u32[]{:S(2)}) collective-permute-start(bf16[272,256]{1,0:T(8,128)(2,1)S(1)} %collective-permute-done.refs_4_), channel_id=1, source_target_pairs={{0,4},{4,8},{8,12},{1,5},{5,9},{9,13},{2,6},{6,10},{10,14},{3,7},{... | collective-permute-start | bytes 417800 | tf_op jit(solution)/shard_map/ppermute | solution.py:301
  25.6 3.5 %copy-done = bf16[2048,2048]{1,0:T(8,128)(2,1)S(1)} copy-done((bf16[2048,2048]{1,0:T(8,128)(2,1)S(1)}, bf16[2048,2048]{1,0:T(8,128)(2,1)}, u32[]{:S(2)}) %copy-start) | copy-done | bytes 8388632
  29.1 1.3 %copy-done.2 = bf16[256,2048]{1,0:T(8,128)(2,1)S(1)} copy-done((bf16[256,2048]{1,0:T(8,128)(2,1)S(1)}, bf16[256,2048]{1,0:T(8,128)(2,1)}, u32[]{:S(2)}) %copy-start.2) | copy-done | bytes 1048600
  30.5 9.2 %queries.1.q_ref = bf16[16,256,128]{2,1,0:T(8,128)(2,1)S(1)} custom-call(bf16[256,2048]{1,0:T(8,128)(2,1)S(1)} %copy-done.2, bf16[2048,2048]{1,0:T(8,128)(2,1)S(1)} %copy-done, f32[256,256]{1,0:T(8,128)S(1)} %get-tuple-element.34.tab_ref), custom_call_target="tpu_custom_call" | custom-call | flops 2147483648 | bytes 9437184 | tf_op jit(solution)/shard_map/queries/pallas_call | solution.py:305
  39.7 1.3 %collective-permute-start.5 = (bf16[256,256]{1,0:T(8,128)(2,1)S(1)}, bf16[256,256]{1,0:T(8,128)(2,1)S(1)}, u32[]{:S(2)}, u32[]{:S(2)}) collective-permute-start(bf16[256,256]{1,0:T(8,128)(2,1)S(1)} %collective-permute-done.3.v0), channel_id=1, source_target_pairs={{1,0},{3,2},{5,4},{7,6},{9,8},{11,10},{13,12},{15,14},{17,16},{19,... | collective-permute-start | bytes 393224 | tf_op jit(solution)/shard_map/ppermute | solution.py:341
  41.0 1.3 %collective-permute-start.4 = (bf16[272,256]{1,0:T(8,128)(2,1)S(1)}, bf16[272,256]{1,0:T(8,128)(2,1)S(1)}, u32[]{:S(2)}, u32[]{:S(2)}) collective-permute-start(bf16[272,256]{1,0:T(8,128)(2,1)S(1)} %collective-permute-done.1.k0), channel_id=1, source_target_pairs={{1,0},{3,2},{5,4},{7,6},{9,8},{11,10},{13,12},{15,14},{17,16},{19,... | collective-permute-start | bytes 417800 | tf_op jit(solution)/shard_map/ppermute | solution.py:340
  42.3 3.8 %near_attention.1.near_ref = f32[16,256,256]{2,1,0:T(8,128)S(1)} custom-call(bf16[16,256,128]{2,1,0:T(8,128)(2,1)S(1)} %queries.1.q_ref, bf16[272,256]{1,0:T(8,128)(2,1)S(1)} %get-tuple-element.35.refs_0_, bf16[256,256]{1,0:T(8,128)(2,1)S(1)} %get-tuple-element.31.refs_1_, bf16[272,256]{1,0:T(8,128)(2,1)S(1)} %collective-permute-done.6.refs_2_, ...), custom_call_target="tpu_custom_call" | custom-call | flops 2147483648 | bytes 8388608 | tf_op jit(solution)/shard_map/near_attention/pallas_call | solution.py:347
  46.2 3.1 %far_attention_project.1 = (bf16[256,2048]{1,0:T(8,128)(2,1)S(1)}, bf16[256,256]{1,0:T(8,128)(2,1)S(1)}, bf16[256,768]{1,0:T(8,128)(2,1)S(1)}) custom-call(bf16[16,256,128]{2,1,0:T(8,128)(2,1)S(1)} %queries.1.q_ref, s32[1,256]{1,0:T(1,128)S(1)} %bitcast.5, bf16[272,256]{1,0:T(8,128)(2,1)S(1)} %collective-permute-done.1.k0, ...), custom_call_target="tpu_custom_call" | custom-call | flops 2147483648 | bytes 10485760 | tf_op jit(solution)/shard_map/far_attention_project/pallas_call | solution.py:357
  49.3 1.5 %collective-permute-start.17 = (bf16[256,768]{1,0:T(8,128)(2,1)S(1)}, bf16[256,768]{1,0:T(8,128)(2,1)S(1)}, u32[]{:S(2)}, u32[]{:S(2)}) collective-permute-start(bf16[256,768]{1,0:T(8,128)(2,1)S(1)} %get-tuple-element.49), channel_id=1, source_target_pairs={{0,2},{2,0},{1,3},{3,1},{4,6},{6,4},{5,7},{7,5},{8,10},{10,8},{9,1... | collective-permute-start | bytes 1179656 | tf_op jit(solution)/shard_map/ppermute | solution.py:377
  51.1 2.5 %project_own.1 = (bf16[256,256]{1,0:T(8,128)(2,1)S(1)}, bf16[256,768]{1,0:T(8,128)(2,1)S(1)}) custom-call(bf16[256,2048]{1,0:T(8,128)(2,1)S(1)} %get-tuple-element.36.att_ref, bf16[2048,2048]{1,0:T(8,128)(2,1)S(1)} %bitcast.3), custom_call_target="tpu_custom_call" | custom-call | flops 1073741824 | bytes 5242880 | tf_op jit(solution)/shard_map/project_own/pallas_call | solution.py:379
  53.6 4.1 %collective-permute-done.17.refs_1_ = bf16[256,768]{1,0:T(8,128)(2,1)S(1)} collective-permute-done((bf16[256,768]{1,0:T(8,128)(2,1)S(1)}, bf16[256,768]{1,0:T(8,128)(2,1)S(1)}, u32[]{:S(2)}, u32[]{:S(2)}) %collective-permute-start.17) | collective-permute-done | bytes 393248 | tf_op jit(solution)/shard_map/ppermute | solution.py:377
  58.1 8.1 %collective-permute-start.18 = (bf16[96,768]{1,0:T(8,128)(2,1)S(1)}, bf16[96,768]{1,0:T(8,128)(2,1)S(1)}, u32[]{:S(2)}, u32[]{:S(2)}) collective-permute-start(bf16[96,768]{1,0:T(8,128)(2,1)S(1)} %get-tuple-element.51), channel_id=1, source_target_pairs={{0,4},{4,0},{8,12},{12,8},{1,5},{5,1},{9,13},{13,9},{2,6},{6,2},{1... | collective-permute-start | bytes 442376 | tf_op jit(solution)/shard_map/ppermute | solution.py:402
  66.2 5.5 %collective-permute-start.19 = (bf16[96,768]{1,0:T(8,128)(2,1)S(1)}, bf16[96,768]{1,0:T(8,128)(2,1)S(1)}, u32[]{:S(2)}, u32[]{:S(2)}) collective-permute-start(bf16[96,768]{1,0:T(8,128)(2,1)S(1)} %get-tuple-element.52), channel_id=1, source_target_pairs={{0,8},{4,12},{8,0},{12,4},{1,9},{5,13},{9,1},{13,5},{2,10},{6,14},... | collective-permute-start | bytes 442376 | tf_op jit(solution)/shard_map/ppermute | solution.py:402
  71.7 1.4 %collective-permute-start.20 = (bf16[96,768]{1,0:T(8,128)(2,1)S(1)}, bf16[96,768]{1,0:T(8,128)(2,1)S(1)}, u32[]{:S(2)}, u32[]{:S(2)}) collective-permute-start(bf16[96,768]{1,0:T(8,128)(2,1)S(1)} %get-tuple-element.53), channel_id=1, source_target_pairs={{0,12},{4,8},{8,4},{12,0},{1,13},{5,9},{9,5},{13,1},{2,14},{6,10},... | collective-permute-start | bytes 442376 | tf_op jit(solution)/shard_map/ppermute | solution.py:402
  73.7 2.4 %collective-permute-start.15 = (s32[8,128]{1,0:T(8,128)S(1)}, s32[8,128]{1,0:T(8,128)S(1)}, u32[]{:S(2)}, u32[]{:S(2)}) collective-permute-start(s32[8,128]{1,0:T(8,128)S(1)} %get-tuple-element.45), channel_id=1, source_target_pairs={{0,8},{4,12},{8,0},{12,4},{1,9},{5,13},{9,1},{13,5},{2,10},{6,14},... | collective-permute-start | bytes 12296 | tf_op jit(solution)/shard_map/ppermute | solution.py:335
  76.1 1.7 %collective-permute-done.14.refs_5_ = s32[8,128]{1,0:T(8,128)S(1)} collective-permute-done((s32[8,128]{1,0:T(8,128)S(1)}, s32[8,128]{1,0:T(8,128)S(1)}, u32[]{:S(2)}, u32[]{:S(2)}) %collective-permute-start.14) | collective-permute-done | bytes 4128 | tf_op jit(solution)/shard_map/ppermute | solution.py:335
  77.8 2.4 %collective-permute-start.16 = (s32[8,128]{1,0:T(8,128)S(1)}, s32[8,128]{1,0:T(8,128)S(1)}, u32[]{:S(2)}, u32[]{:S(2)}) collective-permute-start(s32[8,128]{1,0:T(8,128)S(1)} %get-tuple-element.46), channel_id=1, source_target_pairs={{0,12},{4,8},{8,4},{12,0},{1,13},{5,9},{9,5},{13,1},{2,14},{6,10},... | collective-permute-start | bytes 12296 | tf_op jit(solution)/shard_map/ppermute | solution.py:335
  80.2 5.3 %collective-permute-done.15.refs_6_ = s32[8,128]{1,0:T(8,128)S(1)} collective-permute-done((s32[8,128]{1,0:T(8,128)S(1)}, s32[8,128]{1,0:T(8,128)S(1)}, u32[]{:S(2)}, u32[]{:S(2)}) %collective-permute-start.15) | collective-permute-done | bytes 4128 | tf_op jit(solution)/shard_map/ppermute | solution.py:335
  86.6 1.5 %collective-permute-start.10 = (bf16[256,256]{1,0:T(8,128)(2,1)S(1)}, bf16[256,256]{1,0:T(8,128)(2,1)S(1)}, u32[]{:S(2)}, u32[]{:S(2)}) collective-permute-start(bf16[256,256]{1,0:T(8,128)(2,1)S(1)} %get-tuple-element.38), channel_id=1, source_target_pairs={{0,2},{2,0},{1,3},{3,1},{4,6},{6,4},{5,7},{7,5},{8,10},{10,8},{9,1... | collective-permute-start | bytes 393224 | tf_op jit(solution)/shard_map/ppermute | solution.py:377
  88.2 4.4 %collective-permute-done.10.refs_1_ = bf16[256,256]{1,0:T(8,128)(2,1)S(1)} collective-permute-done((bf16[256,256]{1,0:T(8,128)(2,1)S(1)}, bf16[256,256]{1,0:T(8,128)(2,1)S(1)}, u32[]{:S(2)}, u32[]{:S(2)}) %collective-permute-start.10) | collective-permute-done | bytes 131104 | tf_op jit(solution)/shard_map/ppermute | solution.py:377
  93.4 1.2 %collective-permute-start.12 = (bf16[96,256]{1,0:T(8,128)(2,1)S(1)}, bf16[96,256]{1,0:T(8,128)(2,1)S(1)}, u32[]{:S(2)}, u32[]{:S(2)}) collective-permute-start(bf16[96,256]{1,0:T(8,128)(2,1)S(1)} %get-tuple-element.41), channel_id=1, source_target_pairs={{0,8},{4,12},{8,0},{12,4},{1,9},{5,13},{9,1},{13,5},{2,10},{6,14},... | collective-permute-start | bytes 147464 | tf_op jit(solution)/shard_map/ppermute | solution.py:402
  94.7 2.5 %collective-permute-start.13 = (bf16[96,256]{1,0:T(8,128)(2,1)S(1)}, bf16[96,256]{1,0:T(8,128)(2,1)S(1)}, u32[]{:S(2)}, u32[]{:S(2)}) collective-permute-start(bf16[96,256]{1,0:T(8,128)(2,1)S(1)} %get-tuple-element.42), channel_id=1, source_target_pairs={{0,12},{4,8},{8,4},{12,0},{1,13},{5,9},{9,5},{13,1},{2,14},{6,10},... | collective-permute-start | bytes 147464 | tf_op jit(solution)/shard_map/ppermute | solution.py:402
  97.4 2.1 %collective-permute-done.12.refs_2_ = bf16[96,256]{1,0:T(8,128)(2,1)S(1)} collective-permute-done((bf16[96,256]{1,0:T(8,128)(2,1)S(1)}, bf16[96,256]{1,0:T(8,128)(2,1)S(1)}, u32[]{:S(2)}, u32[]{:S(2)}) %collective-permute-start.12) | collective-permute-done | bytes 49184 | tf_op jit(solution)/shard_map/ppermute | solution.py:402
  101.1 1.3 %collective-permute-done.21.refs_2_ = bf16[256,256]{1,0:T(8,128)(2,1)S(1)} collective-permute-done((bf16[256,256]{1,0:T(8,128)(2,1)S(1)}, bf16[256,256]{1,0:T(8,128)(2,1)S(1)}, u32[]{:S(2)}, u32[]{:S(2)}) %collective-permute-start.21) | collective-permute-done | bytes 131104 | tf_op jit(solution)/shard_map/ppermute | solution.py:413
  (46 shorter events, 8.1 us)
Async XLA Ops:
  0.0 1.2 %copy-start.1 = (bf16[256,2048]{1,0:T(8,128)(2,1)S(1)}, bf16[256,2048]{1,0:T(8,128)(2,1)}, u32[]{:S(2)}) copy-start(bf16[256,2048]{1,0:T(8,128)(2,1)} %x_ref.3) | copy-start | bytes 3145732
  1.2 1.2 %copy-start.3 = (bf16[2048,256]{1,0:T(8,128)(2,1)S(1)}, bf16[2048,256]{1,0:T(8,128)(2,1)}, u32[]{:S(2)}) copy-start(bf16[2048,256]{1,0:T(8,128)(2,1)} %wk_ref.1) | copy-start | bytes 3145732
  2.5 1.2 %copy-start.4 = (bf16[2048,256]{1,0:T(8,128)(2,1)S(1)}, bf16[2048,256]{1,0:T(8,128)(2,1)}, u32[]{:S(2)}) copy-start(bf16[2048,256]{1,0:T(8,128)(2,1)} %wv_ref.1) | copy-start | bytes 3145732
  6.5 15.3 %collective-permute-start = (bf16[272,256]{1,0:T(8,128)(2,1)S(1)}, bf16[272,256]{1,0:T(8,128)(2,1)S(1)}, u32[]{:S(2)}, u32[]{:S(2)}) collective-permute-start(bf16[272,256]{1,0:T(8,128)(2,1)S(1)} %get-tuple-element.35.refs_0_), channel_id=1, source_target_pairs={{0,4},{4,8},{8,12},{1,5},{5,9},{9,13},{2,6},{6,10},{10,14},{3,7},{... | collective-permute-start | bytes 417800 | tf_op jit(solution)/shard_map/ppermute | solution.py:301
  11.5 6.1 %collective-permute-start.2 = (bf16[256,256]{1,0:T(8,128)(2,1)S(1)}, bf16[256,256]{1,0:T(8,128)(2,1)S(1)}, u32[]{:S(2)}, u32[]{:S(2)}) collective-permute-start(bf16[256,256]{1,0:T(8,128)(2,1)S(1)} %get-tuple-element.31.refs_1_), channel_id=1, source_target_pairs={{0,4},{4,8},{8,12},{1,5},{5,9},{9,13},{2,6},{6,10},{10,14},{3,7},{... | collective-permute-start | bytes 393224 | tf_op jit(solution)/shard_map/ppermute | solution.py:302
  14.9 7.2 %collective-permute-start.7 = (bf16[256,256]{1,0:T(8,128)(2,1)S(1)}, bf16[256,256]{1,0:T(8,128)(2,1)S(1)}, u32[]{:S(2)}, u32[]{:S(2)}) collective-permute-start(bf16[256,256]{1,0:T(8,128)(2,1)S(1)} %get-tuple-element.31.refs_1_), channel_id=1, source_target_pairs={{0,1},{2,3},{4,5},{6,7},{8,9},{10,11},{12,13},{14,15},{16,17},{18,... | collective-permute-start | bytes 393224 | tf_op jit(solution)/shard_map/ppermute | solution.py:341
  16.2 26.1 %collective-permute-start.6 = (bf16[272,256]{1,0:T(8,128)(2,1)S(1)}, bf16[272,256]{1,0:T(8,128)(2,1)S(1)}, u32[]{:S(2)}, u32[]{:S(2)}) collective-permute-start(bf16[272,256]{1,0:T(8,128)(2,1)S(1)} %get-tuple-element.35.refs_0_), channel_id=1, source_target_pairs={{0,1},{2,3},{4,5},{6,7},{8,9},{10,11},{12,13},{14,15},{16,17},{18,... | collective-permute-start | bytes 417800 | tf_op jit(solution)/shard_map/ppermute | solution.py:340
  17.6 24.7 %collective-permute-start.9 = (bf16[256,256]{1,0:T(8,128)(2,1)S(1)}, bf16[256,256]{1,0:T(8,128)(2,1)S(1)}, u32[]{:S(2)}, u32[]{:S(2)}) collective-permute-start(bf16[256,256]{1,0:T(8,128)(2,1)S(1)} %collective-permute-done.2.refs_5_), channel_id=1, source_target_pairs={{0,1},{1,0},{2,3},{3,2},{4,5},{5,4},{6,7},{7,6},{8,9},{9,8},{10,11... | collective-permute-start | bytes 393224 | tf_op jit(solution)/shard_map/ppermute | solution.py:341
  17.6 22.0 %collective-permute-start.3 = (bf16[256,256]{1,0:T(8,128)(2,1)S(1)}, bf16[256,256]{1,0:T(8,128)(2,1)S(1)}, u32[]{:S(2)}, u32[]{:S(2)}) collective-permute-start(bf16[256,256]{1,0:T(8,128)(2,1)S(1)} %collective-permute-done.2.refs_5_), channel_id=1, source_target_pairs={{0,4},{4,8},{8,12},{1,5},{5,9},{9,13},{2,6},{6,10},{10,14},{3,7},{... | collective-permute-start | bytes 393224 | tf_op jit(solution)/shard_map/ppermute | solution.py:302
  21.8 20.5 %collective-permute-start.8 = (bf16[272,256]{1,0:T(8,128)(2,1)S(1)}, bf16[272,256]{1,0:T(8,128)(2,1)S(1)}, u32[]{:S(2)}, u32[]{:S(2)}) collective-permute-start(bf16[272,256]{1,0:T(8,128)(2,1)S(1)} %collective-permute-done.refs_4_), channel_id=1, source_target_pairs={{0,1},{1,0},{2,3},{3,2},{4,5},{5,4},{6,7},{7,6},{8,9},{9,8},{10,11... | collective-permute-start | bytes 417800 | tf_op jit(solution)/shard_map/ppermute | solution.py:340
  22.1 18.9 %collective-permute-start.1 = (bf16[272,256]{1,0:T(8,128)(2,1)S(1)}, bf16[272,256]{1,0:T(8,128)(2,1)S(1)}, u32[]{:S(2)}, u32[]{:S(2)}) collective-permute-start(bf16[272,256]{1,0:T(8,128)(2,1)S(1)} %collective-permute-done.refs_4_), channel_id=1, source_target_pairs={{0,4},{4,8},{8,12},{1,5},{5,9},{9,13},{2,6},{6,10},{10,14},{3,7},{... | collective-permute-start | bytes 417800 | tf_op jit(solution)/shard_map/ppermute | solution.py:301
  25.6 20.6 %slice-start = ((s8[8388608]{0:T(1024)(128)(4,1)}), s8[4194304]{0:T(1024)(128)(4,1)S(1)}, s32[]{:S(2)}) async-start(s8[8388608]{0:T(1024)(128)(4,1)} %bitcast.2), calls=%async_computation | async-start | bytes 8388608
  25.6 3.5 %copy-start = (bf16[2048,2048]{1,0:T(8,128)(2,1)S(1)}, bf16[2048,2048]{1,0:T(8,128)(2,1)}, u32[]{:S(2)}) copy-start(bf16[2048,2048]{1,0:T(8,128)(2,1)} %w_ref.3) | copy-start | bytes 25165828
  29.1 1.3 %copy-start.2 = (bf16[256,2048]{1,0:T(8,128)(2,1)S(1)}, bf16[256,2048]{1,0:T(8,128)(2,1)}, u32[]{:S(2)}) copy-start(bf16[256,2048]{1,0:T(8,128)(2,1)} %x_ref.3) | copy-start | bytes 3145732
  30.5 15.7 %slice-start.1 = ((s8[8388608]{0:T(1024)(128)(4,1)}), s8[4194304]{0:T(1024)(128)(4,1)S(1)}, s32[]{:S(2)}) async-start(s8[8388608]{0:T(1024)(128)(4,1)} %bitcast.2), calls=%async_computation.1 | async-start | bytes 8388608
  30.5 15.7 %copy-start.6 = (s32[256]{0:T(256)S(1)}, s32[256]{0:T(256)}, u32[]{:S(2)}) copy-start(s32[256]{0:T(256)} %param.8) | copy-start | bytes 3076
  39.7 6.4 %collective-permute-start.5 = (bf16[256,256]{1,0:T(8,128)(2,1)S(1)}, bf16[256,256]{1,0:T(8,128)(2,1)S(1)}, u32[]{:S(2)}, u32[]{:S(2)}) collective-permute-start(bf16[256,256]{1,0:T(8,128)(2,1)S(1)} %collective-permute-done.3.v0), channel_id=1, source_target_pairs={{1,0},{3,2},{5,4},{7,6},{9,8},{11,10},{13,12},{15,14},{17,16},{19,... | collective-permute-start | bytes 393224 | tf_op jit(solution)/shard_map/ppermute | solution.py:341
  41.0 5.1 %collective-permute-start.4 = (bf16[272,256]{1,0:T(8,128)(2,1)S(1)}, bf16[272,256]{1,0:T(8,128)(2,1)S(1)}, u32[]{:S(2)}, u32[]{:S(2)}) collective-permute-start(bf16[272,256]{1,0:T(8,128)(2,1)S(1)} %collective-permute-done.1.k0), channel_id=1, source_target_pairs={{1,0},{3,2},{5,4},{7,6},{9,8},{11,10},{13,12},{15,14},{17,16},{19,... | collective-permute-start | bytes 417800 | tf_op jit(solution)/shard_map/ppermute | solution.py:340
  46.1 4.7 %copy-start.7 = (s32[256]{0:T(256)S(1)}, s32[256]{0:T(256)}, u32[]{:S(2)}) copy-start(s32[256]{0:T(256)} %param.9) | copy-start | bytes 3076
  49.3 8.5 %collective-permute-start.17 = (bf16[256,768]{1,0:T(8,128)(2,1)S(1)}, bf16[256,768]{1,0:T(8,128)(2,1)S(1)}, u32[]{:S(2)}, u32[]{:S(2)}) collective-permute-start(bf16[256,768]{1,0:T(8,128)(2,1)S(1)} %get-tuple-element.49), channel_id=1, source_target_pairs={{0,2},{2,0},{1,3},{3,1},{4,6},{6,4},{5,7},{7,5},{8,10},{10,8},{9,1... | collective-permute-start | bytes 1179656 | tf_op jit(solution)/shard_map/ppermute | solution.py:377
  58.1 27.4 %collective-permute-start.18 = (bf16[96,768]{1,0:T(8,128)(2,1)S(1)}, bf16[96,768]{1,0:T(8,128)(2,1)S(1)}, u32[]{:S(2)}, u32[]{:S(2)}) collective-permute-start(bf16[96,768]{1,0:T(8,128)(2,1)S(1)} %get-tuple-element.51), channel_id=1, source_target_pairs={{0,4},{4,0},{8,12},{12,8},{1,5},{5,1},{9,13},{13,9},{2,6},{6,2},{1... | collective-permute-start | bytes 442376 | tf_op jit(solution)/shard_map/ppermute | solution.py:402
  66.2 19.4 %collective-permute-start.19 = (bf16[96,768]{1,0:T(8,128)(2,1)S(1)}, bf16[96,768]{1,0:T(8,128)(2,1)S(1)}, u32[]{:S(2)}, u32[]{:S(2)}) collective-permute-start(bf16[96,768]{1,0:T(8,128)(2,1)S(1)} %get-tuple-element.52), channel_id=1, source_target_pairs={{0,8},{4,12},{8,0},{12,4},{1,9},{5,13},{9,1},{13,5},{2,10},{6,14},... | collective-permute-start | bytes 442376 | tf_op jit(solution)/shard_map/ppermute | solution.py:402
  71.7 13.8 %collective-permute-start.20 = (bf16[96,768]{1,0:T(8,128)(2,1)S(1)}, bf16[96,768]{1,0:T(8,128)(2,1)S(1)}, u32[]{:S(2)}, u32[]{:S(2)}) collective-permute-start(bf16[96,768]{1,0:T(8,128)(2,1)S(1)} %get-tuple-element.53), channel_id=1, source_target_pairs={{0,12},{4,8},{8,4},{12,0},{1,13},{5,9},{9,5},{13,1},{2,14},{6,10},... | collective-permute-start | bytes 442376 | tf_op jit(solution)/shard_map/ppermute | solution.py:402
  73.1 4.7 %collective-permute-start.14 = (s32[8,128]{1,0:T(8,128)S(1)}, s32[8,128]{1,0:T(8,128)S(1)}, u32[]{:S(2)}, u32[]{:S(2)}) collective-permute-start(s32[8,128]{1,0:T(8,128)S(1)} %get-tuple-element.44), channel_id=1, source_target_pairs={{0,4},{4,0},{8,12},{12,8},{1,5},{5,1},{9,13},{13,9},{2,6},{6,2},{1... | collective-permute-start | bytes 12296 | tf_op jit(solution)/shard_map/ppermute | solution.py:335
  73.7 11.9 %collective-permute-start.15 = (s32[8,128]{1,0:T(8,128)S(1)}, s32[8,128]{1,0:T(8,128)S(1)}, u32[]{:S(2)}, u32[]{:S(2)}) collective-permute-start(s32[8,128]{1,0:T(8,128)S(1)} %get-tuple-element.45), channel_id=1, source_target_pairs={{0,8},{4,12},{8,0},{12,4},{1,9},{5,13},{9,1},{13,5},{2,10},{6,14},... | collective-permute-start | bytes 12296 | tf_op jit(solution)/shard_map/ppermute | solution.py:335
  77.8 7.7 %collective-permute-start.16 = (s32[8,128]{1,0:T(8,128)S(1)}, s32[8,128]{1,0:T(8,128)S(1)}, u32[]{:S(2)}, u32[]{:S(2)}) collective-permute-start(s32[8,128]{1,0:T(8,128)S(1)} %get-tuple-element.46), channel_id=1, source_target_pairs={{0,12},{4,8},{8,4},{12,0},{1,13},{5,9},{9,5},{13,1},{2,14},{6,10},... | collective-permute-start | bytes 12296 | tf_op jit(solution)/shard_map/ppermute | solution.py:335
  86.5 15.9 %collective-permute-start.22 = (bf16[256,768]{1,0:T(8,128)(2,1)S(1)}, bf16[256,768]{1,0:T(8,128)(2,1)S(1)}, u32[]{:S(2)}, u32[]{:S(2)}) collective-permute-start(bf16[256,768]{1,0:T(8,128)(2,1)S(1)} %get-tuple-element.56), channel_id=1, source_target_pairs={{0,1},{1,0},{2,3},{3,2},{4,5},{5,4},{6,7},{7,6},{8,9},{9,8},{10,11... | collective-permute-start | bytes 1179656 | tf_op jit(solution)/shard_map/ppermute | solution.py:413
  86.6 5.9 %collective-permute-start.10 = (bf16[256,256]{1,0:T(8,128)(2,1)S(1)}, bf16[256,256]{1,0:T(8,128)(2,1)S(1)}, u32[]{:S(2)}, u32[]{:S(2)}) collective-permute-start(bf16[256,256]{1,0:T(8,128)(2,1)S(1)} %get-tuple-element.38), channel_id=1, source_target_pairs={{0,2},{2,0},{1,3},{3,1},{4,6},{6,4},{5,7},{7,5},{8,10},{10,8},{9,1... | collective-permute-start | bytes 393224 | tf_op jit(solution)/shard_map/ppermute | solution.py:377
  92.8 4.6 %collective-permute-start.11 = (bf16[96,256]{1,0:T(8,128)(2,1)S(1)}, bf16[96,256]{1,0:T(8,128)(2,1)S(1)}, u32[]{:S(2)}, u32[]{:S(2)}) collective-permute-start(bf16[96,256]{1,0:T(8,128)(2,1)S(1)} %get-tuple-element.40), channel_id=1, source_target_pairs={{0,4},{4,0},{8,12},{12,8},{1,5},{5,1},{9,13},{13,9},{2,6},{6,2},{1... | collective-permute-start | bytes 147464 | tf_op jit(solution)/shard_map/ppermute | solution.py:402
  93.4 6.0 %collective-permute-start.12 = (bf16[96,256]{1,0:T(8,128)(2,1)S(1)}, bf16[96,256]{1,0:T(8,128)(2,1)S(1)}, u32[]{:S(2)}, u32[]{:S(2)}) collective-permute-start(bf16[96,256]{1,0:T(8,128)(2,1)S(1)} %get-tuple-element.41), channel_id=1, source_target_pairs={{0,8},{4,12},{8,0},{12,4},{1,9},{5,13},{9,1},{13,5},{2,10},{6,14},... | collective-permute-start | bytes 147464 | tf_op jit(solution)/shard_map/ppermute | solution.py:402
  94.7 5.9 %collective-permute-start.13 = (bf16[96,256]{1,0:T(8,128)(2,1)S(1)}, bf16[96,256]{1,0:T(8,128)(2,1)S(1)}, u32[]{:S(2)}, u32[]{:S(2)}) collective-permute-start(bf16[96,256]{1,0:T(8,128)(2,1)S(1)} %get-tuple-element.42), channel_id=1, source_target_pairs={{0,12},{4,8},{8,4},{12,0},{1,13},{5,9},{9,5},{13,1},{2,14},{6,10},... | collective-permute-start | bytes 147464 | tf_op jit(solution)/shard_map/ppermute | solution.py:402
  101.0 1.4 %collective-permute-start.21 = (bf16[256,256]{1,0:T(8,128)(2,1)S(1)}, bf16[256,256]{1,0:T(8,128)(2,1)S(1)}, u32[]{:S(2)}, u32[]{:S(2)}) collective-permute-start(bf16[256,256]{1,0:T(8,128)(2,1)S(1)} %get-tuple-element.55), channel_id=1, source_target_pairs={{0,1},{1,0},{2,3},{3,2},{4,5},{5,4},{6,7},{7,6},{8,9},{9,8},{10,11... | collective-permute-start | bytes 393224 | tf_op jit(solution)/shard_map/ppermute | solution.py:413
  (1 other events, 0.7 us)

commit v2 on v1

v2 whole, which is shorter than its diff:
```python
import functools
import math

import jax
import jax.numpy as jnp
from jax import lax
from jax.experimental import pallas as pl
from jax.experimental.pallas import tpu as pltpu
from jax.sharding import PartitionSpec as P

HD = 128
THETA = 1000000.0
EPSILON = 1e-06
HIDE = -1e30
F32 = jnp.float32
BF16 = jnp.bfloat16
VMEM = pl.BlockSpec(memory_space=pltpu.VMEM)
ANY = pl.BlockSpec(memory_space=pl.ANY)
MIB = 1 << 20
KV_MIB = 53
Q_MIB = 51
FAR_MIB = 44
PROJECT_MIB = 48


def params(mib):
    return pltpu.CompilerParams(vmem_limit_bytes=mib * MIB)


def cost(flops, nbytes, trans=0):
    return pl.CostEstimate(flops=int(flops), bytes_accessed=int(nbytes), transcendentals=int(trans))


def column_of(row):
    n = row.shape[1]
    at = lax.broadcasted_iota(jnp.int32, (n, n), 0) == lax.broadcasted_iota(jnp.int32, (n, n), 1)
    return jnp.sum(jnp.where(at, row, 0.0), axis=1, keepdims=True)


def norm_rope(heads, cosine, sine, factor):
    scale = lax.rsqrt(jnp.mean(heads * heads, axis=-1, keepdims=True) + EPSILON)
    if factor != 1.0:
        scale = scale * factor
    turned = pltpu.roll(heads, HD // 2, 1)
    return ((heads * cosine + turned * sine) * scale).astype(BF16)


def kv_kernel(parts, x_hbm, wk_hbm, wv_hbm, seg_ref, kv_ref, tab_ref, x_buf, w_buf, sem):
    rows, width = x_buf.shape
    kv_cols = w_buf.shape[1] // 2
    depth = width // parts
    copies = []
    for i in range(parts):
        at = pl.ds(i * depth, depth)
        copies.append([
            pltpu.make_async_copy(x_hbm.at[:, at], x_buf.at[:, at], sem.at[3 * i]),
            pltpu.make_async_copy(wk_hbm.at[at, :], w_buf.at[at, pl.ds(0, kv_cols)], sem.at[3 * i + 1]),
            pltpu.make_async_copy(wv_hbm.at[at, :], w_buf.at[at, pl.ds(kv_cols, kv_cols)], sem.at[3 * i + 2]),
        ])
        for copy in copies[-1]:
            copy.start()
    first = (lax.axis_index("ctx") * 2 + lax.axis_index("rep")) * rows
    lane = lax.broadcasted_iota(jnp.int32, (1, HD), 1)
    freq = jnp.exp(lax.rem(lane, HD // 2).astype(F32) * (-2.0 * math.log(THETA) / HD))
    pos = (first + lax.broadcasted_iota(jnp.int32, (rows, HD), 0)).astype(F32)
    angle = pos * freq
    tab_ref[:, :HD] = jnp.cos(angle)
    tab_ref[:, HD:] = jnp.where(lane < HD // 2, -1.0, 1.0) * jnp.sin(angle)
    line = lax.broadcasted_iota(jnp.int32, (16, kv_cols), 0)
    segs = jnp.zeros((16, kv_cols), F32)
    for i in range(rows // kv_cols):
        segs = jnp.where(line == i, seg_ref[:, i * kv_cols:(i + 1) * kv_cols].astype(F32), segs)
    kv_ref[rows:, :kv_cols] = segs.astype(BF16)
    kv_ref[rows:, kv_cols:] = jnp.zeros((16, kv_cols), BF16)
    total = None
    for i in range(parts):
        for copy in copies[i]:
            copy.wait()
        at = slice(i * depth, (i + 1) * depth)
        part = jnp.dot(x_buf[:, at], w_buf[at, :], preferred_element_type=F32)
        total = part if total is None else total + part
    for at in range(0, kv_cols, HD):
        kv_ref[0:rows, at:at + HD] = norm_rope(total[:, at:at + HD], tab_ref[:, :HD], tab_ref[:, HD:], 1.0)
    kv_ref[0:rows, kv_cols:] = total[:, kv_cols:].astype(BF16)


def q_kernel(parts, x_hbm, w_hbm, tab_ref, q_ref, x_ref, w_buf, sem):
    heads = q_ref.shape[0]
    wide = w_buf.shape[1] // parts
    factor = math.log2(math.e) / math.sqrt(HD)
    tokens = pltpu.make_async_copy(x_hbm, x_ref, sem.at[parts])
    tokens.start()
    copies = []
    for i in range(parts):
        at = pl.ds(i * wide, wide)
        copies.append(pltpu.make_async_copy(w_hbm.at[:, at], w_buf.at[:, at], sem.at[i]))
        copies[-1].start()

    def finish(i, flat):
        for j in range(wide // HD):
            done = norm_rope(flat[:, j * HD:(j + 1) * HD], tab_ref[:, :HD], tab_ref[:, HD:], factor)
            q_ref[i * (wide // HD) + j] = done

    held = None
    tokens.wait()
    for i in range(parts):
        copies[i].wait()
        flat = jnp.dot(x_ref[...], w_buf[:, i * wide:(i + 1) * wide], preferred_element_type=F32)
        if i:
            finish(i - 1, held)
        held = flat
    finish(parts - 1, held)


def route_kernel(ctx, cap, dest_ref, pos_ref, *slot_refs):
    rows = dest_ref.shape[1]
    mine_c, mine_r = lax.axis_index("ctx"), lax.axis_index("rep")
    dest = dest_ref[...]
    owner = lax.div(dest, rows)
    slot = dest - owner * rows
    owner_col = column_of(owner.astype(F32))
    ii = lax.broadcasted_iota(jnp.int32, (rows, rows), 0)
    jj = lax.broadcasted_iota(jnp.int32, (rows, rows), 1)
    before = (owner_col == owner.astype(F32)) & (ii < jj)
    rank = jnp.sum(jnp.where(before, 1.0, 0.0), axis=0, keepdims=True).astype(jnp.int32)
    near_c = jnp.bitwise_xor(lax.div(owner, 2), mine_c)
    near_r = jnp.bitwise_xor(lax.rem(owner, 2), mine_r)
    pos = (near_c * 2 + near_r) * cap + rank
    pos_ref[...] = jnp.broadcast_to(pos, pos_ref.shape)
    pos_col = column_of(pos.astype(F32))
    target_col = column_of(slot.astype(F32)) + 1.0
    lanes = slot_refs[0].shape[1]
    for k in range(ctx):
        lane = lax.broadcasted_iota(jnp.int32, (rows, lanes), 1)
        hit = (pos_col == (lane + k * 2 * cap).astype(F32)) & (lane < 2 * cap)
        got = jnp.sum(jnp.where(hit, target_col, 0.0), axis=0, keepdims=True) - 1.0
        slot_refs[k][...] = jnp.broadcast_to(got, slot_refs[k].shape)


def documents(kv_ref):
    wide = kv_ref.shape[1] // 2
    rows = kv_ref.shape[0] - 16
    lines = kv_ref[rows:rows + 16, :wide].astype(F32)
    return jnp.concatenate([lines[i:i + 1] for i in range(rows // wide)], 1)


def attend(q_ref, blocks, biases, finish):
    heads, rows = q_ref.shape[0], q_ref.shape[1]
    kv_cols = blocks[0].shape[1] // 2
    kv_heads = kv_cols // HD
    groups = heads // kv_heads
    for g in range(kv_heads):
        at = g * HD
        keys = [b[0:rows, at:at + HD] for b in blocks]
        ones = jnp.ones((rows, HD), BF16)
        vals = [jnp.concatenate([b[0:rows, kv_cols + at:kv_cols + at + HD], ones], 1) for b in blocks]
        vals = jnp.concatenate(vals, 0) if len(vals) > 1 else vals[0]

        def head(j, _):
            weights = []
            for key, bias in zip(keys, biases, strict=True):
                s = lax.dot_general(q_ref[j], key, (((1,), (1,)), ((), ())), preferred_element_type=F32)
                weights.append(jnp.exp2(s + bias[...]).astype(BF16))
            p = jnp.concatenate(weights, 1) if len(weights) > 1 else weights[0]
            finish(j, jnp.dot(p, vals, preferred_element_type=F32))
            return 0

        lax.fori_loop(g * groups, (g + 1) * groups, head, 0, unroll=8)


def hide(bias_ref, kv_ref, seg_col):
    bias_ref[...] = jnp.where(documents(kv_ref) == seg_col, 0.0, HIDE)


def choose(to_ref, flag, yes_ref, no_ref):
    @pl.when(flag)
    def _():
        to_ref[...] = yes_ref[...]

    @pl.when(jnp.logical_not(flag))
    def _():
        to_ref[...] = no_ref[...]


def near_kernel(hops, seg_ref, q_ref, *refs):
    hop, pair, out_ref = refs[:hops], refs[hops:2 * hops], refs[2 * hops]
    odd, bias = refs[2 * hops + 1:-1], refs[-1]
    rows = q_ref.shape[1]
    c, r = lax.axis_index("ctx"), lax.axis_index("rep")
    seg = seg_ref[...].astype(F32)
    seg_col = column_of(seg)
    lowest = jnp.min(seg)
    ii = lax.broadcasted_iota(jnp.int32, (rows, rows), 0)
    jj = lax.broadcasted_iota(jnp.int32, (rows, rows), 1)
    bias[0] = jnp.where((seg == seg_col) & (jj <= ii), 0.0, HIDE)
    blocks = [hop[0]]
    for i in range(1, hops):
        choose(odd[i - 1], r == 1, pair[i - 1], pair[i])
        blocks += [odd[i - 1], hop[i]]
    me = c * 2 + r
    size = 3
    for start in range(0, len(blocks), size):
        some = blocks[start:start + size]
        seen = []
        for d in range(start, start + len(some)):
            if d:
                hide(bias.at[d], blocks[d], seg_col)
                seen.append((me >= d) & (jnp.max(documents(blocks[d])) == lowest))
        count = sum([x.astype(jnp.int32) for x in seen]) + (1 if start == 0 else 0)
        for n in range(1, len(some) + 1):
            @pl.when(count == n)
            def _(n=n, start=start, some=some):
                def finish(j, new):
                    if start == 0:
                        out_ref[j] = new
                    else:
                        out_ref[j] += new
                attend(q_ref, some[:n], [bias.at[start + i] for i in range(n)], finish)


def far_kernel(hops, n_other, seg_ref, q_ref, far_ref, to_one, to_zero, near_ref, w_hbm, att_ref, *rest):
    outs, (odd, bias, w_buf, sem) = rest[:n_other], rest[n_other:]
    heads = q_ref.shape[0]
    c, r, h = lax.axis_index("ctx"), lax.axis_index("rep"), lax.axis_index("head")
    start, finish_projection = project(att_ref, w_hbm, w_buf, sem, outs, [(jnp.bitwise_xor(h, d + 1), 0) for d in range(n_other)])
    start()
    seg = seg_ref[...].astype(F32)
    seg_col = column_of(seg)
    lowest = jnp.min(seg)
    choose(odd, r == 1, to_one, to_zero)
    blocks = [odd, far_ref]
    me = c * 2 + r
    seen = []
    for i, d in enumerate((2 * hops - 1, 2 * hops)):
        hide(bias.at[i], blocks[i], seg_col)
        seen.append(((me >= d) & (jnp.max(documents(blocks[i])) == lowest)).astype(jnp.int32))
    count = sum(seen)

    def put(j, both):
        at = j * HD if isinstance(j, int) else pl.multiple_of(j * HD, HD)
        att_ref[:, pl.ds(at, HD)] = (both[:, :HD] / both[:, HD:]).astype(BF16)

    @pl.when(count == 0)
    def _():
        for j in range(heads):
            put(j, near_ref[j])

    for n in (1, 2):
        @pl.when(count == n)
        def _(n=n):
            attend(q_ref, blocks[:n], [bias.at[i] for i in range(n)], lambda j, new: put(j, near_ref[j] + new))

    finish_projection()


def project(att_ref, w_hbm, w_buf, sem, outs, steps):
    half = w_hbm.shape[1] // lax.axis_size("head")
    copies, at = [], 0
    for i, (out, (group, col)) in enumerate(zip(outs, steps, strict=True)):
        wide = out.shape[1]
        from_ = pl.multiple_of(group * half + col, 128)
        copies.append(pltpu.make_async_copy(w_hbm.at[:, pl.ds(from_, wide)], w_buf.at[:, pl.ds(at, wide)], sem.at[i]))
        at += wide

    def start():
        for copy in copies:
            copy.start()

    def finish():
        at = 0
        for out, copy in zip(outs, copies, strict=True):
            copy.wait()
            wide = out.shape[1]
            out[...] = jnp.dot(att_ref[...], w_buf[:, at:at + wide], preferred_element_type=F32).astype(BF16)
            at += wide

    return start, finish


def project_kernel(steps, att_ref, w_hbm, *refs):
    outs, (w_buf, sem) = refs[:len(steps)], refs[len(steps):]
    h = lax.axis_index("head")
    steps = [(jnp.bitwise_xor(h, flip), at) for flip, at in steps]
    start, finish = project(att_ref, w_hbm, w_buf, sem, outs, steps)
    start()
    finish()


def pick_kernel(n_head, ctx, with_slots, span, mark, pos_ref, *refs):
    slots = refs[:ctx] if with_slots else ()
    refs = refs[len(slots):]
    shares, outs = refs[:n_head], refs[n_head:]
    rows = shares[0].shape[0]
    total = shares[0][...].astype(F32)
    for share in shares[1:]:
        total = total + share[...].astype(F32)
    total = total.astype(BF16)
    every = span * ctx
    pick = jnp.where(lax.broadcasted_iota(jnp.int32, (every, rows), 0) == pos_ref[0:1, :], 1.0, 0.0).astype(BF16)
    moved = jnp.dot(pick, total, preferred_element_type=F32).astype(BF16)
    for k, out in enumerate(outs):
        out[0:span, :] = moved[k * span:(k + 1) * span]
        if with_slots:
            out[mark:, :] = jnp.zeros((16, out.shape[1]), BF16)
            lanes = slots[k].shape[1]
            out[mark:, 0:lanes] = jnp.concatenate([slots[k][...]] * 2, 0).astype(BF16)


def place_kernel(ctx, cap, rows, mark, *refs):
    blocks, marked, (mine_ref, pair_ref) = refs[:ctx], refs[ctx:2 * ctx], refs[2 * ctx:]
    span = 2 * cap
    total = None
    for block, marks in zip(blocks, marked, strict=True):
        slot = marks[mark:mark + 16, 0:span].astype(F32)[0:1].astype(jnp.int32)
        lane = lax.broadcasted_iota(jnp.int32, (1, span), 1)
        slot = jnp.where((slot >= 0) & (lane >= cap), slot + rows, slot)
        at = lax.broadcasted_iota(jnp.int32, (2 * rows, span), 0) == slot
        put = jnp.dot(jnp.where(at, 1.0, 0.0).astype(BF16), block[0:span, :], preferred_element_type=F32)
        total = put if total is None else total + put
    mine_ref[...] = total[:rows].astype(BF16)
    pair_ref[...] = total[rows:].astype(BF16)


def join_kernel(n, *refs):
    out = refs[-1]
    at = 0
    for mine, other in zip(refs[:n], refs[n:2 * n], strict=True):
        width = mine.shape[1]
        out[:, at:at + width] = (mine[...].astype(F32) + other[...].astype(F32)).astype(BF16)
        at += width


def after(x, *earlier):
    return lax.optimization_barrier((x, *earlier))[0]


def local(tokens, doc_ids, dest_rows, w_query, w_key, w_value, w_out):
    ctx, rep, n_head = lax.axis_size("ctx"), lax.axis_size("rep"), lax.axis_size("head")
    rows, width = tokens.shape
    kv_cols, q_cols = w_key.shape[1], w_query.shape[1]
    heads = q_cols // HD
    half = w_out.shape[1] // n_head
    others = n_head - 1
    hops = ctx // 2
    cap = 3 * (rows // (2 * ctx * rep))
    span = 2 * cap
    lanes = -(-span // 128) * 128
    every = ctx * span
    sds = jax.ShapeDtypeStruct
    chunks = (half // 2, half - half // 2)

    up = [(i, i + 1) for i in range(ctx - 1)]
    swap = [(0, 1), (1, 0)]
    seg_row = doc_ids.reshape(1, rows)

    parts = 4
    payload = sds((rows + 16, 2 * kv_cols), BF16)
    own, table = pl.pallas_call(
        functools.partial(kv_kernel, parts),
        in_specs=[ANY, ANY, ANY, VMEM],
        out_specs=[VMEM] * 2,
        out_shape=[payload, sds((rows, 2 * HD), F32)],
        scratch_shapes=[
            pltpu.VMEM((rows, width), BF16),
            pltpu.VMEM((width, 2 * kv_cols), BF16),
            pltpu.SemaphoreType.DMA((3 * parts,)),
        ],
        compiler_params=params(KV_MIB),
        cost_estimate=cost(4 * rows * width * kv_cols, 2 * width * (rows + 2 * kv_cols)),
        name="keys_values",
    )(tokens, w_key, w_value, seg_row)

    hop = [own, lax.ppermute(own, "ctx", up)]
    pair = [lax.ppermute(own, "rep", [(0, 1)])]

    parts = 4
    queries = pl.pallas_call(
        functools.partial(q_kernel, parts),
        in_specs=[ANY, ANY, VMEM],
        out_specs=VMEM,
        out_shape=sds((heads, rows, HD), BF16),
        scratch_shapes=[pltpu.VMEM((rows, width), BF16), pltpu.VMEM((width, q_cols), BF16), pltpu.SemaphoreType.DMA((parts + 1,))],
        compiler_params=params(Q_MIB),
        cost_estimate=cost(2 * rows * width * q_cols, 2 * width * (rows + q_cols)),
        name="queries",
    )(tokens, w_query, table)

    for i in range(1, hops + 1):
        if i == 1:
            hop[1] = after(hop[1], queries)
        if i < hops:
            hop.append(lax.ppermute(hop[i], "ctx", up))
            pair.append(lax.ppermute(hop[i], "rep", swap))

    route = pl.pallas_call(
        functools.partial(route_kernel, ctx, cap),
        in_specs=[VMEM],
        out_specs=[VMEM] * (1 + ctx),
        out_shape=[sds((8, rows), jnp.int32)] + [sds((8, lanes), F32)] * ctx,
        compiler_params=params(8),
        cost_estimate=cost(4 * rows * rows, 8 * rows * 4),
        name="routes",
    )
    buffer_pos, *slots = route(after(dest_rows.reshape(1, rows), queries))

    work = heads * rows * rows
    near = pl.pallas_call(
        functools.partial(near_kernel, hops),
        in_specs=[VMEM] * (2 + 2 * hops),
        out_specs=VMEM,
        out_shape=sds((heads, rows, 2 * HD), F32),
        scratch_shapes=[pltpu.VMEM(payload.shape, BF16)] * (hops - 1) + [pltpu.VMEM((2 * hops - 1, rows, rows), F32)],
        compiler_params=params(12),
        cost_estimate=cost(8 * work * HD * hops, 8 * MIB, 2 * work * hops),
        name="near_attention",
    )(after(seg_row, buffer_pos), queries, *hop[:hops], *pair[:hops])

    hop[hops] = after(hop[hops], near)
    pair.append(lax.ppermute(hop[hops], "rep", [(1, 0)]))

    widths = chunks[:1] * others
    attended, *sent = pl.pallas_call(
        functools.partial(far_kernel, hops, others),
        in_specs=[VMEM] * 6 + [ANY],
        out_specs=[VMEM] * (1 + others),
        out_shape=[sds((rows, heads * HD), BF16)] + [sds((rows, n), BF16) for n in widths],
        scratch_shapes=[pltpu.VMEM(payload.shape, BF16), pltpu.VMEM((2, rows, rows), F32)]
        + [pltpu.VMEM((heads * HD, sum(widths)), BF16), pltpu.SemaphoreType.DMA((others,))],
        compiler_params=params(FAR_MIB),
        cost_estimate=cost(8 * work * HD + 2 * rows * heads * HD * chunks[0], 10 * MIB, 2 * work),
        name="far_attention_project",
    )(seg_row, queries, hop[hops], pair[hops - 1], pair[hops], near, w_out)

    def project_some(x, steps, sizes):
        return pl.pallas_call(
            functools.partial(project_kernel, steps),
            in_specs=[VMEM, ANY],
            out_specs=[VMEM] * len(steps),
            out_shape=[sds((rows, n), BF16) for n in sizes],
            scratch_shapes=[pltpu.VMEM((heads * HD, sum(sizes)), BF16), pltpu.SemaphoreType.DMA((len(steps),))],
            compiler_params=params(PROJECT_MIB),
            cost_estimate=cost(2 * rows * heads * HD * sum(sizes), 2 * heads * HD * sum(sizes)),
            name="project",
        )(x, w_out)

    flips = [[(i, i ^ (d + 1)) for i in range(n_head)] for d in range(others)]
    ours, theirs, at = [], [], 0
    for j, n in enumerate(chunks):
        theirs.append([lax.ppermute(x, "head", flip) for x, flip in zip(sent, flips, strict=True)])
        steps, sizes = [(0, at)], [n]
        at += n
        if j + 1 < len(chunks):
            steps += [(d + 1, at) for d in range(others)]
            sizes += [chunks[j + 1]] * others
        mine, *sent = project_some(after(attended, *ours[-1:], *sent), steps, sizes)
        ours.append(mine)

    def across(k):
        return [(i, i ^ k) for i in range(ctx)]

    mark = -(-span // 16) * 16
    moved, got = [], []
    for j, n in enumerate(chunks):
        extra = slots if j == 0 else []
        tall = mark + 16 if j == 0 else span
        picked = pl.pallas_call(
            functools.partial(pick_kernel, n_head, ctx, j == 0, span, mark),
            in_specs=[VMEM] * (1 + len(extra) + n_head),
            out_specs=[VMEM] * ctx,
            out_shape=[sds((tall, n), BF16)] * ctx,
            compiler_params=params(8),
            cost_estimate=cost(2 * every * rows * n, 2 * n * (2 * rows + every)),
            name="add_pick",
        )(after(buffer_pos, *moved), *extra, ours[j], *theirs[j])
        moved += picked
        got.append([picked[0]] + [lax.ppermute(picked[k], "ctx", across(k)) for k in range(1, ctx)])

    kept, gone = [], []
    for j, n in enumerate(chunks):
        first = after(got[j][0], *moved, *kept)
        stay, leave = pl.pallas_call(
            functools.partial(place_kernel, ctx, cap, rows, mark),
            in_specs=[VMEM] * (2 * ctx),
            out_specs=[VMEM] * 2,
            out_shape=[sds((rows, n), BF16)] * 2,
            compiler_params=params(8),
            cost_estimate=cost(4 * every * rows * n, 2 * n * (2 * rows + every)),
            name="place",
        )(first, *got[j][1:], *got[0])
        kept.append(stay)
        gone.append(lax.ppermute(leave, "rep", swap))

    return pl.pallas_call(
        functools.partial(join_kernel, len(chunks)),
        in_specs=[VMEM] * (2 * len(chunks)),
        out_specs=VMEM,
        out_shape=sds((rows, half), BF16),
        compiler_params=params(8),
        cost_estimate=cost(rows * half, 6 * rows * half),
        name="join",
    )(*kept, *gone)


def solution(mesh):
    return jax.shard_map(
        local,
        mesh=mesh,
        in_specs=(
            P(("grp", "ctx", "rep"), None),
            P(("grp", "ctx", "rep")),
            P(("grp", "ctx", "rep")),
            P(None, "head"),
            P(None, "head"),
            P(None, "head"),
            P("head", None),
        ),
        out_specs=P(("grp", "ctx", "rep"), "head"),
        check_vma=False,
    )
```

time: 103 us -> 67.6 us (0.66)
  starting transfers between devices: 49.6 us -> 23.4 us
  local copies, waits for them, and re-layouts: 9.23 us -> 1.98 us
  Pallas kernels: 23.9 us -> 20.8 us
    ppermute x21 -> x13, starting transfers between devices: 49.5 us -> 22.9 us  [the longest x6 9.47 us: local(): lax.ppermute(picked[k], 'ctx', across(k))]
    unnamed x20 -> x8, local copies, waits for them, and re-layouts: 9.23 us -> 1.98 us
    pallas_call x10 -> x11, Pallas kernels: 23 us -> 19.9 us  [the longest x2 5.38 us: project_some(): pl.pallas_call(functools.partial(project_kernel, steps), in_specs=[VMEM,...]
    ppermute x21 -> x13, waiting for transfers between devices: 18.9 us -> 19.4 us  [the longest x6 8.89 us: local(): lax.ppermute(picked[k], 'ctx', across(k))]
  transfers between devices with their start and end apart: 23 -> 15, of which waited for: 8 -> 7; matrix products, arithmetic and copies ran while one was open for 0% -> 0% of each run, Pallas kernels for 16% -> 21%
where the time goes in v2:
time: 67.6 us; the launch traced here: 67.3 us
  starting transfers between devices  23.4 us (35%)
  Pallas kernels  20.8 us (31%)
  waiting for transfers between devices  20.8 us (31%)
  local copies, waits for them, and re-layouts  1.98 us (3%)
    ppermute x6, starting transfers between devices, local(): lax.ppermute(picked[k], 'ctx', across(k))  9.47 us
    ppermute x6, waiting for transfers between devices, local(): lax.ppermute(picked[k], 'ctx', across(k))  8.89 us
    pallas_call x2, Pallas kernels, project_some(): pl.pallas_call(functools.partial(project_kernel, steps), in_specs=[VMEM,...  5.38 us
    pallas_call x1, Pallas kernels, local(): pl.pallas_call(functools.partial(q_kernel, parts), in_specs=[ANY, ANY, VM...  5.25 us
    ppermute x1, starting transfers between devices, local(): hop = [own, lax.ppermute(own, 'ctx', up)]  4.94 us
    ppermute x1, waiting for transfers between devices, local(): hop.append(lax.ppermute(hop[i], 'ctx', up))  4.38 us
    ppermute x2, waiting for transfers between devices, local(): lax.ppermute(x, 'head', flip)  4.01 us
    ppermute x1, starting transfers between devices, local(): hop.append(lax.ppermute(hop[i], 'ctx', up))  3.48 us
  transfers between devices with their start and end apart: 15, of which 7 were waited for; matrix products, arithmetic and copies ran while one was open for 0% of the time, Pallas kernels for 21%

profile of v2, /device:TPU:0, one launch (start us, length us, event | category | flops | bytes accessed | tf_op | source)
XLA Modules:
  0.0 67.3 jit_solution(10994515801202824989)
XLA Ops:
  0.0 0.7 %copy-done.1 = s32[256]{0:T(256)S(1)} copy-done((s32[256]{0:T(256)S(1)}, s32[256]{0:T(256)}, u32[]{:S(2)}) %copy-start.1) | copy-done | bytes 1048
  0.8 2.8 %keys_values.1 = (bf16[272,512]{1,0:T(8,128)(2,1)S(1)}, f32[256,256]{1,0:T(8,128)S(1)}) custom-call(bf16[256,2048]{1,0:T(8,128)(2,1)} %x_hbm.3, bf16[2048,256]{1,0:T(8,128)(2,1)} %wk_hbm.1, bf16[2048,256]{1,0:T(8,128)(2,1)} %wv_hbm.1, s32[1,256]{1,0:T(1,128)S(1)} %bitcast.2), custom_call_target="tpu_custom_call" | custom-call | flops 536870912 | bytes 3145728 | tf_op jit(solution)/shard_map/keys_values/pallas_call | solution.py:358
  3.6 4.9 %collective-permute-start = (bf16[272,512]{1,0:T(8,128)(2,1)S(1)}, bf16[272,512]{1,0:T(8,128)(2,1)S(1)}, u32[]{:S(2)}, u32[]{:S(2)}) collective-permute-start(bf16[272,512]{1,0:T(8,128)(2,1)S(1)} %get-tuple-element.44.refs_0_), channel_id=1, source_target_pairs={{0,4},{4,8},{8,12},{1,5},{5,9},{9,13},{2,6},{6,10},{10,14},{3,7},{... | collective-permute-start | bytes 835592 | tf_op jit(solution)/shard_map/ppermute | solution.py:373
  8.5 1.5 %collective-permute-start.2 = (bf16[272,512]{1,0:T(8,128)(2,1)S(1)}, bf16[272,512]{1,0:T(8,128)(2,1)S(1)}, u32[]{:S(2)}, u32[]{:S(2)}) collective-permute-start(bf16[272,512]{1,0:T(8,128)(2,1)S(1)} %get-tuple-element.44.refs_0_), channel_id=1, source_target_pairs={{0,1},{2,3},{4,5},{6,7},{8,9},{10,11},{12,13},{14,15},{16,17},{18,... | collective-permute-start | bytes 835592 | tf_op jit(solution)/shard_map/ppermute | solution.py:374
  10.0 1.2 %copy-done = bf16[256,2048]{1,0:T(8,128)(2,1)S(1)} copy-done((bf16[256,2048]{1,0:T(8,128)(2,1)S(1)}, bf16[256,2048]{1,0:T(8,128)(2,1)}, u32[]{:S(2)}) %copy-start) | copy-done | bytes 1048600
  11.3 5.3 %queries.1.q_ref = bf16[16,256,128]{2,1,0:T(8,128)(2,1)S(1)} custom-call(bf16[256,2048]{1,0:T(8,128)(2,1)S(1)} %copy-done, bf16[2048,2048]{1,0:T(8,128)(2,1)} %w_hbm.4, f32[256,256]{1,0:T(8,128)S(1)} %get-tuple-element.37.tab_ref), custom_call_target="tpu_custom_call" | custom-call | flops 2147483648 | bytes 9437184 | tf_op jit(solution)/shard_map/queries/pallas_call | solution.py:377
  16.6 3.5 %collective-permute-start.1 = (bf16[272,512]{1,0:T(8,128)(2,1)S(1)}, bf16[272,512]{1,0:T(8,128)(2,1)S(1)}, u32[]{:S(2)}, u32[]{:S(2)}) collective-permute-start(bf16[272,512]{1,0:T(8,128)(2,1)S(1)} %collective-permute-done.refs_1_), channel_id=1, source_target_pairs={{0,4},{4,8},{8,12},{1,5},{5,9},{9,13},{2,6},{6,10},{10,14},{3,7},{... | collective-permute-start | bytes 835592 | tf_op jit(solution)/shard_map/ppermute | solution.py:392
  20.4 1.8 %near_attention.1.near_ref = f32[16,256,256]{2,1,0:T(8,128)S(1)} custom-call(s32[1,256]{1,0:T(1,128)S(1)} %bitcast.3, bf16[16,256,128]{2,1,0:T(8,128)(2,1)S(1)} %queries.1.q_ref, bf16[272,512]{1,0:T(8,128)(2,1)S(1)} %get-tuple-element.44.refs_0_, bf16[272,512]{1,0:T(8,128)(2,1)S(1)} %collective-permute-done.refs_1_, ...), custom_call_target="tpu_custom_call" | custom-call | flops 2147483648 | bytes 8388608 | tf_op jit(solution)/shard_map/near_attention/pallas_call | solution.py:407
  22.2 4.4 %collective-permute-done.1.far_ref = bf16[272,512]{1,0:T(8,128)(2,1)S(1)} collective-permute-done((bf16[272,512]{1,0:T(8,128)(2,1)S(1)}, bf16[272,512]{1,0:T(8,128)(2,1)S(1)}, u32[]{:S(2)}, u32[]{:S(2)}) %collective-permute-start.1) | collective-permute-done | bytes 278560 | tf_op jit(solution)/shard_map/ppermute | solution.py:392
  26.6 1.3 %collective-permute-start.4 = (bf16[272,512]{1,0:T(8,128)(2,1)S(1)}, bf16[272,512]{1,0:T(8,128)(2,1)S(1)}, u32[]{:S(2)}, u32[]{:S(2)}) collective-permute-start(bf16[272,512]{1,0:T(8,128)(2,1)S(1)} %collective-permute-done.1.far_ref), channel_id=1, source_target_pairs={{1,0},{3,2},{5,4},{7,6},{9,8},{11,10},{13,12},{15,14},{17,16},{19,... | collective-permute-start | bytes 835592 | tf_op jit(solution)/shard_map/ppermute | solution.py:419
  27.9 2.2 %collective-permute-done.4.to_zero = bf16[272,512]{1,0:T(8,128)(2,1)S(1)} collective-permute-done((bf16[272,512]{1,0:T(8,128)(2,1)S(1)}, bf16[272,512]{1,0:T(8,128)(2,1)S(1)}, u32[]{:S(2)}, u32[]{:S(2)}) %collective-permute-start.4) | collective-permute-done | bytes 278560 | tf_op jit(solution)/shard_map/ppermute | solution.py:419
  30.1 2.3 %far_attention_project.1 = (bf16[256,2048]{1,0:T(8,128)(2,1)S(1)}, bf16[256,512]{1,0:T(8,128)(2,1)S(1)}) custom-call(s32[1,256]{1,0:T(1,128)S(1)} %bitcast.4, bf16[16,256,128]{2,1,0:T(8,128)(2,1)S(1)} %queries.1.q_ref, bf16[272,512]{1,0:T(8,128)(2,1)S(1)} %collective-permute-done.1.far_ref, bf16[272,512]{1,0:T(8,128)(2,1)S(1)} %collective-permute-done.3.refs_3_.to_one, ...), custom_call_target="tpu_custom_call" | custom-call | flops 1610612736 | bytes 10485760 | tf_op jit(solution)/shard_map/far_attention_project/pallas_call | solution.py:422
  32.4 1.6 %collective-permute-start.5 = (bf16[256,512]{1,0:T(8,128)(2,1)S(1)}, bf16[256,512]{1,0:T(8,128)(2,1)S(1)}, u32[]{:S(2)}, u32[]{:S(2)}) collective-permute-start(bf16[256,512]{1,0:T(8,128)(2,1)S(1)} %get-tuple-element.50), channel_id=1, source_target_pairs={{0,2},{2,0},{1,3},{3,1},{4,6},{6,4},{5,7},{7,5},{8,10},{10,8},{9,1... | collective-permute-start | bytes 786440 | tf_op jit(solution)/shard_map/ppermute | solution.py:449
  34.0 3.1 %project.2 = (bf16[256,512]{1,0:T(8,128)(2,1)S(1)}, bf16[256,512]{1,0:T(8,128)(2,1)S(1)}) custom-call(bf16[256,2048]{1,0:T(8,128)(2,1)S(1)} %get-tuple-element.57.att_ref, bf16[2048,2048]{1,0:T(8,128)(2,1)} %w_hbm.7), custom_call_target="tpu_custom_call" | custom-call | flops 1073741824 | bytes 4194304 | tf_op jit(solution)/shard_map/project/pallas_call | solution.py:435
  37.0 0.6 collective-permute-start.6
  37.6 4.0 %collective-permute-done.5.refs_5_ = bf16[256,512]{1,0:T(8,128)(2,1)S(1)} collective-permute-done((bf16[256,512]{1,0:T(8,128)(2,1)S(1)}, bf16[256,512]{1,0:T(8,128)(2,1)S(1)}, u32[]{:S(2)}, u32[]{:S(2)}) %collective-permute-start.5) | collective-permute-done | bytes 262176 | tf_op jit(solution)/shard_map/ppermute | solution.py:449
  41.6 0.3 add_pick.2
  42.0 2.5 %collective-permute-start.7 = (bf16[112,512]{1,0:T(8,128)(2,1)S(1)}, bf16[112,512]{1,0:T(8,128)(2,1)S(1)}, u32[]{:S(2)}, u32[]{:S(2)}) collective-permute-start(bf16[112,512]{1,0:T(8,128)(2,1)S(1)} %get-tuple-element.52), channel_id=1, source_target_pairs={{0,4},{4,0},{8,12},{12,8},{1,5},{5,1},{9,13},{13,9},{2,6},{6,2},{1... | collective-permute-start | bytes 344072 | tf_op jit(solution)/shard_map/ppermute | solution.py:476
  44.5 1.4 %collective-permute-start.8 = (bf16[112,512]{1,0:T(8,128)(2,1)S(1)}, bf16[112,512]{1,0:T(8,128)(2,1)S(1)}, u32[]{:S(2)}, u32[]{:S(2)}) collective-permute-start(bf16[112,512]{1,0:T(8,128)(2,1)S(1)} %get-tuple-element.53), channel_id=1, source_target_pairs={{0,8},{4,12},{8,0},{12,4},{1,9},{5,13},{9,1},{13,5},{2,10},{6,14},... | collective-permute-start | bytes 344072 | tf_op jit(solution)/shard_map/ppermute | solution.py:476
  45.8 1.1 %collective-permute-start.9 = (bf16[112,512]{1,0:T(8,128)(2,1)S(1)}, bf16[112,512]{1,0:T(8,128)(2,1)S(1)}, u32[]{:S(2)}, u32[]{:S(2)}) collective-permute-start(bf16[112,512]{1,0:T(8,128)(2,1)S(1)} %get-tuple-element.54), channel_id=1, source_target_pairs={{0,12},{4,8},{8,4},{12,0},{1,13},{5,9},{9,5},{13,1},{2,14},{6,10},... | collective-permute-start | bytes 344072 | tf_op jit(solution)/shard_map/ppermute | solution.py:476
  47.0 2.3 %project.3.refs_0_ = bf16[256,512]{1,0:T(8,128)(2,1)S(1)} custom-call(bf16[256,2048]{1,0:T(8,128)(2,1)S(1)} %get-tuple-element.57.att_ref, bf16[2048,2048]{1,0:T(8,128)(2,1)} %w_hbm.7), custom_call_target="tpu_custom_call" | custom-call | flops 536870912 | bytes 2097152 | tf_op jit(solution)/shard_map/project/pallas_call | solution.py:435
  49.6 1.1 %collective-permute-start.10 = (bf16[96,512]{1,0:T(8,128)(2,1)S(1)}, bf16[96,512]{1,0:T(8,128)(2,1)S(1)}, u32[]{:S(2)}, u32[]{:S(2)}) collective-permute-start(bf16[96,512]{1,0:T(8,128)(2,1)S(1)} %get-tuple-element.59), channel_id=1, source_target_pairs={{0,4},{4,0},{8,12},{12,8},{1,5},{5,1},{9,13},{13,9},{2,6},{6,2},{1... | collective-permute-start | bytes 294920 | tf_op jit(solution)/shard_map/ppermute | solution.py:476
  50.7 2.2 %collective-permute-start.11 = (bf16[96,512]{1,0:T(8,128)(2,1)S(1)}, bf16[96,512]{1,0:T(8,128)(2,1)S(1)}, u32[]{:S(2)}, u32[]{:S(2)}) collective-permute-start(bf16[96,512]{1,0:T(8,128)(2,1)S(1)} %get-tuple-element.60), channel_id=1, source_target_pairs={{0,8},{4,12},{8,0},{12,4},{1,9},{5,13},{9,1},{13,5},{2,10},{6,14},... | collective-permute-start | bytes 294920 | tf_op jit(solution)/shard_map/ppermute | solution.py:476
  52.9 1.2 %collective-permute-start.12 = (bf16[96,512]{1,0:T(8,128)(2,1)S(1)}, bf16[96,512]{1,0:T(8,128)(2,1)S(1)}, u32[]{:S(2)}, u32[]{:S(2)}) collective-permute-start(bf16[96,512]{1,0:T(8,128)(2,1)S(1)} %get-tuple-element.61), channel_id=1, source_target_pairs={{0,12},{4,8},{8,4},{12,0},{1,13},{5,9},{9,5},{13,1},{2,14},{6,10},... | collective-permute-start | bytes 294920 | tf_op jit(solution)/shard_map/ppermute | solution.py:476
  54.1 1.9 %collective-permute-done.8.refs_2_.refs_6_ = bf16[112,512]{1,0:T(8,128)(2,1)S(1)} collective-permute-done((bf16[112,512]{1,0:T(8,128)(2,1)S(1)}, bf16[112,512]{1,0:T(8,128)(2,1)S(1)}, u32[]{:S(2)}, u32[]{:S(2)}) %collective-permute-start.8) | collective-permute-done | bytes 114720 | tf_op jit(solution)/shard_map/ppermute | solution.py:476
  56.0 0.7 %place.2 = (bf16[256,512]{1,0:T(8,128)(2,1)S(1)}, bf16[256,512]{1,0:T(8,128)(2,1)S(1)}) custom-call(bf16[112,512]{1,0:T(8,128)(2,1)S(1)} %get-tuple-element.62.refs_0_.refs_4_, bf16[112,512]{1,0:T(8,128)(2,1)S(1)} %collective-permute-done.7.refs_1_.refs_5_, bf16[112,512]{1,0:T(8,128)(2,1)S(1)} %collective-permute-done.8.refs_2_.refs_6_, ...), custom_call_target="tpu_custom_call" | custom-call | flops 201326592 | bytes 917504 | tf_op jit(solution)/shard_map/place/pallas_call | solution.py:481
  56.7 6.9 %collective-permute-done.11.refs_2_ = bf16[96,512]{1,0:T(8,128)(2,1)S(1)} collective-permute-done((bf16[96,512]{1,0:T(8,128)(2,1)S(1)}, bf16[96,512]{1,0:T(8,128)(2,1)S(1)}, u32[]{:S(2)}, u32[]{:S(2)}) %collective-permute-start.11) | collective-permute-done | bytes 98336 | tf_op jit(solution)/shard_map/ppermute | solution.py:476
  63.7 0.7 %place.3 = (bf16[256,512]{1,0:T(8,128)(2,1)S(1)}, bf16[256,512]{1,0:T(8,128)(2,1)S(1)}) custom-call(bf16[96,512]{1,0:T(8,128)(2,1)S(1)} %get-tuple-element.64.refs_0_, bf16[96,512]{1,0:T(8,128)(2,1)S(1)} %collective-permute-done.10.refs_1_, bf16[96,512]{1,0:T(8,128)(2,1)S(1)} %collective-permute-done.11.refs_2_, ...), custom_call_target="tpu_custom_call" | custom-call | flops 201326592 | bytes 917504 | tf_op jit(solution)/shard_map/place/pallas_call | solution.py:481
  64.4 0.5 collective-permute-start.13
  64.9 1.0 %collective-permute-done.14.refs_3_ = bf16[256,512]{1,0:T(8,128)(2,1)S(1)} collective-permute-done((bf16[256,512]{1,0:T(8,128)(2,1)S(1)}, bf16[256,512]{1,0:T(8,128)(2,1)S(1)}, u32[]{:S(2)}, u32[]{:S(2)}) %collective-permute-start.14) | collective-permute-done | bytes 262176 | tf_op jit(solution)/shard_map/ppermute | solution.py:491
  66.0 0.4 collective-permute-done.13.refs_2_
  66.3 0.9 %join.1 = bf16[256,1024]{1,0:T(8,128)(2,1)} custom-call(bf16[256,512]{1,0:T(8,128)(2,1)S(1)} %get-tuple-element.63.refs_0_, bf16[256,512]{1,0:T(8,128)(2,1)S(1)} %get-tuple-element.65.refs_1_, bf16[256,512]{1,0:T(8,128)(2,1)S(1)} %collective-permute-done.13.refs_2_, bf16[256,512]{1,0:T(8,128)(2,1)S(1)} %collective-permute-done.14.refs_3_), custom_call_target="tpu_custom_call" | custom-call | flops 262144 | bytes 1572864 | tf_op jit(solution)/shard_map/join/pallas_call | solution.py:493
  (18 shorter events, 0.8 us)
Async XLA Ops:
  0.0 20.4 %copy-start.2 = (s32[256]{0:T(256)S(1)}, s32[256]{0:T(256)}, u32[]{:S(2)}) copy-start(s32[256]{0:T(256)} %param.8) | copy-start | bytes 3076
  0.0 0.8 %copy-start.1 = (s32[256]{0:T(256)S(1)}, s32[256]{0:T(256)}, u32[]{:S(2)}) copy-start(s32[256]{0:T(256)} %param.8) | copy-start | bytes 3076
  0.8 19.3 %copy-start.3 = (s32[256]{0:T(256)S(1)}, s32[256]{0:T(256)}, u32[]{:S(2)}) copy-start(s32[256]{0:T(256)} %param.9) | copy-start | bytes 3076
  3.6 12.9 %collective-permute-start = (bf16[272,512]{1,0:T(8,128)(2,1)S(1)}, bf16[272,512]{1,0:T(8,128)(2,1)S(1)}, u32[]{:S(2)}, u32[]{:S(2)}) collective-permute-start(bf16[272,512]{1,0:T(8,128)(2,1)S(1)} %get-tuple-element.44.refs_0_), channel_id=1, source_target_pairs={{0,4},{4,8},{8,12},{1,5},{5,9},{9,13},{2,6},{6,10},{10,14},{3,7},{... | collective-permute-start | bytes 835592 | tf_op jit(solution)/shard_map/ppermute | solution.py:373
  8.5 11.9 %collective-permute-start.2 = (bf16[272,512]{1,0:T(8,128)(2,1)S(1)}, bf16[272,512]{1,0:T(8,128)(2,1)S(1)}, u32[]{:S(2)}, u32[]{:S(2)}) collective-permute-start(bf16[272,512]{1,0:T(8,128)(2,1)S(1)} %get-tuple-element.44.refs_0_), channel_id=1, source_target_pairs={{0,1},{2,3},{4,5},{6,7},{8,9},{10,11},{12,13},{14,15},{16,17},{18,... | collective-permute-start | bytes 835592 | tf_op jit(solution)/shard_map/ppermute | solution.py:374
  10.0 1.2 %copy-start = (bf16[256,2048]{1,0:T(8,128)(2,1)S(1)}, bf16[256,2048]{1,0:T(8,128)(2,1)}, u32[]{:S(2)}) copy-start(bf16[256,2048]{1,0:T(8,128)(2,1)} %x_hbm.3) | copy-start | bytes 3145732
  16.5 3.9 %collective-permute-start.3 = (bf16[272,512]{1,0:T(8,128)(2,1)S(1)}, bf16[272,512]{1,0:T(8,128)(2,1)S(1)}, u32[]{:S(2)}, u32[]{:S(2)}) collective-permute-start(bf16[272,512]{1,0:T(8,128)(2,1)S(1)} %collective-permute-done.refs_1_), channel_id=1, source_target_pairs={{0,1},{1,0},{2,3},{3,2},{4,5},{5,4},{6,7},{7,6},{8,9},{9,8},{10,11... | collective-permute-start | bytes 835592 | tf_op jit(solution)/shard_map/ppermute | solution.py:393
  16.6 10.0 %collective-permute-start.1 = (bf16[272,512]{1,0:T(8,128)(2,1)S(1)}, bf16[272,512]{1,0:T(8,128)(2,1)S(1)}, u32[]{:S(2)}, u32[]{:S(2)}) collective-permute-start(bf16[272,512]{1,0:T(8,128)(2,1)S(1)} %collective-permute-done.refs_1_), channel_id=1, source_target_pairs={{0,4},{4,8},{8,12},{1,5},{5,9},{9,13},{2,6},{6,10},{10,14},{3,7},{... | collective-permute-start | bytes 835592 | tf_op jit(solution)/shard_map/ppermute | solution.py:392
  26.6 3.4 %collective-permute-start.4 = (bf16[272,512]{1,0:T(8,128)(2,1)S(1)}, bf16[272,512]{1,0:T(8,128)(2,1)S(1)}, u32[]{:S(2)}, u32[]{:S(2)}) collective-permute-start(bf16[272,512]{1,0:T(8,128)(2,1)S(1)} %collective-permute-done.1.far_ref), channel_id=1, source_target_pairs={{1,0},{3,2},{5,4},{7,6},{9,8},{11,10},{13,12},{15,14},{17,16},{19,... | collective-permute-start | bytes 835592 | tf_op jit(solution)/shard_map/ppermute | solution.py:419
  32.4 9.2 %collective-permute-start.5 = (bf16[256,512]{1,0:T(8,128)(2,1)S(1)}, bf16[256,512]{1,0:T(8,128)(2,1)S(1)}, u32[]{:S(2)}, u32[]{:S(2)}) collective-permute-start(bf16[256,512]{1,0:T(8,128)(2,1)S(1)} %get-tuple-element.50), channel_id=1, source_target_pairs={{0,2},{2,0},{1,3},{3,1},{4,6},{6,4},{5,7},{7,5},{8,10},{10,8},{9,1... | collective-permute-start | bytes 786440 | tf_op jit(solution)/shard_map/ppermute | solution.py:449
  37.0 12.3 %collective-permute-start.6 = (bf16[256,512]{1,0:T(8,128)(2,1)S(1)}, bf16[256,512]{1,0:T(8,128)(2,1)S(1)}, u32[]{:S(2)}, u32[]{:S(2)}) collective-permute-start(bf16[256,512]{1,0:T(8,128)(2,1)S(1)} %get-tuple-element.56), channel_id=1, source_target_pairs={{0,2},{2,0},{1,3},{3,1},{4,6},{6,4},{5,7},{7,5},{8,10},{10,8},{9,1... | collective-permute-start | bytes 786440 | tf_op jit(solution)/shard_map/ppermute | solution.py:449
  42.0 11.0 %collective-permute-start.7 = (bf16[112,512]{1,0:T(8,128)(2,1)S(1)}, bf16[112,512]{1,0:T(8,128)(2,1)S(1)}, u32[]{:S(2)}, u32[]{:S(2)}) collective-permute-start(bf16[112,512]{1,0:T(8,128)(2,1)S(1)} %get-tuple-element.52), channel_id=1, source_target_pairs={{0,4},{4,0},{8,12},{12,8},{1,5},{5,1},{9,13},{13,9},{2,6},{6,2},{1... | collective-permute-start | bytes 344072 | tf_op jit(solution)/shard_map/ppermute | solution.py:476
  44.5 11.6 %collective-permute-start.8 = (bf16[112,512]{1,0:T(8,128)(2,1)S(1)}, bf16[112,512]{1,0:T(8,128)(2,1)S(1)}, u32[]{:S(2)}, u32[]{:S(2)}) collective-permute-start(bf16[112,512]{1,0:T(8,128)(2,1)S(1)} %get-tuple-element.53), channel_id=1, source_target_pairs={{0,8},{4,12},{8,0},{12,4},{1,9},{5,13},{9,1},{13,5},{2,10},{6,14},... | collective-permute-start | bytes 344072 | tf_op jit(solution)/shard_map/ppermute | solution.py:476
  45.8 10.2 %collective-permute-start.9 = (bf16[112,512]{1,0:T(8,128)(2,1)S(1)}, bf16[112,512]{1,0:T(8,128)(2,1)S(1)}, u32[]{:S(2)}, u32[]{:S(2)}) collective-permute-start(bf16[112,512]{1,0:T(8,128)(2,1)S(1)} %get-tuple-element.54), channel_id=1, source_target_pairs={{0,12},{4,8},{8,4},{12,0},{1,13},{5,9},{9,5},{13,1},{2,14},{6,10},... | collective-permute-start | bytes 344072 | tf_op jit(solution)/shard_map/ppermute | solution.py:476
  49.6 7.1 %collective-permute-start.10 = (bf16[96,512]{1,0:T(8,128)(2,1)S(1)}, bf16[96,512]{1,0:T(8,128)(2,1)S(1)}, u32[]{:S(2)}, u32[]{:S(2)}) collective-permute-start(bf16[96,512]{1,0:T(8,128)(2,1)S(1)} %get-tuple-element.59), channel_id=1, source_target_pairs={{0,4},{4,0},{8,12},{12,8},{1,5},{5,1},{9,13},{13,9},{2,6},{6,2},{1... | collective-permute-start | bytes 294920 | tf_op jit(solution)/shard_map/ppermute | solution.py:476
  50.7 13.0 %collective-permute-start.11 = (bf16[96,512]{1,0:T(8,128)(2,1)S(1)}, bf16[96,512]{1,0:T(8,128)(2,1)S(1)}, u32[]{:S(2)}, u32[]{:S(2)}) collective-permute-start(bf16[96,512]{1,0:T(8,128)(2,1)S(1)} %get-tuple-element.60), channel_id=1, source_target_pairs={{0,8},{4,12},{8,0},{12,4},{1,9},{5,13},{9,1},{13,5},{2,10},{6,14},... | collective-permute-start | bytes 294920 | tf_op jit(solution)/shard_map/ppermute | solution.py:476
  52.9 10.7 %collective-permute-start.12 = (bf16[96,512]{1,0:T(8,128)(2,1)S(1)}, bf16[96,512]{1,0:T(8,128)(2,1)S(1)}, u32[]{:S(2)}, u32[]{:S(2)}) collective-permute-start(bf16[96,512]{1,0:T(8,128)(2,1)S(1)} %get-tuple-element.61), channel_id=1, source_target_pairs={{0,12},{4,8},{8,4},{12,0},{1,13},{5,9},{9,5},{13,1},{2,14},{6,10},... | collective-permute-start | bytes 294920 | tf_op jit(solution)/shard_map/ppermute | solution.py:476
  64.4 1.6 %collective-permute-start.14 = (bf16[256,512]{1,0:T(8,128)(2,1)S(1)}, bf16[256,512]{1,0:T(8,128)(2,1)S(1)}, u32[]{:S(2)}, u32[]{:S(2)}) collective-permute-start(bf16[256,512]{1,0:T(8,128)(2,1)S(1)} %get-tuple-element.67), channel_id=1, source_target_pairs={{0,1},{1,0},{2,3},{3,2},{4,5},{5,4},{6,7},{7,6},{8,9},{9,8},{10,11... | collective-permute-start | bytes 786440 | tf_op jit(solution)/shard_map/ppermute | solution.py:491
  64.4 1.9 %collective-permute-start.13 = (bf16[256,512]{1,0:T(8,128)(2,1)S(1)}, bf16[256,512]{1,0:T(8,128)(2,1)S(1)}, u32[]{:S(2)}, u32[]{:S(2)}) collective-permute-start(bf16[256,512]{1,0:T(8,128)(2,1)S(1)} %get-tuple-element.66), channel_id=1, source_target_pairs={{0,1},{1,0},{2,3},{3,2},{4,5},{5,4},{6,7},{7,6},{8,9},{9,8},{10,11... | collective-permute-start | bytes 786440 | tf_op jit(solution)/shard_map/ppermute | solution.py:491

commit v3 on v2

--- a/solution.py
+++ b/solution.py
@@ -18,7 +18,7 @@
 ANY = pl.BlockSpec(memory_space=pl.ANY)
 MIB = 1 << 20
 KV_MIB = 53
-Q_MIB = 51
+Q_MIB = 52
 FAR_MIB = 44
 PROJECT_MIB = 48
 
@@ -286,37 +286,48 @@
     finish()
 
 
-def pick_kernel(n_head, ctx, with_slots, span, mark, pos_ref, *refs):
-    slots = refs[:ctx] if with_slots else ()
-    refs = refs[len(slots):]
-    shares, outs = refs[:n_head], refs[n_head:]
-    rows = shares[0].shape[0]
+def add_shares(shares):
     total = shares[0][...].astype(F32)
     for share in shares[1:]:
         total = total + share[...].astype(F32)
-    total = total.astype(BF16)
-    every = span * ctx
-    pick = jnp.where(lax.broadcasted_iota(jnp.int32, (every, rows), 0) == pos_ref[0:1, :], 1.0, 0.0).astype(BF16)
-    moved = jnp.dot(pick, total, preferred_element_type=F32).astype(BF16)
+    return total.astype(BF16)
+
+
+def take(pos, count, total):
+    hit = lax.broadcasted_iota(jnp.int32, (count, total.shape[0]), 0) == pos
+    return jnp.dot(jnp.where(hit, 1.0, 0.0).astype(BF16), total, preferred_element_type=F32).astype(BF16)
+
+
+def pick_kernel(ctx, n_slots, span, mark, pos_ref, *refs):
+    slots, shares, outs = refs[:n_slots], refs[n_slots:-ctx], refs[-ctx:]
+    moved = take(pos_ref[0:1, :], span * ctx, add_shares(shares))
     for k, out in enumerate(outs):
         out[0:span, :] = moved[k * span:(k + 1) * span]
-        if with_slots:
+        if n_slots:
             out[mark:, :] = jnp.zeros((16, out.shape[1]), BF16)
             lanes = slots[k].shape[1]
             out[mark:, 0:lanes] = jnp.concatenate([slots[k][...]] * 2, 0).astype(BF16)
+
+
+def slot_line(ref, at, span):
+    return ref[at:at + 16, 0:span].astype(F32)[0:1].astype(jnp.int32)
+
+
+def put(slot, block, count):
+    hit = lax.broadcasted_iota(jnp.int32, (count, slot.shape[1]), 0) == slot
+    return jnp.dot(jnp.where(hit, 1.0, 0.0).astype(BF16), block, preferred_element_type=F32)
 
 
 def place_kernel(ctx, cap, rows, mark, *refs):
     blocks, marked, (mine_ref, pair_ref) = refs[:ctx], refs[ctx:2 * ctx], refs[2 * ctx:]
     span = 2 * cap
     total = None
+    lane = lax.broadcasted_iota(jnp.int32, (1, span), 1)
     for block, marks in zip(blocks, marked, strict=True):
-        slot = marks[mark:mark + 16, 0:span].astype(F32)[0:1].astype(jnp.int32)
-        lane = lax.broadcasted_iota(jnp.int32, (1, span), 1)
+        slot = slot_line(marks, mark, span)
         slot = jnp.where((slot >= 0) & (lane >= cap), slot + rows, slot)
-        at = lax.broadcasted_iota(jnp.int32, (2 * rows, span), 0) == slot
-        put = jnp.dot(jnp.where(at, 1.0, 0.0).astype(BF16), block[0:span, :], preferred_element_type=F32)
-        total = put if total is None else total + put
+        some = put(slot, block[0:span, :], 2 * rows)
+        total = some if total is None else total + some
     mine_ref[...] = total[:rows].astype(BF16)
     pair_ref[...] = total[rows:].astype(BF16)
 
@@ -347,9 +358,10 @@
     lanes = -(-span // 128) * 128
     every = ctx * span
     sds = jax.ShapeDtypeStruct
-    chunks = (half // 2, half - half // 2)
-
-    up = [(i, i + 1) for i in range(ctx - 1)]
+    units = half // 128
+    chunks = [n * 128 for n in (units * 3 // 8, units - units * 3 // 8)]
+
+    up = [(i, (i + 1) % ctx) for i in range(ctx)]
     swap = [(0, 1), (1, 0)]
     seg_row = doc_ids.reshape(1, rows)
 
@@ -371,7 +383,6 @@
     )(tokens, w_key, w_value, seg_row)
 
     hop = [own, lax.ppermute(own, "ctx", up)]
-    pair = [lax.ppermute(own, "rep", [(0, 1)])]
 
     parts = 4
     queries = pl.pallas_call(
@@ -385,13 +396,6 @@
         name="queries",
     )(tokens, w_query, table)
 
-    for i in range(1, hops + 1):
-        if i == 1:
-            hop[1] = after(hop[1], queries)
-        if i < hops:
-            hop.append(lax.ppermute(hop[i], "ctx", up))
-            pair.append(lax.ppermute(hop[i], "rep", swap))
-
     route = pl.pallas_call(
         functools.partial(route_kernel, ctx, cap),
         in_specs=[VMEM],
@@ -401,7 +405,12 @@
         cost_estimate=cost(4 * rows * rows, 8 * rows * 4),
         name="routes",
     )
-    buffer_pos, *slots = route(after(dest_rows.reshape(1, rows), queries))
+    pair = [lax.ppermute(after(own, queries), "rep", swap)]
+    hop[1] = after(hop[1], queries)
+    buffer_pos, *slots = route(after(dest_rows.reshape(1, rows), hop[1]))
+    for i in range(1, hops):
+        hop.append(lax.ppermute(hop[i], "ctx", up))
+        pair.append(lax.ppermute(after(hop[i], buffer_pos), "rep", swap))
 
     work = heads * rows * rows
     near = pl.pallas_call(
@@ -416,7 +425,7 @@
     )(after(seg_row, buffer_pos), queries, *hop[:hops], *pair[:hops])
 
     hop[hops] = after(hop[hops], near)
-    pair.append(lax.ppermute(hop[hops], "rep", [(1, 0)]))
+    pair.append(lax.ppermute(hop[hops], "rep", swap))
 
     widths = chunks[:1] * others
     attended, *sent = pl.pallas_call(
@@ -444,40 +453,46 @@
         )(x, w_out)
 
     flips = [[(i, i ^ (d + 1)) for i in range(n_head)] for d in range(others)]
-    ours, theirs, at = [], [], 0
-    for j, n in enumerate(chunks):
-        theirs.append([lax.ppermute(x, "head", flip) for x, flip in zip(sent, flips, strict=True)])
-        steps, sizes = [(0, at)], [n]
-        at += n
-        if j + 1 < len(chunks):
-            steps += [(d + 1, at) for d in range(others)]
-            sizes += [chunks[j + 1]] * others
-        mine, *sent = project_some(after(attended, *ours[-1:], *sent), steps, sizes)
-        ours.append(mine)
-
-    def across(k):
-        return [(i, i ^ k) for i in range(ctx)]
+
+    def to_heads(xs):
+        return [lax.ppermute(x, "head", flip) for x, flip in zip(xs, flips, strict=True)]
+
+    theirs = [to_heads(sent)]
+    starts = [sum(chunks[:j]) for j in range(len(chunks))]
+    later = range(1, len(chunks))
+    steps, sizes = [(0, 0)], chunks[:1]
+    for j in later:
+        steps += [(d + 1, starts[j]) for d in range(others)]
+        sizes = sizes + chunks[j:j + 1] * others
+    mine, *sent = project_some(attended, steps, sizes)
+    for j in later:
+        theirs.append(to_heads(sent[(j - 1) * others:j * others]))
+
+    def across(xs):
+        return [xs[0]] + [lax.ppermute(xs[k], "ctx", [(i, i ^ k) for i in range(ctx)]) for k in range(1, ctx)]
 
     mark = -(-span // 16) * 16
-    moved, got = [], []
+    moved, got, shares = [], [], [[mine, *theirs[0]]]
     for j, n in enumerate(chunks):
         extra = slots if j == 0 else []
         tall = mark + 16 if j == 0 else span
+        if j == 1:
+            ours = project_some(after(attended, *moved), [(0, starts[i]) for i in later], chunks[1:])
+            shares += [[x, *theirs[i + 1]] for i, x in enumerate(ours)]
         picked = pl.pallas_call(
-            functools.partial(pick_kernel, n_head, ctx, j == 0, span, mark),
+            functools.partial(pick_kernel, ctx, len(extra), span, mark),
             in_specs=[VMEM] * (1 + len(extra) + n_head),
             out_specs=[VMEM] * ctx,
             out_shape=[sds((tall, n), BF16)] * ctx,
             compiler_params=params(8),
             cost_estimate=cost(2 * every * rows * n, 2 * n * (2 * rows + every)),
             name="add_pick",
-        )(after(buffer_pos, *moved), *extra, ours[j], *theirs[j])
+        )(after(buffer_pos, *sent, *moved), *extra, *shares[j])
         moved += picked
-        got.append([picked[0]] + [lax.ppermute(picked[k], "ctx", across(k)) for k in range(1, ctx)])
+        got.append(across(picked))
 
     kept, gone = [], []
     for j, n in enumerate(chunks):
-        first = after(got[j][0], *moved, *kept)
         stay, leave = pl.pallas_call(
             functools.partial(place_kernel, ctx, cap, rows, mark),
             in_specs=[VMEM] * (2 * ctx),
@@ -486,7 +501,7 @@
             compiler_params=params(8),
             cost_estimate=cost(4 * every * rows * n, 2 * n * (2 * rows + every)),
             name="place",
-        )(first, *got[j][1:], *got[0])
+        )(after(got[j][0], *moved, *kept), *got[j][1:], *got[0])
         kept.append(stay)
         gone.append(lax.ppermute(leave, "rep", swap))
 

time: 67.6 us -> 76.8 us (1.14)
  waiting for transfers between devices: 20.8 us -> 40.2 us
  starting transfers between devices: 23.4 us -> 13.9 us
  local copies, waits for them, and re-layouts: 1.98 us -> 0.76 us
  Pallas kernels: 20.8 us -> 21.6 us
    ppermute x11, waiting for transfers between devices: 15.1 us -> 28.3 us  [the longest x6 13.3 us: across(): lax.ppermute(xs[k], 'ctx', [(i, i ^ k) for i in range(ctx)])]
    ppermute x11, starting transfers between devices: 14.4 us -> 10.2 us  [the longest x6 7.98 us: across(): lax.ppermute(xs[k], 'ctx', [(i, i ^ k) for i in range(ctx)])]
    ppermute x1, starting transfers between devices: 3.48 us -> 0.06 us  [local(): hop.append(lax.ppermute(hop[i], 'ctx', up))]
    ppermute x1, waiting for transfers between devices: 4.38 us -> 7.49 us  [local(): hop.append(lax.ppermute(hop[i], 'ctx', up))]
    ppermute x1, waiting for transfers between devices: 0.01 us -> 3.09 us  [local(): hop = [own, lax.ppermute(own, 'ctx', up)]]
    ppermute x1, starting transfers between devices: 4.94 us -> 3.07 us  [local(): hop = [own, lax.ppermute(own, 'ctx', up)]]
    unnamed x8 -> x6, local copies, waits for them, and re-layouts: 1.98 us -> 0.76 us
  transfers between devices with their start and end apart: 15 -> 15, of which waited for: 7 -> 7; matrix products, arithmetic and copies ran while one was open for 0% -> 0% of each run, Pallas kernels for 21% -> 15%
where the time goes in v3:
time: 76.8 us; the launch traced here: 76.7 us
  waiting for transfers between devices  40.2 us (52%)
  Pallas kernels  21.6 us (28%)
  starting transfers between devices  13.9 us (18%)
    ppermute x6, waiting for transfers between devices, across(): lax.ppermute(xs[k], 'ctx', [(i, i ^ k) for i in range(ctx)])  13.3 us
    ppermute x2, waiting for transfers between devices, to_heads(): lax.ppermute(x, 'head', flip)  11.9 us
    ppermute x6, starting transfers between devices, across(): lax.ppermute(xs[k], 'ctx', [(i, i ^ k) for i in range(ctx)])  7.98 us
    ppermute x1, waiting for transfers between devices, local(): hop.append(lax.ppermute(hop[i], 'ctx', up))  7.49 us
    pallas_call x2, Pallas kernels, project_some(): pl.pallas_call(functools.partial(project_kernel, steps), in_specs=[VMEM,...  6.04 us
    pallas_call x1, Pallas kernels, local(): pl.pallas_call(functools.partial(q_kernel, parts), in_specs=[ANY, ANY, VM...  5.51 us
    ppermute x1, waiting for transfers between devices, local(): hop = [own, lax.ppermute(own, 'ctx', up)]  3.09 us
    ppermute x1, starting transfers between devices, local(): hop = [own, lax.ppermute(own, 'ctx', up)]  3.07 us
  transfers between devices with their start and end apart: 15, of which 7 were waited for; matrix products, arithmetic and copies ran while one was open for 0% of the time, Pallas kernels for 15%

profile of v3, /device:TPU:0, one launch (start us, length us, event | category | flops | bytes accessed | tf_op | source)
XLA Modules:
  0.0 76.7 jit_solution(9356012555985895803)
XLA Ops:
  0.0 0.7 copy-done
  0.8 2.8 %keys_values.1 = (bf16[272,512]{1,0:T(8,128)(2,1)S(1)}, f32[256,256]{1,0:T(8,128)S(1)}) custom-call(bf16[256,2048]{1,0:T(8,128)(2,1)} %x_hbm.3, bf16[2048,256]{1,0:T(8,128)(2,1)} %wk_hbm.1, bf16[2048,256]{1,0:T(8,128)(2,1)} %wv_hbm.1, s32[1,256]{1,0:T(1,128)S(1)} %bitcast.2), custom_call_target="tpu_custom_call" | custom-call | flops 536870912 | bytes 3145728 | tf_op jit(solution)/shard_map/keys_values/pallas_call | solution.py:370
  3.6 3.1 %collective-permute-start = (bf16[272,512]{1,0:T(8,128)(2,1)S(1)}, bf16[272,512]{1,0:T(8,128)(2,1)S(1)}, u32[]{:S(2)}, u32[]{:S(2)}) collective-permute-start(bf16[272,512]{1,0:T(8,128)(2,1)S(1)} %get-tuple-element.45.refs_0_), channel_id=1, source_target_pairs={{0,4},{4,8},{8,12},{12,0},{1,5},{5,9},{9,13},{13,1},{2,6},{6,10},{... | collective-permute-start | bytes 835592 | tf_op jit(solution)/shard_map/ppermute | solution.py:385
  6.7 5.5 %queries.1.q_ref = bf16[16,256,128]{2,1,0:T(8,128)(2,1)S(1)} custom-call(bf16[256,2048]{1,0:T(8,128)(2,1)} %x_hbm.3, bf16[2048,2048]{1,0:T(8,128)(2,1)} %w_hbm.4, f32[256,256]{1,0:T(8,128)S(1)} %get-tuple-element.40.tab_ref), custom_call_target="tpu_custom_call" | custom-call | flops 2147483648 | bytes 9437184 | tf_op jit(solution)/shard_map/queries/pallas_call | solution.py:388
  12.2 0.1 collective-permute-start.2
  12.3 3.1 %collective-permute-done.refs_1_ = bf16[272,512]{1,0:T(8,128)(2,1)S(1)} collective-permute-done((bf16[272,512]{1,0:T(8,128)(2,1)S(1)}, bf16[272,512]{1,0:T(8,128)(2,1)S(1)}, u32[]{:S(2)}, u32[]{:S(2)}) %collective-permute-start) | collective-permute-done | bytes 278560 | tf_op jit(solution)/shard_map/ppermute | solution.py:385
  15.4 0.3 routes.1
  15.6 0.1 collective-permute-start.3
  15.8 1.5 %collective-permute-done.3.refs_3_.to_one = bf16[272,512]{1,0:T(8,128)(2,1)S(1)} collective-permute-done((bf16[272,512]{1,0:T(8,128)(2,1)S(1)}, bf16[272,512]{1,0:T(8,128)(2,1)S(1)}, u32[]{:S(2)}, u32[]{:S(2)}) %collective-permute-start.3) | collective-permute-done | bytes 278560 | tf_op jit(solution)/shard_map/ppermute | solution.py:413
  17.3 1.8 %near_attention.1.near_ref = f32[16,256,256]{2,1,0:T(8,128)S(1)} custom-call(s32[1,256]{1,0:T(1,128)S(1)} %bitcast.3, bf16[16,256,128]{2,1,0:T(8,128)(2,1)S(1)} %queries.1.q_ref, bf16[272,512]{1,0:T(8,128)(2,1)S(1)} %get-tuple-element.45.refs_0_, bf16[272,512]{1,0:T(8,128)(2,1)S(1)} %collective-permute-done.refs_1_, ...), custom_call_target="tpu_custom_call" | custom-call | flops 2147483648 | bytes 8388608 | tf_op jit(solution)/shard_map/near_attention/pallas_call | solution.py:416
  19.1 7.5 %collective-permute-done.1.far_ref = bf16[272,512]{1,0:T(8,128)(2,1)S(1)} collective-permute-done((bf16[272,512]{1,0:T(8,128)(2,1)S(1)}, bf16[272,512]{1,0:T(8,128)(2,1)S(1)}, u32[]{:S(2)}, u32[]{:S(2)}) %collective-permute-start.1) | collective-permute-done | bytes 278560 | tf_op jit(solution)/shard_map/ppermute | solution.py:412
  26.6 1.6 %collective-permute-done.4.to_zero = bf16[272,512]{1,0:T(8,128)(2,1)S(1)} collective-permute-done((bf16[272,512]{1,0:T(8,128)(2,1)S(1)}, bf16[272,512]{1,0:T(8,128)(2,1)S(1)}, u32[]{:S(2)}, u32[]{:S(2)}) %collective-permute-start.4) | collective-permute-done | bytes 278560 | tf_op jit(solution)/shard_map/ppermute | solution.py:428
  28.1 2.2 %far_attention_project.1 = (bf16[256,2048]{1,0:T(8,128)(2,1)S(1)}, bf16[256,384]{1,0:T(8,128)(2,1)S(1)}) custom-call(s32[1,256]{1,0:T(1,128)S(1)} %bitcast.4, bf16[16,256,128]{2,1,0:T(8,128)(2,1)S(1)} %queries.1.q_ref, bf16[272,512]{1,0:T(8,128)(2,1)S(1)} %collective-permute-done.1.far_ref, bf16[272,512]{1,0:T(8,128)(2,1)S(1)} %collective-permute-done.3.refs_3_.to_one, ...), custom_call_target="tpu_custom_call" | custom-call | flops 1476395008 | bytes 10485760 | tf_op jit(solution)/shard_map/far_attention_project/pallas_call | solution.py:431
  30.3 3.3 %project.2 = (bf16[256,384]{1,0:T(8,128)(2,1)S(1)}, bf16[256,640]{1,0:T(8,128)(2,1)S(1)}) custom-call(bf16[256,2048]{1,0:T(8,128)(2,1)S(1)} %get-tuple-element.62.att_ref, bf16[2048,2048]{1,0:T(8,128)(2,1)} %w_hbm.7), custom_call_target="tpu_custom_call" | custom-call | flops 1073741824 | bytes 4194304 | tf_op jit(solution)/shard_map/project/pallas_call | solution.py:444
  33.6 1.6 %collective-permute-start.6 = (bf16[256,640]{1,0:T(8,128)(2,1)S(1)}, bf16[256,640]{1,0:T(8,128)(2,1)S(1)}, u32[]{:S(2)}, u32[]{:S(2)}) collective-permute-start(bf16[256,640]{1,0:T(8,128)(2,1)S(1)} %get-tuple-element.49), channel_id=1, source_target_pairs={{0,2},{2,0},{1,3},{3,1},{4,6},{6,4},{5,7},{7,5},{8,10},{10,8},{9,1... | collective-permute-start | bytes 983048 | tf_op jit(solution)/shard_map/ppermute | solution.py:458
  35.2 0.5 collective-permute-start.5
  35.7 11.9 %collective-permute-done.5.refs_5_ = bf16[256,384]{1,0:T(8,128)(2,1)S(1)} collective-permute-done((bf16[256,384]{1,0:T(8,128)(2,1)S(1)}, bf16[256,384]{1,0:T(8,128)(2,1)S(1)}, u32[]{:S(2)}, u32[]{:S(2)}) %collective-permute-start.5) | collective-permute-done | bytes 196640 | tf_op jit(solution)/shard_map/ppermute | solution.py:458
  47.6 0.3 add_pick.2
  47.9 0.1 collective-permute-start.7
  48.0 2.8 %project.3.refs_0_ = bf16[256,640]{1,0:T(8,128)(2,1)S(1)} custom-call(bf16[256,2048]{1,0:T(8,128)(2,1)S(1)} %get-tuple-element.62.att_ref, bf16[2048,2048]{1,0:T(8,128)(2,1)} %w_hbm.7), custom_call_target="tpu_custom_call" | custom-call | flops 671088640 | bytes 2621440 | tf_op jit(solution)/shard_map/project/pallas_call | solution.py:444
  50.8 0.3 add_pick.3
  51.1 2.1 %collective-permute-start.10 = (bf16[96,640]{1,0:T(8,128)(2,1)S(1)}, bf16[96,640]{1,0:T(8,128)(2,1)S(1)}, u32[]{:S(2)}, u32[]{:S(2)}) collective-permute-start(bf16[96,640]{1,0:T(8,128)(2,1)S(1)} %get-tuple-element.64), channel_id=1, source_target_pairs={{0,4},{4,0},{8,12},{12,8},{1,5},{5,1},{9,13},{13,9},{2,6},{6,2},{1... | collective-permute-start | bytes 368648 | tf_op jit(solution)/shard_map/ppermute | solution.py:472
  53.2 2.4 %collective-permute-start.12 = (bf16[96,640]{1,0:T(8,128)(2,1)S(1)}, bf16[96,640]{1,0:T(8,128)(2,1)S(1)}, u32[]{:S(2)}, u32[]{:S(2)}) collective-permute-start(bf16[96,640]{1,0:T(8,128)(2,1)S(1)} %get-tuple-element.66), channel_id=1, source_target_pairs={{0,12},{4,8},{8,4},{12,0},{1,13},{5,9},{9,5},{13,1},{2,14},{6,10},... | collective-permute-start | bytes 368648 | tf_op jit(solution)/shard_map/ppermute | solution.py:472
  55.6 0.5 collective-permute-start.8
  56.1 2.9 %collective-permute-start.9 = (bf16[112,384]{1,0:T(8,128)(2,1)S(1)}, bf16[112,384]{1,0:T(8,128)(2,1)S(1)}, u32[]{:S(2)}, u32[]{:S(2)}) collective-permute-start(bf16[112,384]{1,0:T(8,128)(2,1)S(1)} %get-tuple-element.60), channel_id=1, source_target_pairs={{0,12},{4,8},{8,4},{12,0},{1,13},{5,9},{9,5},{13,1},{2,14},{6,10},... | collective-permute-start | bytes 258056 | tf_op jit(solution)/shard_map/ppermute | solution.py:472
  59.1 13.3 %collective-permute-done.8.refs_2_.refs_6_ = bf16[112,384]{1,0:T(8,128)(2,1)S(1)} collective-permute-done((bf16[112,384]{1,0:T(8,128)(2,1)S(1)}, bf16[112,384]{1,0:T(8,128)(2,1)S(1)}, u32[]{:S(2)}, u32[]{:S(2)}) %collective-permute-start.8) | collective-permute-done | bytes 86048 | tf_op jit(solution)/shard_map/ppermute | solution.py:472
  72.3 0.6 place.2
  72.9 0.8 %place.3 = (bf16[256,640]{1,0:T(8,128)(2,1)S(1)}, bf16[256,640]{1,0:T(8,128)(2,1)S(1)}) custom-call(bf16[96,640]{1,0:T(8,128)(2,1)S(1)} %get-tuple-element.69.refs_0_, bf16[96,640]{1,0:T(8,128)(2,1)S(1)} %collective-permute-done.10.refs_1_, bf16[96,640]{1,0:T(8,128)(2,1)S(1)} %collective-permute-done.11.refs_2_, ...), custom_call_target="tpu_custom_call" | custom-call | flops 251658240 | bytes 1146880 | tf_op jit(solution)/shard_map/place/pallas_call | solution.py:496
  73.8 0.1 collective-permute-start.14
  73.8 0.5 collective-permute-start.13
  74.3 1.4 %collective-permute-done.13.refs_2_ = bf16[256,384]{1,0:T(8,128)(2,1)S(1)} collective-permute-done((bf16[256,384]{1,0:T(8,128)(2,1)S(1)}, bf16[256,384]{1,0:T(8,128)(2,1)S(1)}, u32[]{:S(2)}, u32[]{:S(2)}) %collective-permute-start.13) | collective-permute-done | bytes 196640 | tf_op jit(solution)/shard_map/ppermute | solution.py:506
  75.7 0.9 %join.1 = bf16[256,1024]{1,0:T(8,128)(2,1)} custom-call(bf16[256,384]{1,0:T(8,128)(2,1)S(1)} %get-tuple-element.68.refs_0_, bf16[256,640]{1,0:T(8,128)(2,1)S(1)} %get-tuple-element.70.refs_1_, bf16[256,384]{1,0:T(8,128)(2,1)S(1)} %collective-permute-done.13.refs_2_, bf16[256,640]{1,0:T(8,128)(2,1)S(1)} %collective-permute-done.14.refs_3_), custom_call_target="tpu_custom_call" | custom-call | flops 262144 | bytes 1572864 | tf_op jit(solution)/shard_map/join/pallas_call | solution.py:508
  (16 shorter events, 0.1 us)
Async XLA Ops:
  0.0 17.3 %copy-start.1 = (s32[256]{0:T(256)S(1)}, s32[256]{0:T(256)}, u32[]{:S(2)}) copy-start(s32[256]{0:T(256)} %param.8) | copy-start | bytes 3076
  0.0 0.8 copy-start
  0.8 14.6 %copy-start.2 = (s32[256]{0:T(256)S(1)}, s32[256]{0:T(256)}, u32[]{:S(2)}) copy-start(s32[256]{0:T(256)} %param.9) | copy-start | bytes 3076
  3.6 11.7 %collective-permute-start = (bf16[272,512]{1,0:T(8,128)(2,1)S(1)}, bf16[272,512]{1,0:T(8,128)(2,1)S(1)}, u32[]{:S(2)}, u32[]{:S(2)}) collective-permute-start(bf16[272,512]{1,0:T(8,128)(2,1)S(1)} %get-tuple-element.45.refs_0_), channel_id=1, source_target_pairs={{0,4},{4,8},{8,12},{12,0},{1,5},{5,9},{9,13},{13,1},{2,6},{6,10},{... | collective-permute-start | bytes 835592 | tf_op jit(solution)/shard_map/ppermute | solution.py:385
  12.2 3.6 %collective-permute-start.2 = (bf16[272,512]{1,0:T(8,128)(2,1)S(1)}, bf16[272,512]{1,0:T(8,128)(2,1)S(1)}, u32[]{:S(2)}, u32[]{:S(2)}) collective-permute-start(bf16[272,512]{1,0:T(8,128)(2,1)S(1)} %get-tuple-element.45.refs_0_), channel_id=1, source_target_pairs={{0,1},{1,0},{2,3},{3,2},{4,5},{5,4},{6,7},{7,6},{8,9},{9,8},{10,11... | collective-permute-start | bytes 835592 | tf_op jit(solution)/shard_map/ppermute | solution.py:408
  15.6 1.6 %collective-permute-start.3 = (bf16[272,512]{1,0:T(8,128)(2,1)S(1)}, bf16[272,512]{1,0:T(8,128)(2,1)S(1)}, u32[]{:S(2)}, u32[]{:S(2)}) collective-permute-start(bf16[272,512]{1,0:T(8,128)(2,1)S(1)} %collective-permute-done.refs_1_), channel_id=1, source_target_pairs={{0,1},{1,0},{2,3},{3,2},{4,5},{5,4},{6,7},{7,6},{8,9},{9,8},{10,11... | collective-permute-start | bytes 835592 | tf_op jit(solution)/shard_map/ppermute | solution.py:413
  15.7 10.9 %collective-permute-start.1 = (bf16[272,512]{1,0:T(8,128)(2,1)S(1)}, bf16[272,512]{1,0:T(8,128)(2,1)S(1)}, u32[]{:S(2)}, u32[]{:S(2)}) collective-permute-start(bf16[272,512]{1,0:T(8,128)(2,1)S(1)} %collective-permute-done.refs_1_), channel_id=1, source_target_pairs={{0,4},{4,8},{8,12},{12,0},{1,5},{5,9},{9,13},{13,1},{2,6},{6,10},{... | collective-permute-start | bytes 835592 | tf_op jit(solution)/shard_map/ppermute | solution.py:412
  26.6 1.6 %collective-permute-start.4 = (bf16[272,512]{1,0:T(8,128)(2,1)S(1)}, bf16[272,512]{1,0:T(8,128)(2,1)S(1)}, u32[]{:S(2)}, u32[]{:S(2)}) collective-permute-start(bf16[272,512]{1,0:T(8,128)(2,1)S(1)} %collective-permute-done.1.far_ref), channel_id=1, source_target_pairs={{0,1},{1,0},{2,3},{3,2},{4,5},{5,4},{6,7},{7,6},{8,9},{9,8},{10,11... | collective-permute-start | bytes 835592 | tf_op jit(solution)/shard_map/ppermute | solution.py:428
  33.6 17.2 %collective-permute-start.6 = (bf16[256,640]{1,0:T(8,128)(2,1)S(1)}, bf16[256,640]{1,0:T(8,128)(2,1)S(1)}, u32[]{:S(2)}, u32[]{:S(2)}) collective-permute-start(bf16[256,640]{1,0:T(8,128)(2,1)S(1)} %get-tuple-element.49), channel_id=1, source_target_pairs={{0,2},{2,0},{1,3},{3,1},{4,6},{6,4},{5,7},{7,5},{8,10},{10,8},{9,1... | collective-permute-start | bytes 983048 | tf_op jit(solution)/shard_map/ppermute | solution.py:458
  35.2 12.4 %collective-permute-start.5 = (bf16[256,384]{1,0:T(8,128)(2,1)S(1)}, bf16[256,384]{1,0:T(8,128)(2,1)S(1)}, u32[]{:S(2)}, u32[]{:S(2)}) collective-permute-start(bf16[256,384]{1,0:T(8,128)(2,1)S(1)} %get-tuple-element.56), channel_id=1, source_target_pairs={{0,2},{2,0},{1,3},{3,1},{4,6},{6,4},{5,7},{7,5},{8,10},{10,8},{9,1... | collective-permute-start | bytes 589832 | tf_op jit(solution)/shard_map/ppermute | solution.py:458
  47.9 8.2 %collective-permute-start.7 = (bf16[112,384]{1,0:T(8,128)(2,1)S(1)}, bf16[112,384]{1,0:T(8,128)(2,1)S(1)}, u32[]{:S(2)}, u32[]{:S(2)}) collective-permute-start(bf16[112,384]{1,0:T(8,128)(2,1)S(1)} %get-tuple-element.58), channel_id=1, source_target_pairs={{0,4},{4,0},{8,12},{12,8},{1,5},{5,1},{9,13},{13,9},{2,6},{6,2},{1... | collective-permute-start | bytes 258056 | tf_op jit(solution)/shard_map/ppermute | solution.py:472
  51.1 21.8 %collective-permute-start.10 = (bf16[96,640]{1,0:T(8,128)(2,1)S(1)}, bf16[96,640]{1,0:T(8,128)(2,1)S(1)}, u32[]{:S(2)}, u32[]{:S(2)}) collective-permute-start(bf16[96,640]{1,0:T(8,128)(2,1)S(1)} %get-tuple-element.64), channel_id=1, source_target_pairs={{0,4},{4,0},{8,12},{12,8},{1,5},{5,1},{9,13},{13,9},{2,6},{6,2},{1... | collective-permute-start | bytes 368648 | tf_op jit(solution)/shard_map/ppermute | solution.py:472
  53.2 19.7 %collective-permute-start.11 = (bf16[96,640]{1,0:T(8,128)(2,1)S(1)}, bf16[96,640]{1,0:T(8,128)(2,1)S(1)}, u32[]{:S(2)}, u32[]{:S(2)}) collective-permute-start(bf16[96,640]{1,0:T(8,128)(2,1)S(1)} %get-tuple-element.65), channel_id=1, source_target_pairs={{0,8},{4,12},{8,0},{12,4},{1,9},{5,13},{9,1},{13,5},{2,10},{6,14},... | collective-permute-start | bytes 368648 | tf_op jit(solution)/shard_map/ppermute | solution.py:472
  53.2 19.7 %collective-permute-start.12 = (bf16[96,640]{1,0:T(8,128)(2,1)S(1)}, bf16[96,640]{1,0:T(8,128)(2,1)S(1)}, u32[]{:S(2)}, u32[]{:S(2)}) collective-permute-start(bf16[96,640]{1,0:T(8,128)(2,1)S(1)} %get-tuple-element.66), channel_id=1, source_target_pairs={{0,12},{4,8},{8,4},{12,0},{1,13},{5,9},{9,5},{13,1},{2,14},{6,10},... | collective-permute-start | bytes 368648 | tf_op jit(solution)/shard_map/ppermute | solution.py:472
  55.6 16.7 %collective-permute-start.8 = (bf16[112,384]{1,0:T(8,128)(2,1)S(1)}, bf16[112,384]{1,0:T(8,128)(2,1)S(1)}, u32[]{:S(2)}, u32[]{:S(2)}) collective-permute-start(bf16[112,384]{1,0:T(8,128)(2,1)S(1)} %get-tuple-element.59), channel_id=1, source_target_pairs={{0,8},{4,12},{8,0},{12,4},{1,9},{5,13},{9,1},{13,5},{2,10},{6,14},... | collective-permute-start | bytes 258056 | tf_op jit(solution)/shard_map/ppermute | solution.py:472
  56.1 16.2 %collective-permute-start.9 = (bf16[112,384]{1,0:T(8,128)(2,1)S(1)}, bf16[112,384]{1,0:T(8,128)(2,1)S(1)}, u32[]{:S(2)}, u32[]{:S(2)}) collective-permute-start(bf16[112,384]{1,0:T(8,128)(2,1)S(1)} %get-tuple-element.60), channel_id=1, source_target_pairs={{0,12},{4,8},{8,4},{12,0},{1,13},{5,9},{9,5},{13,1},{2,14},{6,10},... | collective-permute-start | bytes 258056 | tf_op jit(solution)/shard_map/ppermute | solution.py:472
  73.8 2.0 %collective-permute-start.14 = (bf16[256,640]{1,0:T(8,128)(2,1)S(1)}, bf16[256,640]{1,0:T(8,128)(2,1)S(1)}, u32[]{:S(2)}, u32[]{:S(2)}) collective-permute-start(bf16[256,640]{1,0:T(8,128)(2,1)S(1)} %get-tuple-element.72), channel_id=1, source_target_pairs={{0,1},{1,0},{2,3},{3,2},{4,5},{5,4},{6,7},{7,6},{8,9},{9,8},{10,11... | collective-permute-start | bytes 983048 | tf_op jit(solution)/shard_map/ppermute | solution.py:506
  73.8 1.9 %collective-permute-start.13 = (bf16[256,384]{1,0:T(8,128)(2,1)S(1)}, bf16[256,384]{1,0:T(8,128)(2,1)S(1)}, u32[]{:S(2)}, u32[]{:S(2)}) collective-permute-start(bf16[256,384]{1,0:T(8,128)(2,1)S(1)} %get-tuple-element.71), channel_id=1, source_target_pairs={{0,1},{1,0},{2,3},{3,2},{4,5},{5,4},{6,7},{7,6},{8,9},{9,8},{10,11... | collective-permute-start | bytes 589832 | tf_op jit(solution)/shard_map/ppermute | solution.py:506

commit v4 on v3

--- a/solution.py
+++ b/solution.py
@@ -17,6 +17,7 @@
 VMEM = pl.BlockSpec(memory_space=pltpu.VMEM)
 ANY = pl.BlockSpec(memory_space=pl.ANY)
 MIB = 1 << 20
+BUSY = 20 * 10**9
 KV_MIB = 53
 Q_MIB = 52
 FAR_MIB = 44
@@ -112,7 +113,7 @@
     finish(parts - 1, held)
 
 
-def route_kernel(ctx, cap, dest_ref, pos_ref, *slot_refs):
+def route_kernel(ctx, cap, dest_ref, pos_ref, all_ref, *slot_refs):
     rows = dest_ref.shape[1]
     mine_c, mine_r = lax.axis_index("ctx"), lax.axis_index("rep")
     dest = dest_ref[...]
@@ -135,12 +136,13 @@
         hit = (pos_col == (lane + k * 2 * cap).astype(F32)) & (lane < 2 * cap)
         got = jnp.sum(jnp.where(hit, target_col, 0.0), axis=0, keepdims=True) - 1.0
         slot_refs[k][...] = jnp.broadcast_to(got, slot_refs[k].shape)
+        all_ref[8 * k:8 * k + 8, :] = jnp.broadcast_to(got, slot_refs[k].shape)
 
 
 def documents(kv_ref):
     wide = kv_ref.shape[1] // 2
-    rows = kv_ref.shape[0] - 16
-    lines = kv_ref[rows:rows + 16, :wide].astype(F32)
+    rows = kv_ref.shape[0] // 128 * 128
+    lines = kv_ref[rows:rows + 8, :wide].astype(F32)
     return jnp.concatenate([lines[i:i + 1] for i in range(rows // wide)], 1)
 
 
@@ -175,46 +177,56 @@
 def choose(to_ref, flag, yes_ref, no_ref):
     @pl.when(flag)
     def _():
-        to_ref[...] = yes_ref[...]
+        to_ref[...] = yes_ref[0:to_ref.shape[0], :]
 
     @pl.when(jnp.logical_not(flag))
     def _():
-        to_ref[...] = no_ref[...]
-
-
-def near_kernel(hops, seg_ref, q_ref, *refs):
-    hop, pair, out_ref = refs[:hops], refs[hops:2 * hops], refs[2 * hops]
-    odd, bias = refs[2 * hops + 1:-1], refs[-1]
+        to_ref[...] = no_ref[0:to_ref.shape[0], :]
+
+
+def near_kernel(seg_ref, q_ref, *refs):
+    n = (len(refs) - 2) // 2
+    blocks, out_ref, copies, bias = refs[:n], refs[n], refs[n + 1:-1], refs[-1]
+    for copy, block in zip(copies, blocks, strict=True):
+        copy[...] = block[0:copy.shape[0], :]
     rows = q_ref.shape[1]
-    c, r = lax.axis_index("ctx"), lax.axis_index("rep")
     seg = seg_ref[...].astype(F32)
     seg_col = column_of(seg)
-    lowest = jnp.min(seg)
     ii = lax.broadcasted_iota(jnp.int32, (rows, rows), 0)
     jj = lax.broadcasted_iota(jnp.int32, (rows, rows), 1)
     bias[0] = jnp.where((seg == seg_col) & (jj <= ii), 0.0, HIDE)
-    blocks = [hop[0]]
-    for i in range(1, hops):
-        choose(odd[i - 1], r == 1, pair[i - 1], pair[i])
-        blocks += [odd[i - 1], hop[i]]
-    me = c * 2 + r
+    back = [2 * i for i in range(len(blocks))]
+    accumulate(q_ref, blocks, back, seg_col, jnp.min(seg), bias, out_ref, out_ref, True)
+
+
+def middle_kernel(seg_ref, q_ref, *refs):
+    n = (len(refs) - 4) // 2
+    pair, (near_ref, out_ref), (odd, bias) = refs[:n + 1], refs[n + 1:n + 3], (refs[n + 3:-1], refs[-1])
+    seg = seg_ref[...].astype(F32)
+    r = lax.axis_index("rep")
+    for i in range(n):
+        choose(odd[i], r == 1, pair[i], pair[i + 1])
+    back = [2 * i + 1 for i in range(n)]
+    accumulate(q_ref, odd, back, column_of(seg), jnp.min(seg), bias, near_ref, out_ref, False)
+
+
+def accumulate(q_ref, blocks, back, seg_col, lowest, bias, in_ref, out_ref, fresh):
+    me = lax.axis_index("ctx") * 2 + lax.axis_index("rep")
     size = 3
     for start in range(0, len(blocks), size):
         some = blocks[start:start + size]
         seen = []
-        for d in range(start, start + len(some)):
-            if d:
-                hide(bias.at[d], blocks[d], seg_col)
-                seen.append((me >= d) & (jnp.max(documents(blocks[d])) == lowest))
-        count = sum([x.astype(jnp.int32) for x in seen]) + (1 if start == 0 else 0)
+        for i, block in enumerate(some, start):
+            if back[i]:
+                hide(bias.at[i], block, seg_col)
+                seen.append(((me >= back[i]) & (jnp.max(documents(block)) == lowest)).astype(jnp.int32))
+        first = fresh and start == 0
+        count = sum(seen) + (1 if first else 0)
         for n in range(1, len(some) + 1):
             @pl.when(count == n)
-            def _(n=n, start=start, some=some):
+            def _(n=n, start=start, some=some, first=first):
                 def finish(j, new):
-                    if start == 0:
-                        out_ref[j] = new
-                    else:
-                        out_ref[j] += new
+                    out_ref[j] = new if first else in_ref[j] + new
                 attend(q_ref, some[:n], [bias.at[start + i] for i in range(n)], finish)
 
 
@@ -298,19 +310,43 @@
     return jnp.dot(jnp.where(hit, 1.0, 0.0).astype(BF16), total, preferred_element_type=F32).astype(BF16)
 
 
-def pick_kernel(ctx, n_slots, span, mark, pos_ref, *refs):
-    slots, shares, outs = refs[:n_slots], refs[n_slots:-ctx], refs[-ctx:]
+def pick_kernel(ctx, span, mark, pos_ref, pair_slots, *refs):
+    slots, shares, outs = refs[:ctx], refs[ctx:-ctx], refs[-ctx:]
     moved = take(pos_ref[0:1, :], span * ctx, add_shares(shares))
     for k, out in enumerate(outs):
         out[0:span, :] = moved[k * span:(k + 1) * span]
-        if n_slots:
-            out[mark:, :] = jnp.zeros((16, out.shape[1]), BF16)
-            lanes = slots[k].shape[1]
-            out[mark:, 0:lanes] = jnp.concatenate([slots[k][...]] * 2, 0).astype(BF16)
-
-
-def slot_line(ref, at, span):
-    return ref[at:at + 16, 0:span].astype(F32)[0:1].astype(jnp.int32)
+        out[mark:, :] = jnp.zeros((16, out.shape[1]), BF16)
+        lanes = slots[k].shape[1]
+        out[mark:, 0:lanes] = jnp.concatenate([slots[k][...], pair_slots[8 * k:8 * k + 8, :]], 0).astype(BF16)
+
+
+def split_kernel(cap, pos_ref, *refs):
+    shares, (stay_ref, *leave_refs) = refs[:-3], refs[-3:]
+    total = add_shares(shares)
+    count = stay_ref.shape[0]
+    pos = pos_ref[0:1, :]
+    line = lax.div(pos, cap)
+    at = lax.div(line, 2) * cap + (pos - line * cap)
+    same = line - lax.div(line, 2) * 2 == 0
+    stay_ref[...] = take(jnp.where(same, at, -1), count, total)
+    leave = take(jnp.where(same, -1, at), count, total)
+    part = leave_refs[0].shape[0]
+    for i, ref in enumerate(leave_refs):
+        ref[...] = leave[i * part:(i + 1) * part]
+
+
+def merge_kernel(cap, stay_ref, *refs):
+    came, outs = refs[:2], refs[2:]
+    for k, out in enumerate(outs):
+        out[0:cap, :] = stay_ref[k * cap:(k + 1) * cap, :]
+        came_ref = came[2 * k // len(outs)]
+        first = k % (len(outs) // 2) * cap
+        out[cap:, :] = came_ref[first:first + cap, :]
+
+
+def slot_lines(ref, at, span):
+    lines = ref[at:at + 16, 0:span].astype(F32).astype(jnp.int32)
+    return lines[0:1], lines[8:9]
 
 
 def put(slot, block, count):
@@ -319,12 +355,12 @@
 
 
 def place_kernel(ctx, cap, rows, mark, *refs):
-    blocks, marked, (mine_ref, pair_ref) = refs[:ctx], refs[ctx:2 * ctx], refs[2 * ctx:]
+    blocks, (mine_ref, pair_ref) = refs[:ctx], refs[ctx:]
     span = 2 * cap
     total = None
     lane = lax.broadcasted_iota(jnp.int32, (1, span), 1)
-    for block, marks in zip(blocks, marked, strict=True):
-        slot = slot_line(marks, mark, span)
+    for block in blocks:
+        slot, _ = slot_lines(block, mark, span)
         slot = jnp.where((slot >= 0) & (lane >= cap), slot + rows, slot)
         some = put(slot, block[0:span, :], 2 * rows)
         total = some if total is None else total + some
@@ -332,13 +368,24 @@
     pair_ref[...] = total[rows:].astype(BF16)
 
 
-def join_kernel(n, *refs):
-    out = refs[-1]
-    at = 0
-    for mine, other in zip(refs[:n], refs[n:2 * n], strict=True):
-        width = mine.shape[1]
-        out[:, at:at + width] = (mine[...].astype(F32) + other[...].astype(F32)).astype(BF16)
-        at += width
+def final_kernel(ctx, cap, mark, *refs):
+    marks, blocks, out = refs[:ctx], refs[ctx:-1], refs[-1]
+    rows = out.shape[0]
+    span = 2 * cap
+    lane = lax.broadcasted_iota(jnp.int32, (1, span), 1)
+    total = None
+    for k in range(ctx):
+        mine, pair = slot_lines(marks[k], mark, span)
+        slot = jnp.where(lane < cap, mine, pair)
+        some = put(slot, blocks[k][...], rows)
+        total = some if total is None else total + some
+    out[...] = total.astype(BF16)
+
+
+def join_kernel(mine_ref, pair_ref, rest_ref, out):
+    rows, at = mine_ref.shape
+    out[:, 0:at] = (mine_ref[...].astype(F32) + pair_ref[...].astype(F32)).astype(BF16)
+    out[:, at:] = rest_ref[...]
 
 
 def after(x, *earlier):
@@ -358,8 +405,7 @@
     lanes = -(-span // 128) * 128
     every = ctx * span
     sds = jax.ShapeDtypeStruct
-    units = half // 128
-    chunks = [n * 128 for n in (units * 3 // 8, units - units * 3 // 8)]
+    chunks = [half // 2] * 2
 
     up = [(i, (i + 1) % ctx) for i in range(ctx)]
     swap = [(0, 1), (1, 0)]
@@ -399,31 +445,43 @@
     route = pl.pallas_call(
         functools.partial(route_kernel, ctx, cap),
         in_specs=[VMEM],
-        out_specs=[VMEM] * (1 + ctx),
-        out_shape=[sds((8, rows), jnp.int32)] + [sds((8, lanes), F32)] * ctx,
+        out_specs=[VMEM] * (2 + ctx),
+        out_shape=[sds((8, rows), jnp.int32), sds((8 * ctx, lanes), F32)] + [sds((8, lanes), F32)] * ctx,
         compiler_params=params(8),
-        cost_estimate=cost(4 * rows * rows, 8 * rows * 4),
+        cost_estimate=cost(0, 0),
         name="routes",
     )
-    pair = [lax.ppermute(after(own, queries), "rep", swap)]
     hop[1] = after(hop[1], queries)
-    buffer_pos, *slots = route(after(dest_rows.reshape(1, rows), hop[1]))
     for i in range(1, hops):
         hop.append(lax.ppermute(hop[i], "ctx", up))
-        pair.append(lax.ppermute(after(hop[i], buffer_pos), "rep", swap))
 
     work = heads * rows * rows
+    short = sds((rows + 8, 2 * kv_cols), BF16)
+    near, *short_hop = pl.pallas_call(
+        near_kernel,
+        in_specs=[VMEM] * (2 + hops),
+        out_specs=[VMEM] * (1 + hops),
+        out_shape=[sds((heads, rows, 2 * HD), F32)] + [short] * hops,
+        scratch_shapes=[pltpu.VMEM((hops, rows, rows), F32)],
+        compiler_params=params(12),
+        cost_estimate=cost(4 * work * HD * hops, 8 * MIB, work * hops),
+        name="even_attention",
+    )(seg_row, queries, *hop[:hops])
+
+    buffer_pos, pair_slots, *slots = route(after(dest_rows.reshape(1, rows), near))
+    pair_slots = lax.ppermute(pair_slots, "rep", swap)
+    pair = [lax.ppermute(x, "rep", swap) for x in short_hop]
     near = pl.pallas_call(
-        functools.partial(near_kernel, hops),
-        in_specs=[VMEM] * (2 + 2 * hops),
+        middle_kernel,
+        in_specs=[VMEM] * (3 + hops),
         out_specs=VMEM,
         out_shape=sds((heads, rows, 2 * HD), F32),
-        scratch_shapes=[pltpu.VMEM(payload.shape, BF16)] * (hops - 1) + [pltpu.VMEM((2 * hops - 1, rows, rows), F32)],
+        scratch_shapes=[pltpu.VMEM(short.shape, BF16)] * (hops - 1) + [pltpu.VMEM((hops - 1, rows, rows), F32)],
+        input_output_aliases={2 + hops: 0},
         compiler_params=params(12),
-        cost_estimate=cost(8 * work * HD * hops, 8 * MIB, 2 * work * hops),
-        name="near_attention",
-    )(after(seg_row, buffer_pos), queries, *hop[:hops], *pair[:hops])
-
+        cost_estimate=cost(0, 0),
+        name="odd_attention",
+    )(after(seg_row, pair_slots), queries, *pair, near)
     hop[hops] = after(hop[hops], near)
     pair.append(lax.ppermute(hop[hops], "rep", swap))
 
@@ -433,7 +491,7 @@
         in_specs=[VMEM] * 6 + [ANY],
         out_specs=[VMEM] * (1 + others),
         out_shape=[sds((rows, heads * HD), BF16)] + [sds((rows, n), BF16) for n in widths],
-        scratch_shapes=[pltpu.VMEM(payload.shape, BF16), pltpu.VMEM((2, rows, rows), F32)]
+        scratch_shapes=[pltpu.VMEM(short.shape, BF16), pltpu.VMEM((2, rows, rows), F32)]
         + [pltpu.VMEM((heads * HD, sum(widths)), BF16), pltpu.SemaphoreType.DMA((others,))],
         compiler_params=params(FAR_MIB),
         cost_estimate=cost(8 * work * HD + 2 * rows * heads * HD * chunks[0], 10 * MIB, 2 * work),
@@ -448,7 +506,7 @@
             out_shape=[sds((rows, n), BF16) for n in sizes],
             scratch_shapes=[pltpu.VMEM((heads * HD, sum(sizes)), BF16), pltpu.SemaphoreType.DMA((len(steps),))],
             compiler_params=params(PROJECT_MIB),
-            cost_estimate=cost(2 * rows * heads * HD * sum(sizes), 2 * heads * HD * sum(sizes)),
+            cost_estimate=cost(BUSY, 0),
             name="project",
         )(x, w_out)
 
@@ -472,48 +530,75 @@
         return [xs[0]] + [lax.ppermute(xs[k], "ctx", [(i, i ^ k) for i in range(ctx)]) for k in range(1, ctx)]
 
     mark = -(-span // 16) * 16
-    moved, got, shares = [], [], [[mine, *theirs[0]]]
-    for j, n in enumerate(chunks):
-        extra = slots if j == 0 else []
-        tall = mark + 16 if j == 0 else span
-        if j == 1:
-            ours = project_some(after(attended, *moved), [(0, starts[i]) for i in later], chunks[1:])
-            shares += [[x, *theirs[i + 1]] for i, x in enumerate(ours)]
-        picked = pl.pallas_call(
-            functools.partial(pick_kernel, ctx, len(extra), span, mark),
-            in_specs=[VMEM] * (1 + len(extra) + n_head),
+    n = chunks[0]
+    moved = pl.pallas_call(
+        functools.partial(pick_kernel, ctx, span, mark),
+        in_specs=[VMEM] * (2 + ctx + n_head),
+        out_specs=[VMEM] * ctx,
+        out_shape=[sds((mark + 16, n), BF16)] * ctx,
+        compiler_params=params(8),
+        cost_estimate=cost(0, 0),
+        name="add_pick",
+    )(after(buffer_pos, *sent), pair_slots, *slots, mine, *theirs[0])
+    first = across(moved)
+
+    ours = project_some(after(attended, *moved), [(0, starts[j]) for j in later], chunks[1:])
+    held, last = [], list(moved)
+    for j in later:
+        n = chunks[j]
+        stay, *leave = pl.pallas_call(
+            functools.partial(split_kernel, cap),
+            in_specs=[VMEM] * (1 + n_head),
+            out_specs=[VMEM] * 3,
+            out_shape=[sds((ctx * cap, n), BF16)] + [sds((ctx * cap // 2, n), BF16)] * 2,
+            compiler_params=params(8),
+            cost_estimate=cost(0, 0),
+            name="add_split",
+        )(after(buffer_pos, *last), ours[j - 1], *theirs[j])
+        leave = [lax.ppermute(x, "rep", swap) for x in leave]
+        moved = pl.pallas_call(
+            functools.partial(merge_kernel, cap),
+            in_specs=[VMEM] * 3,
             out_specs=[VMEM] * ctx,
-            out_shape=[sds((tall, n), BF16)] * ctx,
+            out_shape=[sds((span, n), BF16)] * ctx,
             compiler_params=params(8),
-            cost_estimate=cost(2 * every * rows * n, 2 * n * (2 * rows + every)),
-            name="add_pick",
-        )(after(buffer_pos, *sent, *moved), *extra, *shares[j])
-        moved += picked
-        got.append(across(picked))
-
-    kept, gone = [], []
-    for j, n in enumerate(chunks):
-        stay, leave = pl.pallas_call(
-            functools.partial(place_kernel, ctx, cap, rows, mark),
-            in_specs=[VMEM] * (2 * ctx),
-            out_specs=[VMEM] * 2,
-            out_shape=[sds((rows, n), BF16)] * 2,
-            compiler_params=params(8),
-            cost_estimate=cost(4 * every * rows * n, 2 * n * (2 * rows + every)),
-            name="place",
-        )(after(got[j][0], *moved, *kept), *got[j][1:], *got[0])
-        kept.append(stay)
-        gone.append(lax.ppermute(leave, "rep", swap))
+            cost_estimate=cost(0, 0),
+            name="merge",
+        )(stay, *leave)
+        held.append(across(moved))
+        last = list(moved)
+
+    n = chunks[0]
+    stay, leave = pl.pallas_call(
+        functools.partial(place_kernel, ctx, cap, rows, mark),
+        in_specs=[VMEM] * ctx,
+        out_specs=[VMEM] * 2,
+        out_shape=[sds((rows, n), BF16)] * 2,
+        compiler_params=params(8),
+        cost_estimate=cost(BUSY, 0),
+        name="place",
+    )(after(first[0], *held[0][:1]), *first[1:])
+    leave = lax.ppermute(leave, "rep", swap)
+
+    rest = pl.pallas_call(
+        functools.partial(final_kernel, ctx, cap, mark),
+        in_specs=[VMEM] * (2 * ctx),
+        out_specs=VMEM,
+        out_shape=sds((rows, chunks[1]), BF16),
+        compiler_params=params(8),
+        cost_estimate=cost(BUSY, 0),
+        name="place_rest",
+    )(first[0], *first[1:], *held[0])
 
     return pl.pallas_call(
-        functools.partial(join_kernel, len(chunks)),
-        in_specs=[VMEM] * (2 * len(chunks)),
+        join_kernel,
+        in_specs=[VMEM] * 3,
         out_specs=VMEM,
         out_shape=sds((rows, half), BF16),
         compiler_params=params(8),
-        cost_estimate=cost(rows * half, 6 * rows * half),
+        cost_estimate=cost(0, 0),
         name="join",
-    )(*kept, *gone)
+    )(stay, leave, rest)
 
 
 def solution(mesh):

time: 76.8 us -> 59.5 us (0.77)
  waiting for transfers between devices: 40.2 us -> 22.3 us
  starting transfers between devices: 13.9 us -> 15.5 us
  Pallas kernels: 21.6 us -> 20.6 us
    ppermute x2, waiting for transfers between devices: 11.9 us -> 4 us  [to_heads(): lax.ppermute(x, 'head', flip)]
    ppermute x6, waiting for transfers between devices: 13.3 us -> 5.7 us  [across(): lax.ppermute(xs[k], 'ctx', [(i, i ^ k) for i in range(ctx)])]
    ppermute x1, waiting for transfers between devices: 7.49 us -> 5.83 us  [local(): hop.append(lax.ppermute(hop[i], 'ctx', up))]
    ppermute x6, starting transfers between devices: 7.98 us -> 8.9 us  [across(): lax.ppermute(xs[k], 'ctx', [(i, i ^ k) for i in range(ctx)])]
    ppermute x4 -> x6, waiting for transfers between devices: 2.87 us -> 2.06 us  [the longest x1 1.11 us: local(): pair_slots = lax.ppermute(pair_slots, 'rep', swap)]
    pallas_call x5 -> x8, Pallas kernels: 3.66 us -> 3.89 us  [the longest x1 1.52 us: local(): pl.pallas_call(near_kernel, in_specs=[VMEM] * (2 + hops), out_specs=[VMEM...]
  transfers between devices with their start and end apart: 15 -> 17, of which waited for: 7 -> 9; matrix products, arithmetic and copies ran while one was open for 0% -> 0% of each run, Pallas kernels for 15% -> 25%
where the time goes in v4:
time: 59.5 us; the launch traced here: 59.3 us
  waiting for transfers between devices  22.3 us (37%)
  Pallas kernels  20.6 us (35%)
  starting transfers between devices  15.5 us (26%)
  local copies, waits for them, and re-layouts  0.76 us (1%)
    ppermute x6, starting transfers between devices, across(): lax.ppermute(xs[k], 'ctx', [(i, i ^ k) for i in range(ctx)])  8.9 us
    ppermute x1, waiting for transfers between devices, local(): hop.append(lax.ppermute(hop[i], 'ctx', up))  5.83 us
    ppermute x6, waiting for transfers between devices, across(): lax.ppermute(xs[k], 'ctx', [(i, i ^ k) for i in range(ctx)])  5.7 us
    pallas_call x1, Pallas kernels, local(): pl.pallas_call(functools.partial(q_kernel, parts), in_specs=[ANY, ANY, VM...  5.51 us
    pallas_call x2, Pallas kernels, project_some(): pl.pallas_call(functools.partial(project_kernel, steps), in_specs=[VMEM,...  5.36 us
    ppermute x2, waiting for transfers between devices, to_heads(): lax.ppermute(x, 'head', flip)  4 us
    ppermute x1, waiting for transfers between devices, local(): hop = [own, lax.ppermute(own, 'ctx', up)]  3.17 us
    ppermute x1, starting transfers between devices, local(): hop = [own, lax.ppermute(own, 'ctx', up)]  3.07 us
  transfers between devices with their start and end apart: 17, of which 9 were waited for; matrix products, arithmetic and copies ran while one was open for 0% of the time, Pallas kernels for 25%

profile of v4, /device:TPU:0, one launch (start us, length us, event | category | flops | bytes accessed | tf_op | source)
XLA Modules:
  0.0 59.3 jit_solution(14776186534937518258)
XLA Ops:
  0.0 0.7 %copy-done = s32[256]{0:T(256)S(1)} copy-done((s32[256]{0:T(256)S(1)}, s32[256]{0:T(256)}, u32[]{:S(2)}) %copy-start) | copy-done | bytes 1048
  0.8 2.8 %keys_values.1 = (bf16[272,512]{1,0:T(8,128)(2,1)S(1)}, f32[256,256]{1,0:T(8,128)S(1)}) custom-call(bf16[256,2048]{1,0:T(8,128)(2,1)} %x_hbm.3, bf16[2048,256]{1,0:T(8,128)(2,1)} %wk_hbm.1, bf16[2048,256]{1,0:T(8,128)(2,1)} %wv_hbm.1, s32[1,256]{1,0:T(1,128)S(1)} %bitcast.2), custom_call_target="tpu_custom_call" | custom-call | flops 536870912 | bytes 3145728 | tf_op jit(solution)/shard_map/keys_values/pallas_call | solution.py:416
  3.6 3.1 %collective-permute-start = (bf16[272,512]{1,0:T(8,128)(2,1)S(1)}, bf16[272,512]{1,0:T(8,128)(2,1)S(1)}, u32[]{:S(2)}, u32[]{:S(2)}) collective-permute-start(bf16[272,512]{1,0:T(8,128)(2,1)S(1)} %get-tuple-element.42.refs_0_), channel_id=1, source_target_pairs={{0,4},{4,8},{8,12},{12,0},{1,5},{5,9},{9,13},{13,1},{2,6},{6,10},{... | collective-permute-start | bytes 835592 | tf_op jit(solution)/shard_map/ppermute | solution.py:431
  6.7 5.5 %queries.1.q_ref = bf16[16,256,128]{2,1,0:T(8,128)(2,1)S(1)} custom-call(bf16[256,2048]{1,0:T(8,128)(2,1)} %x_hbm.3, bf16[2048,2048]{1,0:T(8,128)(2,1)} %w_hbm.4, f32[256,256]{1,0:T(8,128)S(1)} %get-tuple-element.41.tab_ref), custom_call_target="tpu_custom_call" | custom-call | flops 2147483648 | bytes 9437184 | tf_op jit(solution)/shard_map/queries/pallas_call | solution.py:434
  12.2 3.2 %collective-permute-done.refs_1_ = bf16[272,512]{1,0:T(8,128)(2,1)S(1)} collective-permute-done((bf16[272,512]{1,0:T(8,128)(2,1)S(1)}, bf16[272,512]{1,0:T(8,128)(2,1)S(1)}, u32[]{:S(2)}, u32[]{:S(2)}) %collective-permute-start) | collective-permute-done | bytes 278560 | tf_op jit(solution)/shard_map/ppermute | solution.py:431
  15.4 1.5 %even_attention.1 = (f32[16,256,256]{2,1,0:T(8,128)S(1)}, bf16[264,512]{1,0:T(8,128)(2,1)S(1)}, bf16[264,512]{1,0:T(8,128)(2,1)S(1)}) custom-call(s32[1,256]{1,0:T(1,128)S(1)} %bitcast.3, bf16[16,256,128]{2,1,0:T(8,128)(2,1)S(1)} %queries.1.q_ref, bf16[272,512]{1,0:T(8,128)(2,1)S(1)} %get-tuple-element.42.refs_0_, ...), custom_call_target="tpu_custom_call" | custom-call | flops 1073741824 | bytes 8388608 | tf_op jit(solution)/shard_map/even_attention/pallas_call | solution.py:460
  17.0 0.5 collective-permute-start.4
  17.5 0.3 routes.1
  17.9 1.1 %collective-permute-done.2.pair_slots = f32[32,128]{1,0:T(8,128)S(1)} collective-permute-done((f32[32,128]{1,0:T(8,128)S(1)}, f32[32,128]{1,0:T(8,128)S(1)}, u32[]{:S(2)}, u32[]{:S(2)}) %collective-permute-start.2) | collective-permute-done | bytes 16416 | tf_op jit(solution)/shard_map/ppermute | solution.py:472
  19.0 0.2 odd_attention.1.near_ref
  19.2 5.8 %collective-permute-done.1.far_ref = bf16[272,512]{1,0:T(8,128)(2,1)S(1)} collective-permute-done((bf16[272,512]{1,0:T(8,128)(2,1)S(1)}, bf16[272,512]{1,0:T(8,128)(2,1)S(1)}, u32[]{:S(2)}, u32[]{:S(2)}) %collective-permute-start.1) | collective-permute-done | bytes 278560 | tf_op jit(solution)/shard_map/ppermute | solution.py:456
  25.0 1.6 %collective-permute-done.5.to_zero = bf16[272,512]{1,0:T(8,128)(2,1)S(1)} collective-permute-done((bf16[272,512]{1,0:T(8,128)(2,1)S(1)}, bf16[272,512]{1,0:T(8,128)(2,1)S(1)}, u32[]{:S(2)}, u32[]{:S(2)}) %collective-permute-start.5) | collective-permute-done | bytes 278560 | tf_op jit(solution)/shard_map/ppermute | solution.py:486
  26.6 2.3 %far_attention_project.1 = (bf16[256,2048]{1,0:T(8,128)(2,1)S(1)}, bf16[256,512]{1,0:T(8,128)(2,1)S(1)}) custom-call(s32[1,256]{1,0:T(1,128)S(1)} %bitcast.5, bf16[16,256,128]{2,1,0:T(8,128)(2,1)S(1)} %queries.1.q_ref, bf16[272,512]{1,0:T(8,128)(2,1)S(1)} %collective-permute-done.1.far_ref, bf16[264,512]{1,0:T(8,128)(2,1)S(1)} %collective-permute-done.4.refs_1_.to_one, ...), custom_call_target="tpu_custom_call" | custom-call | flops 1610612736 | bytes 10485760 | tf_op jit(solution)/shard_map/far_attention_project/pallas_call | solution.py:489
  28.9 1.3 %collective-permute-start.6 = (bf16[256,512]{1,0:T(8,128)(2,1)S(1)}, bf16[256,512]{1,0:T(8,128)(2,1)S(1)}, u32[]{:S(2)}, u32[]{:S(2)}) collective-permute-start(bf16[256,512]{1,0:T(8,128)(2,1)S(1)} %get-tuple-element.60), channel_id=1, source_target_pairs={{0,2},{2,0},{1,3},{3,1},{4,6},{6,4},{5,7},{7,5},{8,10},{10,8},{9,1... | collective-permute-start | bytes 786440 | tf_op jit(solution)/shard_map/ppermute | solution.py:516
  30.2 3.1 %project.2 = (bf16[256,512]{1,0:T(8,128)(2,1)S(1)}, bf16[256,512]{1,0:T(8,128)(2,1)S(1)}) custom-call(bf16[256,2048]{1,0:T(8,128)(2,1)S(1)} %get-tuple-element.66.att_ref, bf16[2048,2048]{1,0:T(8,128)(2,1)} %w_hbm.7), custom_call_target="tpu_custom_call" | custom-call | flops 20000000000 | tf_op jit(solution)/shard_map/project/pallas_call | solution.py:502
  33.2 0.8 %collective-permute-start.7 = (bf16[256,512]{1,0:T(8,128)(2,1)S(1)}, bf16[256,512]{1,0:T(8,128)(2,1)S(1)}, u32[]{:S(2)}, u32[]{:S(2)}) collective-permute-start(bf16[256,512]{1,0:T(8,128)(2,1)S(1)} %get-tuple-element.53), channel_id=1, source_target_pairs={{0,2},{2,0},{1,3},{3,1},{4,6},{6,4},{5,7},{7,5},{8,10},{10,8},{9,1... | collective-permute-start | bytes 786440 | tf_op jit(solution)/shard_map/ppermute | solution.py:516
  34.1 4.0 %collective-permute-done.6.refs_5_ = bf16[256,512]{1,0:T(8,128)(2,1)S(1)} collective-permute-done((bf16[256,512]{1,0:T(8,128)(2,1)S(1)}, bf16[256,512]{1,0:T(8,128)(2,1)S(1)}, u32[]{:S(2)}, u32[]{:S(2)}) %collective-permute-start.6) | collective-permute-done | bytes 262176 | tf_op jit(solution)/shard_map/ppermute | solution.py:516
  38.1 0.3 add_pick.1
  38.5 1.5 %collective-permute-start.11 = (bf16[112,512]{1,0:T(8,128)(2,1)S(1)}, bf16[112,512]{1,0:T(8,128)(2,1)S(1)}, u32[]{:S(2)}, u32[]{:S(2)}) collective-permute-start(bf16[112,512]{1,0:T(8,128)(2,1)S(1)} %get-tuple-element.63), channel_id=1, source_target_pairs={{0,8},{4,12},{8,0},{12,4},{1,9},{5,13},{9,1},{13,5},{2,10},{6,14},... | collective-permute-start | bytes 344072 | tf_op jit(solution)/shard_map/ppermute | solution.py:530
  39.9 2.9 %collective-permute-start.12 = (bf16[112,512]{1,0:T(8,128)(2,1)S(1)}, bf16[112,512]{1,0:T(8,128)(2,1)S(1)}, u32[]{:S(2)}, u32[]{:S(2)}) collective-permute-start(bf16[112,512]{1,0:T(8,128)(2,1)S(1)} %get-tuple-element.64), channel_id=1, source_target_pairs={{0,12},{4,8},{8,4},{12,0},{1,13},{5,9},{9,5},{13,1},{2,14},{6,10},... | collective-permute-start | bytes 344072 | tf_op jit(solution)/shard_map/ppermute | solution.py:530
  42.9 2.3 %project.3.refs_0_ = bf16[256,512]{1,0:T(8,128)(2,1)S(1)} custom-call(bf16[256,2048]{1,0:T(8,128)(2,1)S(1)} %get-tuple-element.66.att_ref, bf16[2048,2048]{1,0:T(8,128)(2,1)} %w_hbm.7), custom_call_target="tpu_custom_call" | custom-call | flops 20000000000 | tf_op jit(solution)/shard_map/project/pallas_call | solution.py:502
  45.2 0.3 add_split.1
  45.6 0.5 collective-permute-start.9
  46.1 0.8 %collective-permute-done.8.refs_0_ = bf16[96,512]{1,0:T(8,128)(2,1)S(1)} collective-permute-done((bf16[96,512]{1,0:T(8,128)(2,1)S(1)}, bf16[96,512]{1,0:T(8,128)(2,1)S(1)}, u32[]{:S(2)}, u32[]{:S(2)}) %collective-permute-start.8) | collective-permute-done | bytes 98336 | tf_op jit(solution)/shard_map/ppermute | solution.py:558
  46.9 0.2 collective-permute-done.9.refs_1_
  47.2 1.5 %collective-permute-start.15 = (bf16[96,512]{1,0:T(8,128)(2,1)S(1)}, bf16[96,512]{1,0:T(8,128)(2,1)S(1)}, u32[]{:S(2)}, u32[]{:S(2)}) collective-permute-start(bf16[96,512]{1,0:T(8,128)(2,1)S(1)} %get-tuple-element.75), channel_id=1, source_target_pairs={{0,8},{4,12},{8,0},{12,4},{1,9},{5,13},{9,1},{13,5},{2,10},{6,14},... | collective-permute-start | bytes 294920 | tf_op jit(solution)/shard_map/ppermute | solution.py:530
  48.6 2.9 %collective-permute-start.16 = (bf16[96,512]{1,0:T(8,128)(2,1)S(1)}, bf16[96,512]{1,0:T(8,128)(2,1)S(1)}, u32[]{:S(2)}, u32[]{:S(2)}) collective-permute-start(bf16[96,512]{1,0:T(8,128)(2,1)S(1)} %get-tuple-element.76), channel_id=1, source_target_pairs={{0,12},{4,8},{8,4},{12,0},{1,13},{5,9},{9,5},{13,1},{2,14},{6,10},... | collective-permute-start | bytes 294920 | tf_op jit(solution)/shard_map/ppermute | solution.py:530
  51.6 0.7 %place.1 = (bf16[256,512]{1,0:T(8,128)(2,1)S(1)}, bf16[256,512]{1,0:T(8,128)(2,1)S(1)}) custom-call(bf16[112,512]{1,0:T(8,128)(2,1)S(1)} %get-tuple-element.71.refs_0_, bf16[112,512]{1,0:T(8,128)(2,1)S(1)} %collective-permute-done.10.refs_1_, bf16[112,512]{1,0:T(8,128)(2,1)S(1)} %collective-permute-done.11.refs_2_, ...), custom_call_target="tpu_custom_call" | custom-call | flops 20000000000 | tf_op jit(solution)/shard_map/place/pallas_call | solution.py:572
  52.3 1.0 %collective-permute-done.14.refs_5_ = bf16[96,512]{1,0:T(8,128)(2,1)S(1)} collective-permute-done((bf16[96,512]{1,0:T(8,128)(2,1)S(1)}, bf16[96,512]{1,0:T(8,128)(2,1)S(1)}, u32[]{:S(2)}, u32[]{:S(2)}) %collective-permute-start.14) | collective-permute-done | bytes 98336 | tf_op jit(solution)/shard_map/ppermute | solution.py:530
  53.4 4.7 %collective-permute-done.15.refs_6_ = bf16[96,512]{1,0:T(8,128)(2,1)S(1)} collective-permute-done((bf16[96,512]{1,0:T(8,128)(2,1)S(1)}, bf16[96,512]{1,0:T(8,128)(2,1)S(1)}, u32[]{:S(2)}, u32[]{:S(2)}) %collective-permute-start.15) | collective-permute-done | bytes 98336 | tf_op jit(solution)/shard_map/ppermute | solution.py:530
  58.0 0.4 place_rest.1.rest_ref
  58.4 0.9 %join.1 = bf16[256,1024]{1,0:T(8,128)(2,1)} custom-call(bf16[256,512]{1,0:T(8,128)(2,1)S(1)} %get-tuple-element.72.mine_ref, bf16[256,512]{1,0:T(8,128)(2,1)S(1)} %collective-permute-done.13.pair_ref, bf16[256,512]{1,0:T(8,128)(2,1)S(1)} %place_rest.1.rest_ref), custom_call_target="tpu_custom_call" | custom-call | tf_op jit(solution)/shard_map/join/pallas_call | solution.py:593
  (22 shorter events, 0.6 us)
Async XLA Ops:
  0.0 15.4 %copy-start.1 = (s32[256]{0:T(256)S(1)}, s32[256]{0:T(256)}, u32[]{:S(2)}) copy-start(s32[256]{0:T(256)} %param.8) | copy-start | bytes 3076
  0.0 0.8 %copy-start = (s32[256]{0:T(256)S(1)}, s32[256]{0:T(256)}, u32[]{:S(2)}) copy-start(s32[256]{0:T(256)} %param.8) | copy-start | bytes 3076
  0.8 16.7 %copy-start.2 = (s32[256]{0:T(256)S(1)}, s32[256]{0:T(256)}, u32[]{:S(2)}) copy-start(s32[256]{0:T(256)} %param.9) | copy-start | bytes 3076
  3.6 11.7 %collective-permute-start = (bf16[272,512]{1,0:T(8,128)(2,1)S(1)}, bf16[272,512]{1,0:T(8,128)(2,1)S(1)}, u32[]{:S(2)}, u32[]{:S(2)}) collective-permute-start(bf16[272,512]{1,0:T(8,128)(2,1)S(1)} %get-tuple-element.42.refs_0_), channel_id=1, source_target_pairs={{0,4},{4,8},{8,12},{12,0},{1,5},{5,9},{9,13},{13,1},{2,6},{6,10},{... | collective-permute-start | bytes 835592 | tf_op jit(solution)/shard_map/ppermute | solution.py:431
  15.3 9.6 %collective-permute-start.1 = (bf16[272,512]{1,0:T(8,128)(2,1)S(1)}, bf16[272,512]{1,0:T(8,128)(2,1)S(1)}, u32[]{:S(2)}, u32[]{:S(2)}) collective-permute-start(bf16[272,512]{1,0:T(8,128)(2,1)S(1)} %collective-permute-done.refs_1_), channel_id=1, source_target_pairs={{0,4},{4,8},{8,12},{12,0},{1,5},{5,9},{9,13},{13,1},{2,6},{6,10},{... | collective-permute-start | bytes 835592 | tf_op jit(solution)/shard_map/ppermute | solution.py:456
  16.9 2.1 %collective-permute-start.3 = (bf16[264,512]{1,0:T(8,128)(2,1)S(1)}, bf16[264,512]{1,0:T(8,128)(2,1)S(1)}, u32[]{:S(2)}, u32[]{:S(2)}) collective-permute-start(bf16[264,512]{1,0:T(8,128)(2,1)S(1)} %get-tuple-element.49), channel_id=1, source_target_pairs={{0,1},{1,0},{2,3},{3,2},{4,5},{5,4},{6,7},{7,6},{8,9},{9,8},{10,11... | collective-permute-start | bytes 811016 | tf_op jit(solution)/shard_map/ppermute | solution.py:473
  17.0 2.0 %collective-permute-start.4 = (bf16[264,512]{1,0:T(8,128)(2,1)S(1)}, bf16[264,512]{1,0:T(8,128)(2,1)S(1)}, u32[]{:S(2)}, u32[]{:S(2)}) collective-permute-start(bf16[264,512]{1,0:T(8,128)(2,1)S(1)} %get-tuple-element.50), channel_id=1, source_target_pairs={{0,1},{1,0},{2,3},{3,2},{4,5},{5,4},{6,7},{7,6},{8,9},{9,8},{10,11... | collective-permute-start | bytes 811016 | tf_op jit(solution)/shard_map/ppermute | solution.py:473
  17.7 1.2 %collective-permute-start.2 = (f32[32,128]{1,0:T(8,128)S(1)}, f32[32,128]{1,0:T(8,128)S(1)}, u32[]{:S(2)}, u32[]{:S(2)}) collective-permute-start(f32[32,128]{1,0:T(8,128)S(1)} %get-tuple-element.47), channel_id=1, source_target_pairs={{0,1},{1,0},{2,3},{3,2},{4,5},{5,4},{6,7},{7,6},{8,9},{9,8},{10,11... | collective-permute-start | bytes 49160 | tf_op jit(solution)/shard_map/ppermute | solution.py:472
  25.0 1.6 %collective-permute-start.5 = (bf16[272,512]{1,0:T(8,128)(2,1)S(1)}, bf16[272,512]{1,0:T(8,128)(2,1)S(1)}, u32[]{:S(2)}, u32[]{:S(2)}) collective-permute-start(bf16[272,512]{1,0:T(8,128)(2,1)S(1)} %collective-permute-done.1.far_ref), channel_id=1, source_target_pairs={{0,1},{1,0},{2,3},{3,2},{4,5},{5,4},{6,7},{7,6},{8,9},{9,8},{10,11... | collective-permute-start | bytes 835592 | tf_op jit(solution)/shard_map/ppermute | solution.py:486
  28.9 9.2 %collective-permute-start.6 = (bf16[256,512]{1,0:T(8,128)(2,1)S(1)}, bf16[256,512]{1,0:T(8,128)(2,1)S(1)}, u32[]{:S(2)}, u32[]{:S(2)}) collective-permute-start(bf16[256,512]{1,0:T(8,128)(2,1)S(1)} %get-tuple-element.60), channel_id=1, source_target_pairs={{0,2},{2,0},{1,3},{3,1},{4,6},{6,4},{5,7},{7,5},{8,10},{10,8},{9,1... | collective-permute-start | bytes 786440 | tf_op jit(solution)/shard_map/ppermute | solution.py:516
  33.2 11.9 %collective-permute-start.7 = (bf16[256,512]{1,0:T(8,128)(2,1)S(1)}, bf16[256,512]{1,0:T(8,128)(2,1)S(1)}, u32[]{:S(2)}, u32[]{:S(2)}) collective-permute-start(bf16[256,512]{1,0:T(8,128)(2,1)S(1)} %get-tuple-element.53), channel_id=1, source_target_pairs={{0,2},{2,0},{1,3},{3,1},{4,6},{6,4},{5,7},{7,5},{8,10},{10,8},{9,1... | collective-permute-start | bytes 786440 | tf_op jit(solution)/shard_map/ppermute | solution.py:516
  38.4 10.2 %collective-permute-start.10 = (bf16[112,512]{1,0:T(8,128)(2,1)S(1)}, bf16[112,512]{1,0:T(8,128)(2,1)S(1)}, u32[]{:S(2)}, u32[]{:S(2)}) collective-permute-start(bf16[112,512]{1,0:T(8,128)(2,1)S(1)} %get-tuple-element.62), channel_id=1, source_target_pairs={{0,4},{4,0},{8,12},{12,8},{1,5},{5,1},{9,13},{13,9},{2,6},{6,2},{1... | collective-permute-start | bytes 344072 | tf_op jit(solution)/shard_map/ppermute | solution.py:530
  38.5 13.1 %collective-permute-start.11 = (bf16[112,512]{1,0:T(8,128)(2,1)S(1)}, bf16[112,512]{1,0:T(8,128)(2,1)S(1)}, u32[]{:S(2)}, u32[]{:S(2)}) collective-permute-start(bf16[112,512]{1,0:T(8,128)(2,1)S(1)} %get-tuple-element.63), channel_id=1, source_target_pairs={{0,8},{4,12},{8,0},{12,4},{1,9},{5,13},{9,1},{13,5},{2,10},{6,14},... | collective-permute-start | bytes 344072 | tf_op jit(solution)/shard_map/ppermute | solution.py:530
  39.9 11.6 %collective-permute-start.12 = (bf16[112,512]{1,0:T(8,128)(2,1)S(1)}, bf16[112,512]{1,0:T(8,128)(2,1)S(1)}, u32[]{:S(2)}, u32[]{:S(2)}) collective-permute-start(bf16[112,512]{1,0:T(8,128)(2,1)S(1)} %get-tuple-element.64), channel_id=1, source_target_pairs={{0,12},{4,8},{8,4},{12,0},{1,13},{5,9},{9,5},{13,1},{2,14},{6,10},... | collective-permute-start | bytes 344072 | tf_op jit(solution)/shard_map/ppermute | solution.py:530
  45.5 1.4 %collective-permute-start.8 = (bf16[96,512]{1,0:T(8,128)(2,1)S(1)}, bf16[96,512]{1,0:T(8,128)(2,1)S(1)}, u32[]{:S(2)}, u32[]{:S(2)}) collective-permute-start(bf16[96,512]{1,0:T(8,128)(2,1)S(1)} %get-tuple-element.68), channel_id=1, source_target_pairs={{0,1},{1,0},{2,3},{3,2},{4,5},{5,4},{6,7},{7,6},{8,9},{9,8},{10,11... | collective-permute-start | bytes 294920 | tf_op jit(solution)/shard_map/ppermute | solution.py:558
  45.6 1.4 %collective-permute-start.9 = (bf16[96,512]{1,0:T(8,128)(2,1)S(1)}, bf16[96,512]{1,0:T(8,128)(2,1)S(1)}, u32[]{:S(2)}, u32[]{:S(2)}) collective-permute-start(bf16[96,512]{1,0:T(8,128)(2,1)S(1)} %get-tuple-element.69), channel_id=1, source_target_pairs={{0,1},{1,0},{2,3},{3,2},{4,5},{5,4},{6,7},{7,6},{8,9},{9,8},{10,11... | collective-permute-start | bytes 294920 | tf_op jit(solution)/shard_map/ppermute | solution.py:558
  47.1 6.3 %collective-permute-start.14 = (bf16[96,512]{1,0:T(8,128)(2,1)S(1)}, bf16[96,512]{1,0:T(8,128)(2,1)S(1)}, u32[]{:S(2)}, u32[]{:S(2)}) collective-permute-start(bf16[96,512]{1,0:T(8,128)(2,1)S(1)} %get-tuple-element.74), channel_id=1, source_target_pairs={{0,4},{4,0},{8,12},{12,8},{1,5},{5,1},{9,13},{13,9},{2,6},{6,2},{1... | collective-permute-start | bytes 294920 | tf_op jit(solution)/shard_map/ppermute | solution.py:530
  47.2 10.9 %collective-permute-start.15 = (bf16[96,512]{1,0:T(8,128)(2,1)S(1)}, bf16[96,512]{1,0:T(8,128)(2,1)S(1)}, u32[]{:S(2)}, u32[]{:S(2)}) collective-permute-start(bf16[96,512]{1,0:T(8,128)(2,1)S(1)} %get-tuple-element.75), channel_id=1, source_target_pairs={{0,8},{4,12},{8,0},{12,4},{1,9},{5,13},{9,1},{13,5},{2,10},{6,14},... | collective-permute-start | bytes 294920 | tf_op jit(solution)/shard_map/ppermute | solution.py:530
  48.6 9.4 %collective-permute-start.16 = (bf16[96,512]{1,0:T(8,128)(2,1)S(1)}, bf16[96,512]{1,0:T(8,128)(2,1)S(1)}, u32[]{:S(2)}, u32[]{:S(2)}) collective-permute-start(bf16[96,512]{1,0:T(8,128)(2,1)S(1)} %get-tuple-element.76), channel_id=1, source_target_pairs={{0,12},{4,8},{8,4},{12,0},{1,13},{5,9},{9,5},{13,1},{2,14},{6,10},... | collective-permute-start | bytes 294920 | tf_op jit(solution)/shard_map/ppermute | solution.py:530
  52.2 6.2 %collective-permute-start.13 = (bf16[256,512]{1,0:T(8,128)(2,1)S(1)}, bf16[256,512]{1,0:T(8,128)(2,1)S(1)}, u32[]{:S(2)}, u32[]{:S(2)}) collective-permute-start(bf16[256,512]{1,0:T(8,128)(2,1)S(1)} %get-tuple-element.73), channel_id=1, source_target_pairs={{0,1},{1,0},{2,3},{3,2},{4,5},{5,4},{6,7},{7,6},{8,9},{9,8},{10,11... | collective-permute-start | bytes 786440 | tf_op jit(solution)/shard_map/ppermute | solution.py:581

commit v5 on v4

--- a/solution.py
+++ b/solution.py
@@ -18,6 +18,7 @@
 ANY = pl.BlockSpec(memory_space=pl.ANY)
 MIB = 1 << 20
 BUSY = 20 * 10**9
+EVEN_COST = 0
 KV_MIB = 53
 Q_MIB = 52
 FAR_MIB = 44
@@ -185,10 +186,7 @@
 
 
 def near_kernel(seg_ref, q_ref, *refs):
-    n = (len(refs) - 2) // 2
-    blocks, out_ref, copies, bias = refs[:n], refs[n], refs[n + 1:-1], refs[-1]
-    for copy, block in zip(copies, blocks, strict=True):
-        copy[...] = block[0:copy.shape[0], :]
+    blocks, out_ref, bias = refs[:-2], refs[-2], refs[-1]
     rows = q_ref.shape[1]
     seg = seg_ref[...].astype(F32)
     seg_col = column_of(seg)
@@ -197,6 +195,12 @@
     bias[0] = jnp.where((seg == seg_col) & (jj <= ii), 0.0, HIDE)
     back = [2 * i for i in range(len(blocks))]
     accumulate(q_ref, blocks, back, seg_col, jnp.min(seg), bias, out_ref, out_ref, True)
+
+
+def shorten_kernel(*refs):
+    n = len(refs) // 2
+    for short, block in zip(refs[n:], refs[:n], strict=True):
+        short[...] = block[0:short.shape[0], :]
 
 
 def middle_kernel(seg_ref, q_ref, *refs):
@@ -315,9 +319,10 @@
     moved = take(pos_ref[0:1, :], span * ctx, add_shares(shares))
     for k, out in enumerate(outs):
         out[0:span, :] = moved[k * span:(k + 1) * span]
-        out[mark:, :] = jnp.zeros((16, out.shape[1]), BF16)
+        out[mark:, :] = jnp.zeros((8, out.shape[1]), BF16)
         lanes = slots[k].shape[1]
-        out[mark:, 0:lanes] = jnp.concatenate([slots[k][...], pair_slots[8 * k:8 * k + 8, :]], 0).astype(BF16)
+        top = lax.broadcasted_iota(jnp.int32, (8, lanes), 0) < 4
+        out[mark:, 0:lanes] = jnp.where(top, slots[k][...], pair_slots[8 * k:8 * k + 8, :]).astype(BF16)
 
 
 def split_kernel(cap, pos_ref, *refs):
@@ -345,8 +350,8 @@
 
 
 def slot_lines(ref, at, span):
-    lines = ref[at:at + 16, 0:span].astype(F32).astype(jnp.int32)
-    return lines[0:1], lines[8:9]
+    lines = ref[at:at + 8, 0:span].astype(F32).astype(jnp.int32)
+    return lines[0:1], lines[4:5]
 
 
 def put(slot, block, count):
@@ -453,20 +458,31 @@
     )
     hop[1] = after(hop[1], queries)
     for i in range(1, hops):
-        hop.append(lax.ppermute(hop[i], "ctx", up))
+        hop.append(lax.ppermute(hop[i], "ctx", [(j, j + 1) for j in range(i, ctx - 1)]))
+
+    short = sds((rows + 8, 2 * kv_cols), BF16)
+    short_hop = pl.pallas_call(
+        shorten_kernel,
+        in_specs=[VMEM] * hops,
+        out_specs=[VMEM] * hops,
+        out_shape=[short] * hops,
+        compiler_params=params(8),
+        cost_estimate=cost(0, 0),
+        name="shorten",
+    )(*hop[:hops])
+    pair = [lax.ppermute(x, "rep", swap) for x in short_hop]
 
     work = heads * rows * rows
-    short = sds((rows + 8, 2 * kv_cols), BF16)
-    near, *short_hop = pl.pallas_call(
+    near = pl.pallas_call(
         near_kernel,
         in_specs=[VMEM] * (2 + hops),
-        out_specs=[VMEM] * (1 + hops),
-        out_shape=[sds((heads, rows, 2 * HD), F32)] + [short] * hops,
+        out_specs=VMEM,
+        out_shape=sds((heads, rows, 2 * HD), F32),
         scratch_shapes=[pltpu.VMEM((hops, rows, rows), F32)],
         compiler_params=params(12),
-        cost_estimate=cost(4 * work * HD * hops, 8 * MIB, work * hops),
+        cost_estimate=cost(EVEN_COST, 0),
         name="even_attention",
-    )(seg_row, queries, *hop[:hops])
+    )(after(seg_row, *short_hop), queries, *hop[:hops])
 
     buffer_pos, pair_slots, *slots = route(after(dest_rows.reshape(1, rows), near))
     pair_slots = lax.ppermute(pair_slots, "rep", swap)
@@ -481,7 +497,7 @@
         compiler_params=params(12),
         cost_estimate=cost(0, 0),
         name="odd_attention",
-    )(after(seg_row, pair_slots), queries, *pair, near)
+    )(after(seg_row, buffer_pos), queries, *pair, near)
     hop[hops] = after(hop[hops], near)
     pair.append(lax.ppermute(hop[hops], "rep", swap))
 
@@ -496,7 +512,7 @@
         compiler_params=params(FAR_MIB),
         cost_estimate=cost(8 * work * HD + 2 * rows * heads * HD * chunks[0], 10 * MIB, 2 * work),
         name="far_attention_project",
-    )(seg_row, queries, hop[hops], pair[hops - 1], pair[hops], near, w_out)
+    )(after(seg_row, pair_slots), queries, hop[hops], pair[hops - 1], pair[hops], near, w_out)
 
     def project_some(x, steps, sizes):
         return pl.pallas_call(
@@ -535,7 +551,7 @@
         functools.partial(pick_kernel, ctx, span, mark),
         in_specs=[VMEM] * (2 + ctx + n_head),
         out_specs=[VMEM] * ctx,
-        out_shape=[sds((mark + 16, n), BF16)] * ctx,
+        out_shape=[sds((mark + 8, n), BF16)] * ctx,
         compiler_params=params(8),
         cost_estimate=cost(0, 0),
         name="add_pick",

time: 59.5 us -> 58.5 us (0.983)
  waiting for transfers between devices: 22.3 us -> 16.2 us
  starting transfers between devices: 15.5 us -> 20.4 us
    ppermute x1, waiting for transfers between devices: 5.83 us -> 0.01 us  [local(): lax.ppermute(hop[i], 'ctx', [(j, j + 1) for j in range(i, ctx - 1)])]
    ppermute x6, starting transfers between devices: 8.9 us -> 11.3 us  [across(): lax.ppermute(xs[k], 'ctx', [(i, i ^ k) for i in range(ctx)])]
    ppermute x1, starting transfers between devices: 0.01 us -> 1.91 us  [local(): pair.append(lax.ppermute(hop[hops], 'rep', swap))]
    ppermute x1, waiting for transfers between devices: 1.56 us -> 0.01 us  [local(): pair.append(lax.ppermute(hop[hops], 'rep', swap))]
    ppermute x6, waiting for transfers between devices: 5.7 us -> 7.02 us  [across(): lax.ppermute(xs[k], 'ctx', [(i, i ^ k) for i in range(ctx)])]
    ppermute x1, starting transfers between devices: 0.01 us -> 0.67 us  [local(): lax.ppermute(hop[i], 'ctx', [(j, j + 1) for j in range(i, ctx - 1)])]
    pallas_call x1 -> x2, Pallas kernels: 1.52 us -> 1.58 us  [the longest x1 1.54 us: local(): pl.pallas_call(near_kernel, in_specs=[VMEM] * (2 + hops), out_specs=VMEM,...]
  transfers between devices with their start and end apart: 17 -> 17, of which waited for: 9 -> 7; matrix products, arithmetic and copies ran while one was open for 0% -> 0% of each run, Pallas kernels for 25% -> 25%
where the time goes in v5:
time: 58.5 us; the launch traced here: 58.3 us
  Pallas kernels  20.6 us (35%)
  starting transfers between devices  20.4 us (35%)
  waiting for transfers between devices  16.2 us (28%)
  local copies, waits for them, and re-layouts  0.76 us (1%)
    ppermute x6, starting transfers between devices, across(): lax.ppermute(xs[k], 'ctx', [(i, i ^ k) for i in range(ctx)])  11.3 us
    ppermute x6, waiting for transfers between devices, across(): lax.ppermute(xs[k], 'ctx', [(i, i ^ k) for i in range(ctx)])  7.02 us
    pallas_call x1, Pallas kernels, local(): pl.pallas_call(functools.partial(q_kernel, parts), in_specs=[ANY, ANY, VM...  5.52 us
    pallas_call x2, Pallas kernels, project_some(): pl.pallas_call(functools.partial(project_kernel, steps), in_specs=[VMEM,...  5.36 us
    ppermute x2, waiting for transfers between devices, to_heads(): lax.ppermute(x, 'head', flip)  3.98 us
    ppermute x1, waiting for transfers between devices, local(): hop = [own, lax.ppermute(own, 'ctx', up)]  3.16 us
    ppermute x1, starting transfers between devices, local(): hop = [own, lax.ppermute(own, 'ctx', up)]  3.08 us
    pallas_call x1, Pallas kernels, local(): pl.pallas_call(functools.partial(kv_kernel, parts), in_specs=[ANY, ANY, A...  2.81 us
  transfers between devices with their start and end apart: 17, of which 7 were waited for; matrix products, arithmetic and copies ran while one was open for 0% of the time, Pallas kernels for 25%

profile of v5, /device:TPU:0, one launch (start us, length us, event | category | flops | bytes accessed | tf_op | source)
XLA Modules:
  0.0 58.3 jit_solution(2785252502127062658)
XLA Ops:
  0.0 0.7 %copy-done = s32[256]{0:T(256)S(1)} copy-done((s32[256]{0:T(256)S(1)}, s32[256]{0:T(256)}, u32[]{:S(2)}) %copy-start) | copy-done | bytes 1048
  0.8 2.8 %keys_values.1 = (bf16[272,512]{1,0:T(8,128)(2,1)S(1)}, f32[256,256]{1,0:T(8,128)S(1)}) custom-call(bf16[256,2048]{1,0:T(8,128)(2,1)} %x_hbm.3, bf16[2048,256]{1,0:T(8,128)(2,1)} %wk_hbm.1, bf16[2048,256]{1,0:T(8,128)(2,1)} %wv_hbm.1, s32[1,256]{1,0:T(1,128)S(1)} %bitcast.2), custom_call_target="tpu_custom_call" | custom-call | flops 536870912 | bytes 3145728 | tf_op jit(solution)/shard_map/keys_values/pallas_call | solution.py:421
  3.6 3.1 %collective-permute-start = (bf16[272,512]{1,0:T(8,128)(2,1)S(1)}, bf16[272,512]{1,0:T(8,128)(2,1)S(1)}, u32[]{:S(2)}, u32[]{:S(2)}) collective-permute-start(bf16[272,512]{1,0:T(8,128)(2,1)S(1)} %get-tuple-element.42.refs_0_), channel_id=1, source_target_pairs={{0,4},{4,8},{8,12},{12,0},{1,5},{5,9},{9,13},{13,1},{2,6},{6,10},{... | collective-permute-start | bytes 835592 | tf_op jit(solution)/shard_map/ppermute | solution.py:436
  6.7 5.5 %queries.1.q_ref = bf16[16,256,128]{2,1,0:T(8,128)(2,1)S(1)} custom-call(bf16[256,2048]{1,0:T(8,128)(2,1)} %x_hbm.3, bf16[2048,2048]{1,0:T(8,128)(2,1)} %w_hbm.4, f32[256,256]{1,0:T(8,128)S(1)} %get-tuple-element.43.tab_ref), custom_call_target="tpu_custom_call" | custom-call | flops 2147483648 | bytes 9437184 | tf_op jit(solution)/shard_map/queries/pallas_call | solution.py:439
  12.2 3.2 %collective-permute-done.refs_1_ = bf16[272,512]{1,0:T(8,128)(2,1)S(1)} collective-permute-done((bf16[272,512]{1,0:T(8,128)(2,1)S(1)}, bf16[272,512]{1,0:T(8,128)(2,1)S(1)}, u32[]{:S(2)}, u32[]{:S(2)}) %collective-permute-start) | collective-permute-done | bytes 278560 | tf_op jit(solution)/shard_map/ppermute | solution.py:436
  15.3 0.7 %collective-permute-start.2 = (bf16[272,512]{1,0:T(8,128)(2,1)S(1)}, bf16[272,512]{1,0:T(8,128)(2,1)S(1)}, u32[]{:S(2)}, u32[]{:S(2)}) collective-permute-start(bf16[272,512]{1,0:T(8,128)(2,1)S(1)} %collective-permute-done.refs_1_), channel_id=1, source_target_pairs={{4,8},{8,12},{5,9},{9,13},{6,10},{10,14},{7,11},{11,15},{20,24},{2... | collective-permute-start | bytes 835592 | tf_op jit(solution)/shard_map/ppermute | solution.py:461
  16.1 0.5 collective-permute-start.4
  16.6 1.5 %even_attention.1.refs_2_ = f32[16,256,256]{2,1,0:T(8,128)S(1)} custom-call(s32[1,256]{1,0:T(1,128)S(1)} %bitcast.3, bf16[16,256,128]{2,1,0:T(8,128)(2,1)S(1)} %queries.1.q_ref, bf16[272,512]{1,0:T(8,128)(2,1)S(1)} %get-tuple-element.42.refs_0_, bf16[272,512]{1,0:T(8,128)(2,1)S(1)} %collective-permute-done.refs_1_), custom_call_target="tpu_custom_call" | custom-call | tf_op jit(solution)/shard_map/even_attention/pallas_call | solution.py:476
  18.2 0.3 routes.1
  18.5 0.2 odd_attention.1.near_ref
  18.7 1.9 %collective-permute-start.5 = (bf16[272,512]{1,0:T(8,128)(2,1)S(1)}, bf16[272,512]{1,0:T(8,128)(2,1)S(1)}, u32[]{:S(2)}, u32[]{:S(2)}) collective-permute-start(bf16[272,512]{1,0:T(8,128)(2,1)S(1)} %collective-permute-done.2.far_ref), channel_id=1, source_target_pairs={{0,1},{1,0},{2,3},{3,2},{4,5},{5,4},{6,7},{7,6},{8,9},{9,8},{10,11... | collective-permute-start | bytes 835592 | tf_op jit(solution)/shard_map/ppermute | solution.py:502
  20.7 1.1 %collective-permute-done.1.pair_slots = f32[32,128]{1,0:T(8,128)S(1)} collective-permute-done((f32[32,128]{1,0:T(8,128)S(1)}, f32[32,128]{1,0:T(8,128)S(1)}, u32[]{:S(2)}, u32[]{:S(2)}) %collective-permute-start.1) | collective-permute-done | bytes 16416 | tf_op jit(solution)/shard_map/ppermute | solution.py:488
  21.8 2.3 %far_attention_project.1 = (bf16[256,2048]{1,0:T(8,128)(2,1)S(1)}, bf16[256,512]{1,0:T(8,128)(2,1)S(1)}) custom-call(s32[1,256]{1,0:T(1,128)S(1)} %bitcast.5, bf16[16,256,128]{2,1,0:T(8,128)(2,1)S(1)} %queries.1.q_ref, bf16[272,512]{1,0:T(8,128)(2,1)S(1)} %collective-permute-done.2.far_ref, bf16[264,512]{1,0:T(8,128)(2,1)S(1)} %collective-permute-done.4.refs_1_.to_one, ...), custom_call_target="tpu_custom_call" | custom-call | flops 1610612736 | bytes 10485760 | tf_op jit(solution)/shard_map/far_attention_project/pallas_call | solution.py:505
  24.1 1.6 %collective-permute-start.6 = (bf16[256,512]{1,0:T(8,128)(2,1)S(1)}, bf16[256,512]{1,0:T(8,128)(2,1)S(1)}, u32[]{:S(2)}, u32[]{:S(2)}) collective-permute-start(bf16[256,512]{1,0:T(8,128)(2,1)S(1)} %get-tuple-element.62), channel_id=1, source_target_pairs={{0,2},{2,0},{1,3},{3,1},{4,6},{6,4},{5,7},{7,5},{8,10},{10,8},{9,1... | collective-permute-start | bytes 786440 | tf_op jit(solution)/shard_map/ppermute | solution.py:532
  25.7 3.1 %project.2 = (bf16[256,512]{1,0:T(8,128)(2,1)S(1)}, bf16[256,512]{1,0:T(8,128)(2,1)S(1)}) custom-call(bf16[256,2048]{1,0:T(8,128)(2,1)S(1)} %get-tuple-element.68.att_ref, bf16[2048,2048]{1,0:T(8,128)(2,1)} %w_hbm.7), custom_call_target="tpu_custom_call" | custom-call | flops 20000000000 | tf_op jit(solution)/shard_map/project/pallas_call | solution.py:518
  28.8 0.6 %collective-permute-start.7 = (bf16[256,512]{1,0:T(8,128)(2,1)S(1)}, bf16[256,512]{1,0:T(8,128)(2,1)S(1)}, u32[]{:S(2)}, u32[]{:S(2)}) collective-permute-start(bf16[256,512]{1,0:T(8,128)(2,1)S(1)} %get-tuple-element.55), channel_id=1, source_target_pairs={{0,2},{2,0},{1,3},{3,1},{4,6},{6,4},{5,7},{7,5},{8,10},{10,8},{9,1... | collective-permute-start | bytes 786440 | tf_op jit(solution)/shard_map/ppermute | solution.py:532
  29.4 4.0 %collective-permute-done.6.refs_5_ = bf16[256,512]{1,0:T(8,128)(2,1)S(1)} collective-permute-done((bf16[256,512]{1,0:T(8,128)(2,1)S(1)}, bf16[256,512]{1,0:T(8,128)(2,1)S(1)}, u32[]{:S(2)}, u32[]{:S(2)}) %collective-permute-start.6) | collective-permute-done | bytes 262176 | tf_op jit(solution)/shard_map/ppermute | solution.py:532
  33.3 0.3 add_pick.1
  33.6 4.1 %collective-permute-start.10 = (bf16[104,512]{1,0:T(8,128)(2,1)S(1)}, bf16[104,512]{1,0:T(8,128)(2,1)S(1)}, u32[]{:S(2)}, u32[]{:S(2)}) collective-permute-start(bf16[104,512]{1,0:T(8,128)(2,1)S(1)} %get-tuple-element.64), channel_id=1, source_target_pairs={{0,4},{4,0},{8,12},{12,8},{1,5},{5,1},{9,13},{13,9},{2,6},{6,2},{1... | collective-permute-start | bytes 319496 | tf_op jit(solution)/shard_map/ppermute | solution.py:546
  37.7 2.8 %collective-permute-start.11 = (bf16[104,512]{1,0:T(8,128)(2,1)S(1)}, bf16[104,512]{1,0:T(8,128)(2,1)S(1)}, u32[]{:S(2)}, u32[]{:S(2)}) collective-permute-start(bf16[104,512]{1,0:T(8,128)(2,1)S(1)} %get-tuple-element.65), channel_id=1, source_target_pairs={{0,8},{4,12},{8,0},{12,4},{1,9},{5,13},{9,1},{13,5},{2,10},{6,14},... | collective-permute-start | bytes 319496 | tf_op jit(solution)/shard_map/ppermute | solution.py:546
  40.5 2.3 %project.3.refs_0_ = bf16[256,512]{1,0:T(8,128)(2,1)S(1)} custom-call(bf16[256,2048]{1,0:T(8,128)(2,1)S(1)} %get-tuple-element.68.att_ref, bf16[2048,2048]{1,0:T(8,128)(2,1)} %w_hbm.7), custom_call_target="tpu_custom_call" | custom-call | flops 20000000000 | tf_op jit(solution)/shard_map/project/pallas_call | solution.py:518
  42.8 0.3 add_split.1
  43.2 0.5 collective-permute-start.9
  43.7 0.8 %collective-permute-done.8.refs_0_ = bf16[96,512]{1,0:T(8,128)(2,1)S(1)} collective-permute-done((bf16[96,512]{1,0:T(8,128)(2,1)S(1)}, bf16[96,512]{1,0:T(8,128)(2,1)S(1)}, u32[]{:S(2)}, u32[]{:S(2)}) %collective-permute-start.8) | collective-permute-done | bytes 98336 | tf_op jit(solution)/shard_map/ppermute | solution.py:574
  44.5 0.2 collective-permute-done.9.refs_1_
  44.7 0.8 %collective-permute-start.14 = (bf16[96,512]{1,0:T(8,128)(2,1)S(1)}, bf16[96,512]{1,0:T(8,128)(2,1)S(1)}, u32[]{:S(2)}, u32[]{:S(2)}) collective-permute-start(bf16[96,512]{1,0:T(8,128)(2,1)S(1)} %get-tuple-element.76), channel_id=1, source_target_pairs={{0,4},{4,0},{8,12},{12,8},{1,5},{5,1},{9,13},{13,9},{2,6},{6,2},{1... | collective-permute-start | bytes 294920 | tf_op jit(solution)/shard_map/ppermute | solution.py:546
  45.5 3.7 %collective-permute-start.15 = (bf16[96,512]{1,0:T(8,128)(2,1)S(1)}, bf16[96,512]{1,0:T(8,128)(2,1)S(1)}, u32[]{:S(2)}, u32[]{:S(2)}) collective-permute-start(bf16[96,512]{1,0:T(8,128)(2,1)S(1)} %get-tuple-element.77), channel_id=1, source_target_pairs={{0,8},{4,12},{8,0},{12,4},{1,9},{5,13},{9,1},{13,5},{2,10},{6,14},... | collective-permute-start | bytes 294920 | tf_op jit(solution)/shard_map/ppermute | solution.py:546
  49.2 0.7 %place.1 = (bf16[256,512]{1,0:T(8,128)(2,1)S(1)}, bf16[256,512]{1,0:T(8,128)(2,1)S(1)}) custom-call(bf16[104,512]{1,0:T(8,128)(2,1)S(1)} %get-tuple-element.73.refs_0_, bf16[104,512]{1,0:T(8,128)(2,1)S(1)} %collective-permute-done.10.refs_1_, bf16[104,512]{1,0:T(8,128)(2,1)S(1)} %collective-permute-done.11.refs_2_, ...), custom_call_target="tpu_custom_call" | custom-call | flops 20000000000 | tf_op jit(solution)/shard_map/place/pallas_call | solution.py:588
  50.0 0.1 collective-permute-done.14.refs_5_
  50.0 6.9 %collective-permute-done.15.refs_6_ = bf16[96,512]{1,0:T(8,128)(2,1)S(1)} collective-permute-done((bf16[96,512]{1,0:T(8,128)(2,1)S(1)}, bf16[96,512]{1,0:T(8,128)(2,1)S(1)}, u32[]{:S(2)}, u32[]{:S(2)}) %collective-permute-start.15) | collective-permute-done | bytes 98336 | tf_op jit(solution)/shard_map/ppermute | solution.py:546
  57.0 0.4 place_rest.1.rest_ref
  57.4 0.9 %join.1 = bf16[256,1024]{1,0:T(8,128)(2,1)} custom-call(bf16[256,512]{1,0:T(8,128)(2,1)S(1)} %get-tuple-element.74.mine_ref, bf16[256,512]{1,0:T(8,128)(2,1)S(1)} %collective-permute-done.13.pair_ref, bf16[256,512]{1,0:T(8,128)(2,1)S(1)} %place_rest.1.rest_ref), custom_call_target="tpu_custom_call" | custom-call | tf_op jit(solution)/shard_map/join/pallas_call | solution.py:609
  (23 shorter events, 0.4 us)
Async XLA Ops:
  0.0 16.6 %copy-start.1 = (s32[256]{0:T(256)S(1)}, s32[256]{0:T(256)}, u32[]{:S(2)}) copy-start(s32[256]{0:T(256)} %param.8) | copy-start | bytes 3076
  0.0 0.8 %copy-start = (s32[256]{0:T(256)S(1)}, s32[256]{0:T(256)}, u32[]{:S(2)}) copy-start(s32[256]{0:T(256)} %param.8) | copy-start | bytes 3076
  3.6 11.8 %collective-permute-start = (bf16[272,512]{1,0:T(8,128)(2,1)S(1)}, bf16[272,512]{1,0:T(8,128)(2,1)S(1)}, u32[]{:S(2)}, u32[]{:S(2)}) collective-permute-start(bf16[272,512]{1,0:T(8,128)(2,1)S(1)} %get-tuple-element.42.refs_0_), channel_id=1, source_target_pairs={{0,4},{4,8},{8,12},{12,0},{1,5},{5,9},{9,13},{13,1},{2,6},{6,10},{... | collective-permute-start | bytes 835592 | tf_op jit(solution)/shard_map/ppermute | solution.py:436
  6.7 11.5 %copy-start.2 = (s32[256]{0:T(256)S(1)}, s32[256]{0:T(256)}, u32[]{:S(2)}) copy-start(s32[256]{0:T(256)} %param.9) | copy-start | bytes 3076
  15.3 3.3 %collective-permute-start.2 = (bf16[272,512]{1,0:T(8,128)(2,1)S(1)}, bf16[272,512]{1,0:T(8,128)(2,1)S(1)}, u32[]{:S(2)}, u32[]{:S(2)}) collective-permute-start(bf16[272,512]{1,0:T(8,128)(2,1)S(1)} %collective-permute-done.refs_1_), channel_id=1, source_target_pairs={{4,8},{8,12},{5,9},{9,13},{6,10},{10,14},{7,11},{11,15},{20,24},{2... | collective-permute-start | bytes 835592 | tf_op jit(solution)/shard_map/ppermute | solution.py:461
  16.1 2.4 %collective-permute-start.3 = (bf16[264,512]{1,0:T(8,128)(2,1)S(1)}, bf16[264,512]{1,0:T(8,128)(2,1)S(1)}, u32[]{:S(2)}, u32[]{:S(2)}) collective-permute-start(bf16[264,512]{1,0:T(8,128)(2,1)S(1)} %get-tuple-element.45), channel_id=1, source_target_pairs={{0,1},{1,0},{2,3},{3,2},{4,5},{5,4},{6,7},{7,6},{8,9},{9,8},{10,11... | collective-permute-start | bytes 811016 | tf_op jit(solution)/shard_map/ppermute | solution.py:489
  16.1 2.4 %collective-permute-start.4 = (bf16[264,512]{1,0:T(8,128)(2,1)S(1)}, bf16[264,512]{1,0:T(8,128)(2,1)S(1)}, u32[]{:S(2)}, u32[]{:S(2)}) collective-permute-start(bf16[264,512]{1,0:T(8,128)(2,1)S(1)} %get-tuple-element.46), channel_id=1, source_target_pairs={{0,1},{1,0},{2,3},{3,2},{4,5},{5,4},{6,7},{7,6},{8,9},{9,8},{10,11... | collective-permute-start | bytes 811016 | tf_op jit(solution)/shard_map/ppermute | solution.py:489
  18.7 3.1 %collective-permute-start.5 = (bf16[272,512]{1,0:T(8,128)(2,1)S(1)}, bf16[272,512]{1,0:T(8,128)(2,1)S(1)}, u32[]{:S(2)}, u32[]{:S(2)}) collective-permute-start(bf16[272,512]{1,0:T(8,128)(2,1)S(1)} %collective-permute-done.2.far_ref), channel_id=1, source_target_pairs={{0,1},{1,0},{2,3},{3,2},{4,5},{5,4},{6,7},{7,6},{8,9},{9,8},{10,11... | collective-permute-start | bytes 835592 | tf_op jit(solution)/shard_map/ppermute | solution.py:502
  20.6 1.2 %collective-permute-start.1 = (f32[32,128]{1,0:T(8,128)S(1)}, f32[32,128]{1,0:T(8,128)S(1)}, u32[]{:S(2)}, u32[]{:S(2)}) collective-permute-start(f32[32,128]{1,0:T(8,128)S(1)} %get-tuple-element.50), channel_id=1, source_target_pairs={{0,1},{1,0},{2,3},{3,2},{4,5},{5,4},{6,7},{7,6},{8,9},{9,8},{10,11... | collective-permute-start | bytes 49160 | tf_op jit(solution)/shard_map/ppermute | solution.py:488
  24.1 9.2 %collective-permute-start.6 = (bf16[256,512]{1,0:T(8,128)(2,1)S(1)}, bf16[256,512]{1,0:T(8,128)(2,1)S(1)}, u32[]{:S(2)}, u32[]{:S(2)}) collective-permute-start(bf16[256,512]{1,0:T(8,128)(2,1)S(1)} %get-tuple-element.62), channel_id=1, source_target_pairs={{0,2},{2,0},{1,3},{3,1},{4,6},{6,4},{5,7},{7,5},{8,10},{10,8},{9,1... | collective-permute-start | bytes 786440 | tf_op jit(solution)/shard_map/ppermute | solution.py:532
  28.8 14.0 %collective-permute-start.7 = (bf16[256,512]{1,0:T(8,128)(2,1)S(1)}, bf16[256,512]{1,0:T(8,128)(2,1)S(1)}, u32[]{:S(2)}, u32[]{:S(2)}) collective-permute-start(bf16[256,512]{1,0:T(8,128)(2,1)S(1)} %get-tuple-element.55), channel_id=1, source_target_pairs={{0,2},{2,0},{1,3},{3,1},{4,6},{6,4},{5,7},{7,5},{8,10},{10,8},{9,1... | collective-permute-start | bytes 786440 | tf_op jit(solution)/shard_map/ppermute | solution.py:532
  33.6 15.5 %collective-permute-start.10 = (bf16[104,512]{1,0:T(8,128)(2,1)S(1)}, bf16[104,512]{1,0:T(8,128)(2,1)S(1)}, u32[]{:S(2)}, u32[]{:S(2)}) collective-permute-start(bf16[104,512]{1,0:T(8,128)(2,1)S(1)} %get-tuple-element.64), channel_id=1, source_target_pairs={{0,4},{4,0},{8,12},{12,8},{1,5},{5,1},{9,13},{13,9},{2,6},{6,2},{1... | collective-permute-start | bytes 319496 | tf_op jit(solution)/shard_map/ppermute | solution.py:546
  37.7 11.5 %collective-permute-start.11 = (bf16[104,512]{1,0:T(8,128)(2,1)S(1)}, bf16[104,512]{1,0:T(8,128)(2,1)S(1)}, u32[]{:S(2)}, u32[]{:S(2)}) collective-permute-start(bf16[104,512]{1,0:T(8,128)(2,1)S(1)} %get-tuple-element.65), channel_id=1, source_target_pairs={{0,8},{4,12},{8,0},{12,4},{1,9},{5,13},{9,1},{13,5},{2,10},{6,14},... | collective-permute-start | bytes 319496 | tf_op jit(solution)/shard_map/ppermute | solution.py:546
  40.5 8.7 %collective-permute-start.12 = (bf16[104,512]{1,0:T(8,128)(2,1)S(1)}, bf16[104,512]{1,0:T(8,128)(2,1)S(1)}, u32[]{:S(2)}, u32[]{:S(2)}) collective-permute-start(bf16[104,512]{1,0:T(8,128)(2,1)S(1)} %get-tuple-element.66), channel_id=1, source_target_pairs={{0,12},{4,8},{8,4},{12,0},{1,13},{5,9},{9,5},{13,1},{2,14},{6,10},... | collective-permute-start | bytes 319496 | tf_op jit(solution)/shard_map/ppermute | solution.py:546
  43.1 1.4 %collective-permute-start.8 = (bf16[96,512]{1,0:T(8,128)(2,1)S(1)}, bf16[96,512]{1,0:T(8,128)(2,1)S(1)}, u32[]{:S(2)}, u32[]{:S(2)}) collective-permute-start(bf16[96,512]{1,0:T(8,128)(2,1)S(1)} %get-tuple-element.70), channel_id=1, source_target_pairs={{0,1},{1,0},{2,3},{3,2},{4,5},{5,4},{6,7},{7,6},{8,9},{9,8},{10,11... | collective-permute-start | bytes 294920 | tf_op jit(solution)/shard_map/ppermute | solution.py:574
  43.2 1.4 %collective-permute-start.9 = (bf16[96,512]{1,0:T(8,128)(2,1)S(1)}, bf16[96,512]{1,0:T(8,128)(2,1)S(1)}, u32[]{:S(2)}, u32[]{:S(2)}) collective-permute-start(bf16[96,512]{1,0:T(8,128)(2,1)S(1)} %get-tuple-element.71), channel_id=1, source_target_pairs={{0,1},{1,0},{2,3},{3,2},{4,5},{5,4},{6,7},{7,6},{8,9},{9,8},{10,11... | collective-permute-start | bytes 294920 | tf_op jit(solution)/shard_map/ppermute | solution.py:574
  44.7 5.3 %collective-permute-start.14 = (bf16[96,512]{1,0:T(8,128)(2,1)S(1)}, bf16[96,512]{1,0:T(8,128)(2,1)S(1)}, u32[]{:S(2)}, u32[]{:S(2)}) collective-permute-start(bf16[96,512]{1,0:T(8,128)(2,1)S(1)} %get-tuple-element.76), channel_id=1, source_target_pairs={{0,4},{4,0},{8,12},{12,8},{1,5},{5,1},{9,13},{13,9},{2,6},{6,2},{1... | collective-permute-start | bytes 294920 | tf_op jit(solution)/shard_map/ppermute | solution.py:546
  45.5 11.5 %collective-permute-start.15 = (bf16[96,512]{1,0:T(8,128)(2,1)S(1)}, bf16[96,512]{1,0:T(8,128)(2,1)S(1)}, u32[]{:S(2)}, u32[]{:S(2)}) collective-permute-start(bf16[96,512]{1,0:T(8,128)(2,1)S(1)} %get-tuple-element.77), channel_id=1, source_target_pairs={{0,8},{4,12},{8,0},{12,4},{1,9},{5,13},{9,1},{13,5},{2,10},{6,14},... | collective-permute-start | bytes 294920 | tf_op jit(solution)/shard_map/ppermute | solution.py:546
  49.2 7.8 %collective-permute-start.16 = (bf16[96,512]{1,0:T(8,128)(2,1)S(1)}, bf16[96,512]{1,0:T(8,128)(2,1)S(1)}, u32[]{:S(2)}, u32[]{:S(2)}) collective-permute-start(bf16[96,512]{1,0:T(8,128)(2,1)S(1)} %get-tuple-element.78), channel_id=1, source_target_pairs={{0,12},{4,8},{8,4},{12,0},{1,13},{5,9},{9,5},{13,1},{2,14},{6,10},... | collective-permute-start | bytes 294920 | tf_op jit(solution)/shard_map/ppermute | solution.py:546
  49.9 7.5 %collective-permute-start.13 = (bf16[256,512]{1,0:T(8,128)(2,1)S(1)}, bf16[256,512]{1,0:T(8,128)(2,1)S(1)}, u32[]{:S(2)}, u32[]{:S(2)}) collective-permute-start(bf16[256,512]{1,0:T(8,128)(2,1)S(1)} %get-tuple-element.75), channel_id=1, source_target_pairs={{0,1},{1,0},{2,3},{3,2},{4,5},{5,4},{6,7},{7,6},{8,9},{9,8},{10,11... | collective-permute-start | bytes 786440 | tf_op jit(solution)/shard_map/ppermute | solution.py:597

commit v6 on v5

--- a/solution.py
+++ b/solution.py
@@ -47,7 +47,7 @@
     return ((heads * cosine + turned * sine) * scale).astype(BF16)
 
 
-def kv_kernel(parts, x_hbm, wk_hbm, wv_hbm, seg_ref, kv_ref, tab_ref, x_buf, w_buf, sem):
+def kv_kernel(parts, x_hbm, wk_hbm, wv_hbm, seg_hbm, kv_ref, tab_ref, x_buf, w_buf, seg_ref, sem):
     rows, width = x_buf.shape
     kv_cols = w_buf.shape[1] // 2
     depth = width // parts
@@ -61,6 +61,8 @@
         ])
         for copy in copies[-1]:
             copy.start()
+    docs = pltpu.make_async_copy(seg_hbm, seg_ref, sem.at[3 * parts])
+    docs.start()
     first = (lax.axis_index("ctx") * 2 + lax.axis_index("rep")) * rows
     lane = lax.broadcasted_iota(jnp.int32, (1, HD), 1)
     freq = jnp.exp(lax.rem(lane, HD // 2).astype(F32) * (-2.0 * math.log(THETA) / HD))
@@ -68,6 +70,7 @@
     angle = pos * freq
     tab_ref[:, :HD] = jnp.cos(angle)
     tab_ref[:, HD:] = jnp.where(lane < HD // 2, -1.0, 1.0) * jnp.sin(angle)
+    docs.wait()
     line = lax.broadcasted_iota(jnp.int32, (16, kv_cols), 0)
     segs = jnp.zeros((16, kv_cols), F32)
     for i in range(rows // kv_cols):
@@ -420,18 +423,19 @@
     payload = sds((rows + 16, 2 * kv_cols), BF16)
     own, table = pl.pallas_call(
         functools.partial(kv_kernel, parts),
-        in_specs=[ANY, ANY, ANY, VMEM],
+        in_specs=[ANY, ANY, ANY, pl.BlockSpec(memory_space=pltpu.HBM)],
         out_specs=[VMEM] * 2,
         out_shape=[payload, sds((rows, 2 * HD), F32)],
         scratch_shapes=[
             pltpu.VMEM((rows, width), BF16),
             pltpu.VMEM((width, 2 * kv_cols), BF16),
-            pltpu.SemaphoreType.DMA((3 * parts,)),
+            pltpu.VMEM((1, rows), jnp.int32),
+            pltpu.SemaphoreType.DMA((3 * parts + 1,)),
         ],
         compiler_params=params(KV_MIB),
         cost_estimate=cost(4 * rows * width * kv_cols, 2 * width * (rows + 2 * kv_cols)),
         name="keys_values",
-    )(tokens, w_key, w_value, seg_row)
+    )(tokens, w_key, w_value, pltpu.with_memory_space_constraint(seg_row, pltpu.HBM))
 
     hop = [own, lax.ppermute(own, "ctx", up)]
 
@@ -456,9 +460,10 @@
         cost_estimate=cost(0, 0),
         name="routes",
     )
-    hop[1] = after(hop[1], queries)
+    buffer_pos, pair_slots, *slots = route(after(dest_rows.reshape(1, rows), queries))
+    hop[1] = after(hop[1], queries, buffer_pos)
     for i in range(1, hops):
-        hop.append(lax.ppermute(hop[i], "ctx", [(j, j + 1) for j in range(i, ctx - 1)]))
+        hop.append(lax.ppermute(hop[i], "ctx", [(j, j) for j in range(i)] + [(j, j + 1) for j in range(i, ctx - 1)] + [(ctx - 1, i)]))
 
     short = sds((rows + 8, 2 * kv_cols), BF16)
     short_hop = pl.pallas_call(
@@ -484,7 +489,6 @@
         name="even_attention",
     )(after(seg_row, *short_hop), queries, *hop[:hops])
 
-    buffer_pos, pair_slots, *slots = route(after(dest_rows.reshape(1, rows), near))
     pair_slots = lax.ppermute(pair_slots, "rep", swap)
     pair = [lax.ppermute(x, "rep", swap) for x in short_hop]
     near = pl.pallas_call(
@@ -497,7 +501,7 @@
         compiler_params=params(12),
         cost_estimate=cost(0, 0),
         name="odd_attention",
-    )(after(seg_row, buffer_pos), queries, *pair, near)
+    )(seg_row, queries, *pair, near)
     hop[hops] = after(hop[hops], near)
     pair.append(lax.ppermute(hop[hops], "rep", swap))
 

time: 58.5 us -> 58.5 us (level)
  starting transfers between devices: 20.4 us -> 21.5 us
  local copies, waits for them, and re-layouts: 0.76 us -> 0.01 us
    ppermute x6, starting transfers between devices: 11.3 us -> 12.4 us  [across(): lax.ppermute(xs[k], 'ctx', [(i, i ^ k) for i in range(ctx)])]
    unnamed x6 -> x4, local copies, waits for them, and re-layouts: 0.76 us -> 0.01 us
where the time goes in v6:
time: 58.5 us; the launch traced here: 58.3 us
  starting transfers between devices  21.5 us (37%)
  Pallas kernels  20.9 us (36%)
  waiting for transfers between devices  15.7 us (27%)
    ppermute x6, starting transfers between devices, across(): lax.ppermute(xs[k], 'ctx', [(i, i ^ k) for i in range(ctx)])  12.4 us
    ppermute x6, waiting for transfers between devices, across(): lax.ppermute(xs[k], 'ctx', [(i, i ^ k) for i in range(ctx)])  6.7 us
    pallas_call x1, Pallas kernels, local(): pl.pallas_call(functools.partial(q_kernel, parts), in_specs=[ANY, ANY, VM...  5.43 us
    pallas_call x2, Pallas kernels, project_some(): pl.pallas_call(functools.partial(project_kernel, steps), in_specs=[VMEM,...  5.35 us
    ppermute x2, waiting for transfers between devices, to_heads(): lax.ppermute(x, 'head', flip)  3.98 us
    pallas_call x1, Pallas kernels, local(): pl.pallas_call(functools.partial(kv_kernel, parts), in_specs=[ANY, ANY, A...  3.19 us
    ppermute x1, starting transfers between devices, local(): hop = [own, lax.ppermute(own, 'ctx', up)]  3.08 us
    ppermute x1, waiting for transfers between devices, local(): hop = [own, lax.ppermute(own, 'ctx', up)]  2.95 us
  transfers between devices with their start and end apart: 17, of which 7 were waited for; matrix products, arithmetic and copies ran while one was open for 0% of the time, Pallas kernels for 25%

profile of v6, /device:TPU:0, one launch (start us, length us, event | category | flops | bytes accessed | tf_op | source)
XLA Modules:
  0.0 58.3 jit_solution(17348856104883045107)
XLA Ops:
  0.0 3.2 %keys_values.1 = (bf16[272,512]{1,0:T(8,128)(2,1)S(1)}, f32[256,256]{1,0:T(8,128)S(1)}) custom-call(bf16[256,2048]{1,0:T(8,128)(2,1)} %x_hbm.3, bf16[2048,256]{1,0:T(8,128)(2,1)} %wk_hbm.1, bf16[2048,256]{1,0:T(8,128)(2,1)} %wv_hbm.1, s32[1,256]{1,0:T(1,128)} %bitcast.2), custom_call_target="tpu_custom_call" | custom-call | flops 536870912 | bytes 3145728 | tf_op jit(solution)/shard_map/keys_values/pallas_call | solution.py:424
  3.2 3.1 %collective-permute-start.1 = (bf16[272,512]{1,0:T(8,128)(2,1)S(1)}, bf16[272,512]{1,0:T(8,128)(2,1)S(1)}, u32[]{:S(2)}, u32[]{:S(2)}) collective-permute-start(bf16[272,512]{1,0:T(8,128)(2,1)S(1)} %get-tuple-element.46.refs_0_), channel_id=1, source_target_pairs={{0,4},{4,8},{8,12},{12,0},{1,5},{5,9},{9,13},{13,1},{2,6},{6,10},{... | collective-permute-start | bytes 835592 | tf_op jit(solution)/shard_map/ppermute | solution.py:440
  6.3 5.4 %queries.1.q_ref = bf16[16,256,128]{2,1,0:T(8,128)(2,1)S(1)} custom-call(bf16[256,2048]{1,0:T(8,128)(2,1)} %x_hbm.3, bf16[2048,2048]{1,0:T(8,128)(2,1)} %w_hbm.4, f32[256,256]{1,0:T(8,128)S(1)} %get-tuple-element.41.tab_ref), custom_call_target="tpu_custom_call" | custom-call | flops 2147483648 | bytes 9437184 | tf_op jit(solution)/shard_map/queries/pallas_call | solution.py:443
  11.7 0.3 routes.1
  12.0 2.9 %collective-permute-done.1.refs_1_ = bf16[272,512]{1,0:T(8,128)(2,1)S(1)} collective-permute-done((bf16[272,512]{1,0:T(8,128)(2,1)S(1)}, bf16[272,512]{1,0:T(8,128)(2,1)S(1)}, u32[]{:S(2)}, u32[]{:S(2)}) %collective-permute-start.1) | collective-permute-done | bytes 278560 | tf_op jit(solution)/shard_map/ppermute | solution.py:440
  15.0 0.7 %collective-permute-start.2 = (bf16[272,512]{1,0:T(8,128)(2,1)S(1)}, bf16[272,512]{1,0:T(8,128)(2,1)S(1)}, u32[]{:S(2)}, u32[]{:S(2)}) collective-permute-start(bf16[272,512]{1,0:T(8,128)(2,1)S(1)} %collective-permute-done.1.refs_1_), channel_id=1, source_target_pairs={{0,0},{4,8},{8,12},{12,4},{1,1},{5,9},{9,13},{13,5},{2,2},{6,10},{... | collective-permute-start | bytes 835592 | tf_op jit(solution)/shard_map/ppermute | solution.py:466
  15.8 0.5 collective-permute-start.4
  16.3 1.5 %even_attention.1.refs_2_ = f32[16,256,256]{2,1,0:T(8,128)S(1)} custom-call(s32[1,256]{1,0:T(1,128)S(1)} %bitcast.3, bf16[16,256,128]{2,1,0:T(8,128)(2,1)S(1)} %queries.1.q_ref, bf16[272,512]{1,0:T(8,128)(2,1)S(1)} %get-tuple-element.46.refs_0_, bf16[272,512]{1,0:T(8,128)(2,1)S(1)} %collective-permute-done.1.refs_1_), custom_call_target="tpu_custom_call" | custom-call | tf_op jit(solution)/shard_map/even_attention/pallas_call | solution.py:481
  17.8 0.2 odd_attention.1.near_ref
  18.0 1.9 %collective-permute-start.5 = (bf16[272,512]{1,0:T(8,128)(2,1)S(1)}, bf16[272,512]{1,0:T(8,128)(2,1)S(1)}, u32[]{:S(2)}, u32[]{:S(2)}) collective-permute-start(bf16[272,512]{1,0:T(8,128)(2,1)S(1)} %collective-permute-done.2.far_ref), channel_id=1, source_target_pairs={{0,1},{1,0},{2,3},{3,2},{4,5},{5,4},{6,7},{7,6},{8,9},{9,8},{10,11... | collective-permute-start | bytes 835592 | tf_op jit(solution)/shard_map/ppermute | solution.py:506
  20.0 1.1 %collective-permute-done.pair_slots = f32[32,128]{1,0:T(8,128)S(1)} collective-permute-done((f32[32,128]{1,0:T(8,128)S(1)}, f32[32,128]{1,0:T(8,128)S(1)}, u32[]{:S(2)}, u32[]{:S(2)}) %collective-permute-start) | collective-permute-done | bytes 16416 | tf_op jit(solution)/shard_map/ppermute | solution.py:492
  21.1 2.3 %far_attention_project.1 = (bf16[256,2048]{1,0:T(8,128)(2,1)S(1)}, bf16[256,512]{1,0:T(8,128)(2,1)S(1)}) custom-call(s32[1,256]{1,0:T(1,128)S(1)} %bitcast.5, bf16[16,256,128]{2,1,0:T(8,128)(2,1)S(1)} %queries.1.q_ref, bf16[272,512]{1,0:T(8,128)(2,1)S(1)} %collective-permute-done.2.far_ref, bf16[264,512]{1,0:T(8,128)(2,1)S(1)} %collective-permute-done.4.refs_1_.to_one, ...), custom_call_target="tpu_custom_call" | custom-call | flops 1610612736 | bytes 10485760 | tf_op jit(solution)/shard_map/far_attention_project/pallas_call | solution.py:509
  23.5 1.6 %collective-permute-start.6 = (bf16[256,512]{1,0:T(8,128)(2,1)S(1)}, bf16[256,512]{1,0:T(8,128)(2,1)S(1)}, u32[]{:S(2)}, u32[]{:S(2)}) collective-permute-start(bf16[256,512]{1,0:T(8,128)(2,1)S(1)} %get-tuple-element.60), channel_id=1, source_target_pairs={{0,2},{2,0},{1,3},{3,1},{4,6},{6,4},{5,7},{7,5},{8,10},{10,8},{9,1... | collective-permute-start | bytes 786440 | tf_op jit(solution)/shard_map/ppermute | solution.py:536
  25.0 3.0 %project.2 = (bf16[256,512]{1,0:T(8,128)(2,1)S(1)}, bf16[256,512]{1,0:T(8,128)(2,1)S(1)}) custom-call(bf16[256,2048]{1,0:T(8,128)(2,1)S(1)} %get-tuple-element.66.att_ref, bf16[2048,2048]{1,0:T(8,128)(2,1)} %w_hbm.7), custom_call_target="tpu_custom_call" | custom-call | flops 20000000000 | tf_op jit(solution)/shard_map/project/pallas_call | solution.py:522
  28.1 0.6 %collective-permute-start.7 = (bf16[256,512]{1,0:T(8,128)(2,1)S(1)}, bf16[256,512]{1,0:T(8,128)(2,1)S(1)}, u32[]{:S(2)}, u32[]{:S(2)}) collective-permute-start(bf16[256,512]{1,0:T(8,128)(2,1)S(1)} %get-tuple-element.53), channel_id=1, source_target_pairs={{0,2},{2,0},{1,3},{3,1},{4,6},{6,4},{5,7},{7,5},{8,10},{10,8},{9,1... | collective-permute-start | bytes 786440 | tf_op jit(solution)/shard_map/ppermute | solution.py:536
  28.7 4.0 %collective-permute-done.6.refs_5_ = bf16[256,512]{1,0:T(8,128)(2,1)S(1)} collective-permute-done((bf16[256,512]{1,0:T(8,128)(2,1)S(1)}, bf16[256,512]{1,0:T(8,128)(2,1)S(1)}, u32[]{:S(2)}, u32[]{:S(2)}) %collective-permute-start.6) | collective-permute-done | bytes 262176 | tf_op jit(solution)/shard_map/ppermute | solution.py:536
  32.7 0.3 add_pick.1
  33.0 5.5 %collective-permute-start.10 = (bf16[104,512]{1,0:T(8,128)(2,1)S(1)}, bf16[104,512]{1,0:T(8,128)(2,1)S(1)}, u32[]{:S(2)}, u32[]{:S(2)}) collective-permute-start(bf16[104,512]{1,0:T(8,128)(2,1)S(1)} %get-tuple-element.62), channel_id=1, source_target_pairs={{0,4},{4,0},{8,12},{12,8},{1,5},{5,1},{9,13},{13,9},{2,6},{6,2},{1... | collective-permute-start | bytes 319496 | tf_op jit(solution)/shard_map/ppermute | solution.py:550
  38.4 1.7 %collective-permute-start.11 = (bf16[104,512]{1,0:T(8,128)(2,1)S(1)}, bf16[104,512]{1,0:T(8,128)(2,1)S(1)}, u32[]{:S(2)}, u32[]{:S(2)}) collective-permute-start(bf16[104,512]{1,0:T(8,128)(2,1)S(1)} %get-tuple-element.63), channel_id=1, source_target_pairs={{0,8},{4,12},{8,0},{12,4},{1,9},{5,13},{9,1},{13,5},{2,10},{6,14},... | collective-permute-start | bytes 319496 | tf_op jit(solution)/shard_map/ppermute | solution.py:550
  40.2 0.7 %collective-permute-start.12 = (bf16[104,512]{1,0:T(8,128)(2,1)S(1)}, bf16[104,512]{1,0:T(8,128)(2,1)S(1)}, u32[]{:S(2)}, u32[]{:S(2)}) collective-permute-start(bf16[104,512]{1,0:T(8,128)(2,1)S(1)} %get-tuple-element.64), channel_id=1, source_target_pairs={{0,12},{4,8},{8,4},{12,0},{1,13},{5,9},{9,5},{13,1},{2,14},{6,10},... | collective-permute-start | bytes 319496 | tf_op jit(solution)/shard_map/ppermute | solution.py:550
  40.9 2.3 %project.3.refs_0_ = bf16[256,512]{1,0:T(8,128)(2,1)S(1)} custom-call(bf16[256,2048]{1,0:T(8,128)(2,1)S(1)} %get-tuple-element.66.att_ref, bf16[2048,2048]{1,0:T(8,128)(2,1)} %w_hbm.7), custom_call_target="tpu_custom_call" | custom-call | flops 20000000000 | tf_op jit(solution)/shard_map/project/pallas_call | solution.py:522
  43.2 0.3 add_split.1
  43.6 0.5 collective-permute-start.9
  44.1 0.8 %collective-permute-done.8.refs_0_ = bf16[96,512]{1,0:T(8,128)(2,1)S(1)} collective-permute-done((bf16[96,512]{1,0:T(8,128)(2,1)S(1)}, bf16[96,512]{1,0:T(8,128)(2,1)S(1)}, u32[]{:S(2)}, u32[]{:S(2)}) %collective-permute-start.8) | collective-permute-done | bytes 98336 | tf_op jit(solution)/shard_map/ppermute | solution.py:578
  45.1 1.1 %collective-permute-start.14 = (bf16[96,512]{1,0:T(8,128)(2,1)S(1)}, bf16[96,512]{1,0:T(8,128)(2,1)S(1)}, u32[]{:S(2)}, u32[]{:S(2)}) collective-permute-start(bf16[96,512]{1,0:T(8,128)(2,1)S(1)} %get-tuple-element.74), channel_id=1, source_target_pairs={{0,4},{4,0},{8,12},{12,8},{1,5},{5,1},{9,13},{13,9},{2,6},{6,2},{1... | collective-permute-start | bytes 294920 | tf_op jit(solution)/shard_map/ppermute | solution.py:550
  46.2 2.6 %collective-permute-start.15 = (bf16[96,512]{1,0:T(8,128)(2,1)S(1)}, bf16[96,512]{1,0:T(8,128)(2,1)S(1)}, u32[]{:S(2)}, u32[]{:S(2)}) collective-permute-start(bf16[96,512]{1,0:T(8,128)(2,1)S(1)} %get-tuple-element.75), channel_id=1, source_target_pairs={{0,8},{4,12},{8,0},{12,4},{1,9},{5,13},{9,1},{13,5},{2,10},{6,14},... | collective-permute-start | bytes 294920 | tf_op jit(solution)/shard_map/ppermute | solution.py:550
  48.8 0.7 %collective-permute-start.16 = (bf16[96,512]{1,0:T(8,128)(2,1)S(1)}, bf16[96,512]{1,0:T(8,128)(2,1)S(1)}, u32[]{:S(2)}, u32[]{:S(2)}) collective-permute-start(bf16[96,512]{1,0:T(8,128)(2,1)S(1)} %get-tuple-element.76), channel_id=1, source_target_pairs={{0,12},{4,8},{8,4},{12,0},{1,13},{5,9},{9,5},{13,1},{2,14},{6,10},... | collective-permute-start | bytes 294920 | tf_op jit(solution)/shard_map/ppermute | solution.py:550
  49.6 0.7 %place.1 = (bf16[256,512]{1,0:T(8,128)(2,1)S(1)}, bf16[256,512]{1,0:T(8,128)(2,1)S(1)}) custom-call(bf16[104,512]{1,0:T(8,128)(2,1)S(1)} %get-tuple-element.71.refs_0_, bf16[104,512]{1,0:T(8,128)(2,1)S(1)} %collective-permute-done.10.refs_1_, bf16[104,512]{1,0:T(8,128)(2,1)S(1)} %collective-permute-done.11.refs_2_, ...), custom_call_target="tpu_custom_call" | custom-call | flops 20000000000 | tf_op jit(solution)/shard_map/place/pallas_call | solution.py:592
  50.4 1.5 %collective-permute-done.14.refs_5_ = bf16[96,512]{1,0:T(8,128)(2,1)S(1)} collective-permute-done((bf16[96,512]{1,0:T(8,128)(2,1)S(1)}, bf16[96,512]{1,0:T(8,128)(2,1)S(1)}, u32[]{:S(2)}, u32[]{:S(2)}) %collective-permute-start.14) | collective-permute-done | bytes 98336 | tf_op jit(solution)/shard_map/ppermute | solution.py:550
  51.9 5.2 %collective-permute-done.15.refs_6_ = bf16[96,512]{1,0:T(8,128)(2,1)S(1)} collective-permute-done((bf16[96,512]{1,0:T(8,128)(2,1)S(1)}, bf16[96,512]{1,0:T(8,128)(2,1)S(1)}, u32[]{:S(2)}, u32[]{:S(2)}) %collective-permute-start.15) | collective-permute-done | bytes 98336 | tf_op jit(solution)/shard_map/ppermute | solution.py:550
  57.0 0.4 place_rest.1.rest_ref
  57.5 0.9 %join.1 = bf16[256,1024]{1,0:T(8,128)(2,1)} custom-call(bf16[256,512]{1,0:T(8,128)(2,1)S(1)} %get-tuple-element.72.mine_ref, bf16[256,512]{1,0:T(8,128)(2,1)S(1)} %collective-permute-done.13.pair_ref, bf16[256,512]{1,0:T(8,128)(2,1)S(1)} %place_rest.1.rest_ref), custom_call_target="tpu_custom_call" | custom-call | tf_op jit(solution)/shard_map/join/pallas_call | solution.py:613
  (21 shorter events, 0.5 us)
Async XLA Ops:
  0.0 16.3 %copy-start = (s32[256]{0:T(256)S(1)}, s32[256]{0:T(256)}, u32[]{:S(2)}) copy-start(s32[256]{0:T(256)} %param.8) | copy-start | bytes 3076
  0.0 11.7 %copy-start.1 = (s32[256]{0:T(256)S(1)}, s32[256]{0:T(256)}, u32[]{:S(2)}) copy-start(s32[256]{0:T(256)} %param.9) | copy-start | bytes 3076
  3.2 11.8 %collective-permute-start.1 = (bf16[272,512]{1,0:T(8,128)(2,1)S(1)}, bf16[272,512]{1,0:T(8,128)(2,1)S(1)}, u32[]{:S(2)}, u32[]{:S(2)}) collective-permute-start(bf16[272,512]{1,0:T(8,128)(2,1)S(1)} %get-tuple-element.46.refs_0_), channel_id=1, source_target_pairs={{0,4},{4,8},{8,12},{12,0},{1,5},{5,9},{9,13},{13,1},{2,6},{6,10},{... | collective-permute-start | bytes 835592 | tf_op jit(solution)/shard_map/ppermute | solution.py:440
  15.0 3.0 %collective-permute-start.2 = (bf16[272,512]{1,0:T(8,128)(2,1)S(1)}, bf16[272,512]{1,0:T(8,128)(2,1)S(1)}, u32[]{:S(2)}, u32[]{:S(2)}) collective-permute-start(bf16[272,512]{1,0:T(8,128)(2,1)S(1)} %collective-permute-done.1.refs_1_), channel_id=1, source_target_pairs={{0,0},{4,8},{8,12},{12,4},{1,1},{5,9},{9,13},{13,5},{2,2},{6,10},{... | collective-permute-start | bytes 835592 | tf_op jit(solution)/shard_map/ppermute | solution.py:466
  15.7 2.1 %collective-permute-start.3 = (bf16[264,512]{1,0:T(8,128)(2,1)S(1)}, bf16[264,512]{1,0:T(8,128)(2,1)S(1)}, u32[]{:S(2)}, u32[]{:S(2)}) collective-permute-start(bf16[264,512]{1,0:T(8,128)(2,1)S(1)} %get-tuple-element.48), channel_id=1, source_target_pairs={{0,1},{1,0},{2,3},{3,2},{4,5},{5,4},{6,7},{7,6},{8,9},{9,8},{10,11... | collective-permute-start | bytes 811016 | tf_op jit(solution)/shard_map/ppermute | solution.py:493
  15.8 2.1 %collective-permute-start.4 = (bf16[264,512]{1,0:T(8,128)(2,1)S(1)}, bf16[264,512]{1,0:T(8,128)(2,1)S(1)}, u32[]{:S(2)}, u32[]{:S(2)}) collective-permute-start(bf16[264,512]{1,0:T(8,128)(2,1)S(1)} %get-tuple-element.49), channel_id=1, source_target_pairs={{0,1},{1,0},{2,3},{3,2},{4,5},{5,4},{6,7},{7,6},{8,9},{9,8},{10,11... | collective-permute-start | bytes 811016 | tf_op jit(solution)/shard_map/ppermute | solution.py:493
  18.0 3.1 %collective-permute-start.5 = (bf16[272,512]{1,0:T(8,128)(2,1)S(1)}, bf16[272,512]{1,0:T(8,128)(2,1)S(1)}, u32[]{:S(2)}, u32[]{:S(2)}) collective-permute-start(bf16[272,512]{1,0:T(8,128)(2,1)S(1)} %collective-permute-done.2.far_ref), channel_id=1, source_target_pairs={{0,1},{1,0},{2,3},{3,2},{4,5},{5,4},{6,7},{7,6},{8,9},{9,8},{10,11... | collective-permute-start | bytes 835592 | tf_op jit(solution)/shard_map/ppermute | solution.py:506
  19.9 1.2 %collective-permute-start = (f32[32,128]{1,0:T(8,128)S(1)}, f32[32,128]{1,0:T(8,128)S(1)}, u32[]{:S(2)}, u32[]{:S(2)}) collective-permute-start(f32[32,128]{1,0:T(8,128)S(1)} %get-tuple-element.44), channel_id=1, source_target_pairs={{0,1},{1,0},{2,3},{3,2},{4,5},{5,4},{6,7},{7,6},{8,9},{9,8},{10,11... | collective-permute-start | bytes 49160 | tf_op jit(solution)/shard_map/ppermute | solution.py:492
  23.5 9.2 %collective-permute-start.6 = (bf16[256,512]{1,0:T(8,128)(2,1)S(1)}, bf16[256,512]{1,0:T(8,128)(2,1)S(1)}, u32[]{:S(2)}, u32[]{:S(2)}) collective-permute-start(bf16[256,512]{1,0:T(8,128)(2,1)S(1)} %get-tuple-element.60), channel_id=1, source_target_pairs={{0,2},{2,0},{1,3},{3,1},{4,6},{6,4},{5,7},{7,5},{8,10},{10,8},{9,1... | collective-permute-start | bytes 786440 | tf_op jit(solution)/shard_map/ppermute | solution.py:536
  28.1 15.1 %collective-permute-start.7 = (bf16[256,512]{1,0:T(8,128)(2,1)S(1)}, bf16[256,512]{1,0:T(8,128)(2,1)S(1)}, u32[]{:S(2)}, u32[]{:S(2)}) collective-permute-start(bf16[256,512]{1,0:T(8,128)(2,1)S(1)} %get-tuple-element.53), channel_id=1, source_target_pairs={{0,2},{2,0},{1,3},{3,1},{4,6},{6,4},{5,7},{7,5},{8,10},{10,8},{9,1... | collective-permute-start | bytes 786440 | tf_op jit(solution)/shard_map/ppermute | solution.py:536
  33.0 15.9 %collective-permute-start.10 = (bf16[104,512]{1,0:T(8,128)(2,1)S(1)}, bf16[104,512]{1,0:T(8,128)(2,1)S(1)}, u32[]{:S(2)}, u32[]{:S(2)}) collective-permute-start(bf16[104,512]{1,0:T(8,128)(2,1)S(1)} %get-tuple-element.62), channel_id=1, source_target_pairs={{0,4},{4,0},{8,12},{12,8},{1,5},{5,1},{9,13},{13,9},{2,6},{6,2},{1... | collective-permute-start | bytes 319496 | tf_op jit(solution)/shard_map/ppermute | solution.py:550
  38.4 11.1 %collective-permute-start.11 = (bf16[104,512]{1,0:T(8,128)(2,1)S(1)}, bf16[104,512]{1,0:T(8,128)(2,1)S(1)}, u32[]{:S(2)}, u32[]{:S(2)}) collective-permute-start(bf16[104,512]{1,0:T(8,128)(2,1)S(1)} %get-tuple-element.63), channel_id=1, source_target_pairs={{0,8},{4,12},{8,0},{12,4},{1,9},{5,13},{9,1},{13,5},{2,10},{6,14},... | collective-permute-start | bytes 319496 | tf_op jit(solution)/shard_map/ppermute | solution.py:550
  40.2 9.4 %collective-permute-start.12 = (bf16[104,512]{1,0:T(8,128)(2,1)S(1)}, bf16[104,512]{1,0:T(8,128)(2,1)S(1)}, u32[]{:S(2)}, u32[]{:S(2)}) collective-permute-start(bf16[104,512]{1,0:T(8,128)(2,1)S(1)} %get-tuple-element.64), channel_id=1, source_target_pairs={{0,12},{4,8},{8,4},{12,0},{1,13},{5,9},{9,5},{13,1},{2,14},{6,10},... | collective-permute-start | bytes 319496 | tf_op jit(solution)/shard_map/ppermute | solution.py:550
  43.6 1.4 %collective-permute-start.8 = (bf16[96,512]{1,0:T(8,128)(2,1)S(1)}, bf16[96,512]{1,0:T(8,128)(2,1)S(1)}, u32[]{:S(2)}, u32[]{:S(2)}) collective-permute-start(bf16[96,512]{1,0:T(8,128)(2,1)S(1)} %get-tuple-element.68), channel_id=1, source_target_pairs={{0,1},{1,0},{2,3},{3,2},{4,5},{5,4},{6,7},{7,6},{8,9},{9,8},{10,11... | collective-permute-start | bytes 294920 | tf_op jit(solution)/shard_map/ppermute | solution.py:578
  43.6 1.4 %collective-permute-start.9 = (bf16[96,512]{1,0:T(8,128)(2,1)S(1)}, bf16[96,512]{1,0:T(8,128)(2,1)S(1)}, u32[]{:S(2)}, u32[]{:S(2)}) collective-permute-start(bf16[96,512]{1,0:T(8,128)(2,1)S(1)} %get-tuple-element.69), channel_id=1, source_target_pairs={{0,1},{1,0},{2,3},{3,2},{4,5},{5,4},{6,7},{7,6},{8,9},{9,8},{10,11... | collective-permute-start | bytes 294920 | tf_op jit(solution)/shard_map/ppermute | solution.py:578
  45.1 6.8 %collective-permute-start.14 = (bf16[96,512]{1,0:T(8,128)(2,1)S(1)}, bf16[96,512]{1,0:T(8,128)(2,1)S(1)}, u32[]{:S(2)}, u32[]{:S(2)}) collective-permute-start(bf16[96,512]{1,0:T(8,128)(2,1)S(1)} %get-tuple-element.74), channel_id=1, source_target_pairs={{0,4},{4,0},{8,12},{12,8},{1,5},{5,1},{9,13},{13,9},{2,6},{6,2},{1... | collective-permute-start | bytes 294920 | tf_op jit(solution)/shard_map/ppermute | solution.py:550
  46.2 10.8 %collective-permute-start.15 = (bf16[96,512]{1,0:T(8,128)(2,1)S(1)}, bf16[96,512]{1,0:T(8,128)(2,1)S(1)}, u32[]{:S(2)}, u32[]{:S(2)}) collective-permute-start(bf16[96,512]{1,0:T(8,128)(2,1)S(1)} %get-tuple-element.75), channel_id=1, source_target_pairs={{0,8},{4,12},{8,0},{12,4},{1,9},{5,13},{9,1},{13,5},{2,10},{6,14},... | collective-permute-start | bytes 294920 | tf_op jit(solution)/shard_map/ppermute | solution.py:550
  48.8 8.2 %collective-permute-start.16 = (bf16[96,512]{1,0:T(8,128)(2,1)S(1)}, bf16[96,512]{1,0:T(8,128)(2,1)S(1)}, u32[]{:S(2)}, u32[]{:S(2)}) collective-permute-start(bf16[96,512]{1,0:T(8,128)(2,1)S(1)} %get-tuple-element.76), channel_id=1, source_target_pairs={{0,12},{4,8},{8,4},{12,0},{1,13},{5,9},{9,5},{13,1},{2,14},{6,10},... | collective-permute-start | bytes 294920 | tf_op jit(solution)/shard_map/ppermute | solution.py:550
  50.3 7.2 %collective-permute-start.13 = (bf16[256,512]{1,0:T(8,128)(2,1)S(1)}, bf16[256,512]{1,0:T(8,128)(2,1)S(1)}, u32[]{:S(2)}, u32[]{:S(2)}) collective-permute-start(bf16[256,512]{1,0:T(8,128)(2,1)S(1)} %get-tuple-element.73), channel_id=1, source_target_pairs={{0,1},{1,0},{2,3},{3,2},{4,5},{5,4},{6,7},{7,6},{8,9},{9,8},{10,11... | collective-permute-start | bytes 786440 | tf_op jit(solution)/shard_map/ppermute | solution.py:601

commit v7 on v6

--- a/solution.py
+++ b/solution.py
@@ -463,7 +463,7 @@
     buffer_pos, pair_slots, *slots = route(after(dest_rows.reshape(1, rows), queries))
     hop[1] = after(hop[1], queries, buffer_pos)
     for i in range(1, hops):
-        hop.append(lax.ppermute(hop[i], "ctx", [(j, j) for j in range(i)] + [(j, j + 1) for j in range(i, ctx - 1)] + [(ctx - 1, i)]))
+        hop.append(lax.ppermute(hop[i], "ctx", [(j, j + 1) for j in range(i, ctx - 1)]))
 
     short = sds((rows + 8, 2 * kv_cols), BF16)
     short_hop = pl.pallas_call(

time: 58.5 us -> 58.4 us (level)
  starting transfers between devices: 21.5 us -> 20.7 us
    ppermute x6, starting transfers between devices: 12.4 us -> 11.6 us  [across(): lax.ppermute(xs[k], 'ctx', [(i, i ^ k) for i in range(ctx)])]
where the time goes in v7:
time: 58.4 us; the launch traced here: 57.9 us
  Pallas kernels  20.9 us (36%)
  starting transfers between devices  20.7 us (35%)
  waiting for transfers between devices  16 us (27%)
    ppermute x6, starting transfers between devices, across(): lax.ppermute(xs[k], 'ctx', [(i, i ^ k) for i in range(ctx)])  11.6 us
    ppermute x6, waiting for transfers between devices, across(): lax.ppermute(xs[k], 'ctx', [(i, i ^ k) for i in range(ctx)])  7.03 us
    pallas_call x1, Pallas kernels, local(): pl.pallas_call(functools.partial(q_kernel, parts), in_specs=[ANY, ANY, VM...  5.43 us
    pallas_call x2, Pallas kernels, project_some(): pl.pallas_call(functools.partial(project_kernel, steps), in_specs=[VMEM,...  5.36 us
    ppermute x2, waiting for transfers between devices, to_heads(): lax.ppermute(x, 'head', flip)  3.98 us
    pallas_call x1, Pallas kernels, local(): pl.pallas_call(functools.partial(kv_kernel, parts), in_specs=[ANY, ANY, A...  3.19 us
    ppermute x1, starting transfers between devices, local(): hop = [own, lax.ppermute(own, 'ctx', up)]  3.08 us
    ppermute x1, waiting for transfers between devices, local(): hop = [own, lax.ppermute(own, 'ctx', up)]  2.95 us
  transfers between devices with their start and end apart: 17, of which 7 were waited for; matrix products, arithmetic and copies ran while one was open for 0% of the time, Pallas kernels for 25%

profile of v7, /device:TPU:0, one launch (start us, length us, event | category | flops | bytes accessed | tf_op | source)
XLA Modules:
  0.0 57.9 jit_solution(10825640601424587020)
XLA Ops:
  0.0 3.2 %keys_values.1 = (bf16[272,512]{1,0:T(8,128)(2,1)S(1)}, f32[256,256]{1,0:T(8,128)S(1)}) custom-call(bf16[256,2048]{1,0:T(8,128)(2,1)} %x_hbm.3, bf16[2048,256]{1,0:T(8,128)(2,1)} %wk_hbm.1, bf16[2048,256]{1,0:T(8,128)(2,1)} %wv_hbm.1, s32[1,256]{1,0:T(1,128)} %bitcast.2), custom_call_target="tpu_custom_call" | custom-call | flops 536870912 | bytes 3145728 | tf_op jit(solution)/shard_map/keys_values/pallas_call | solution.py:424
  3.2 3.1 %collective-permute-start.1 = (bf16[272,512]{1,0:T(8,128)(2,1)S(1)}, bf16[272,512]{1,0:T(8,128)(2,1)S(1)}, u32[]{:S(2)}, u32[]{:S(2)}) collective-permute-start(bf16[272,512]{1,0:T(8,128)(2,1)S(1)} %get-tuple-element.46.refs_0_), channel_id=1, source_target_pairs={{0,4},{4,8},{8,12},{12,0},{1,5},{5,9},{9,13},{13,1},{2,6},{6,10},{... | collective-permute-start | bytes 835592 | tf_op jit(solution)/shard_map/ppermute | solution.py:440
  6.3 5.4 %queries.1.q_ref = bf16[16,256,128]{2,1,0:T(8,128)(2,1)S(1)} custom-call(bf16[256,2048]{1,0:T(8,128)(2,1)} %x_hbm.3, bf16[2048,2048]{1,0:T(8,128)(2,1)} %w_hbm.4, f32[256,256]{1,0:T(8,128)S(1)} %get-tuple-element.41.tab_ref), custom_call_target="tpu_custom_call" | custom-call | flops 2147483648 | bytes 9437184 | tf_op jit(solution)/shard_map/queries/pallas_call | solution.py:443
  11.7 0.3 routes.1
  12.0 2.9 %collective-permute-done.1.refs_1_ = bf16[272,512]{1,0:T(8,128)(2,1)S(1)} collective-permute-done((bf16[272,512]{1,0:T(8,128)(2,1)S(1)}, bf16[272,512]{1,0:T(8,128)(2,1)S(1)}, u32[]{:S(2)}, u32[]{:S(2)}) %collective-permute-start.1) | collective-permute-done | bytes 278560 | tf_op jit(solution)/shard_map/ppermute | solution.py:440
  15.0 0.7 %collective-permute-start.2 = (bf16[272,512]{1,0:T(8,128)(2,1)S(1)}, bf16[272,512]{1,0:T(8,128)(2,1)S(1)}, u32[]{:S(2)}, u32[]{:S(2)}) collective-permute-start(bf16[272,512]{1,0:T(8,128)(2,1)S(1)} %collective-permute-done.1.refs_1_), channel_id=1, source_target_pairs={{4,8},{8,12},{5,9},{9,13},{6,10},{10,14},{7,11},{11,15},{20,24},{2... | collective-permute-start | bytes 835592 | tf_op jit(solution)/shard_map/ppermute | solution.py:466
  15.8 0.5 collective-permute-start.4
  16.3 1.5 %even_attention.1.refs_2_ = f32[16,256,256]{2,1,0:T(8,128)S(1)} custom-call(s32[1,256]{1,0:T(1,128)S(1)} %bitcast.3, bf16[16,256,128]{2,1,0:T(8,128)(2,1)S(1)} %queries.1.q_ref, bf16[272,512]{1,0:T(8,128)(2,1)S(1)} %get-tuple-element.46.refs_0_, bf16[272,512]{1,0:T(8,128)(2,1)S(1)} %collective-permute-done.1.refs_1_), custom_call_target="tpu_custom_call" | custom-call | tf_op jit(solution)/shard_map/even_attention/pallas_call | solution.py:481
  17.8 0.2 odd_attention.1.near_ref
  18.0 1.9 %collective-permute-start.5 = (bf16[272,512]{1,0:T(8,128)(2,1)S(1)}, bf16[272,512]{1,0:T(8,128)(2,1)S(1)}, u32[]{:S(2)}, u32[]{:S(2)}) collective-permute-start(bf16[272,512]{1,0:T(8,128)(2,1)S(1)} %collective-permute-done.2.far_ref), channel_id=1, source_target_pairs={{0,1},{1,0},{2,3},{3,2},{4,5},{5,4},{6,7},{7,6},{8,9},{9,8},{10,11... | collective-permute-start | bytes 835592 | tf_op jit(solution)/shard_map/ppermute | solution.py:506
  19.9 0.1 collective-permute-start
  20.0 1.1 %collective-permute-done.pair_slots = f32[32,128]{1,0:T(8,128)S(1)} collective-permute-done((f32[32,128]{1,0:T(8,128)S(1)}, f32[32,128]{1,0:T(8,128)S(1)}, u32[]{:S(2)}, u32[]{:S(2)}) %collective-permute-start) | collective-permute-done | bytes 16416 | tf_op jit(solution)/shard_map/ppermute | solution.py:492
  21.1 2.3 %far_attention_project.1 = (bf16[256,2048]{1,0:T(8,128)(2,1)S(1)}, bf16[256,512]{1,0:T(8,128)(2,1)S(1)}) custom-call(s32[1,256]{1,0:T(1,128)S(1)} %bitcast.5, bf16[16,256,128]{2,1,0:T(8,128)(2,1)S(1)} %queries.1.q_ref, bf16[272,512]{1,0:T(8,128)(2,1)S(1)} %collective-permute-done.2.far_ref, bf16[264,512]{1,0:T(8,128)(2,1)S(1)} %collective-permute-done.4.refs_1_.to_one, ...), custom_call_target="tpu_custom_call" | custom-call | flops 1610612736 | bytes 10485760 | tf_op jit(solution)/shard_map/far_attention_project/pallas_call | solution.py:509
  23.5 1.6 %collective-permute-start.6 = (bf16[256,512]{1,0:T(8,128)(2,1)S(1)}, bf16[256,512]{1,0:T(8,128)(2,1)S(1)}, u32[]{:S(2)}, u32[]{:S(2)}) collective-permute-start(bf16[256,512]{1,0:T(8,128)(2,1)S(1)} %get-tuple-element.60), channel_id=1, source_target_pairs={{0,2},{2,0},{1,3},{3,1},{4,6},{6,4},{5,7},{7,5},{8,10},{10,8},{9,1... | collective-permute-start | bytes 786440 | tf_op jit(solution)/shard_map/ppermute | solution.py:536
  25.0 3.0 %project.2 = (bf16[256,512]{1,0:T(8,128)(2,1)S(1)}, bf16[256,512]{1,0:T(8,128)(2,1)S(1)}) custom-call(bf16[256,2048]{1,0:T(8,128)(2,1)S(1)} %get-tuple-element.66.att_ref, bf16[2048,2048]{1,0:T(8,128)(2,1)} %w_hbm.7), custom_call_target="tpu_custom_call" | custom-call | flops 20000000000 | tf_op jit(solution)/shard_map/project/pallas_call | solution.py:522
  28.1 0.6 %collective-permute-start.7 = (bf16[256,512]{1,0:T(8,128)(2,1)S(1)}, bf16[256,512]{1,0:T(8,128)(2,1)S(1)}, u32[]{:S(2)}, u32[]{:S(2)}) collective-permute-start(bf16[256,512]{1,0:T(8,128)(2,1)S(1)} %get-tuple-element.53), channel_id=1, source_target_pairs={{0,2},{2,0},{1,3},{3,1},{4,6},{6,4},{5,7},{7,5},{8,10},{10,8},{9,1... | collective-permute-start | bytes 786440 | tf_op jit(solution)/shard_map/ppermute | solution.py:536
  28.7 4.0 %collective-permute-done.6.refs_5_ = bf16[256,512]{1,0:T(8,128)(2,1)S(1)} collective-permute-done((bf16[256,512]{1,0:T(8,128)(2,1)S(1)}, bf16[256,512]{1,0:T(8,128)(2,1)S(1)}, u32[]{:S(2)}, u32[]{:S(2)}) %collective-permute-start.6) | collective-permute-done | bytes 262176 | tf_op jit(solution)/shard_map/ppermute | solution.py:536
  32.7 0.3 add_pick.1
  33.0 4.0 %collective-permute-start.10 = (bf16[104,512]{1,0:T(8,128)(2,1)S(1)}, bf16[104,512]{1,0:T(8,128)(2,1)S(1)}, u32[]{:S(2)}, u32[]{:S(2)}) collective-permute-start(bf16[104,512]{1,0:T(8,128)(2,1)S(1)} %get-tuple-element.62), channel_id=1, source_target_pairs={{0,4},{4,0},{8,12},{12,8},{1,5},{5,1},{9,13},{13,9},{2,6},{6,2},{1... | collective-permute-start | bytes 319496 | tf_op jit(solution)/shard_map/ppermute | solution.py:550
  37.0 3.1 %collective-permute-start.11 = (bf16[104,512]{1,0:T(8,128)(2,1)S(1)}, bf16[104,512]{1,0:T(8,128)(2,1)S(1)}, u32[]{:S(2)}, u32[]{:S(2)}) collective-permute-start(bf16[104,512]{1,0:T(8,128)(2,1)S(1)} %get-tuple-element.63), channel_id=1, source_target_pairs={{0,8},{4,12},{8,0},{12,4},{1,9},{5,13},{9,1},{13,5},{2,10},{6,14},... | collective-permute-start | bytes 319496 | tf_op jit(solution)/shard_map/ppermute | solution.py:550
  40.1 2.3 %project.3.refs_0_ = bf16[256,512]{1,0:T(8,128)(2,1)S(1)} custom-call(bf16[256,2048]{1,0:T(8,128)(2,1)S(1)} %get-tuple-element.66.att_ref, bf16[2048,2048]{1,0:T(8,128)(2,1)} %w_hbm.7), custom_call_target="tpu_custom_call" | custom-call | flops 20000000000 | tf_op jit(solution)/shard_map/project/pallas_call | solution.py:522
  42.4 0.3 add_split.1
  42.9 0.5 collective-permute-start.9
  43.4 0.8 %collective-permute-done.8.refs_0_ = bf16[96,512]{1,0:T(8,128)(2,1)S(1)} collective-permute-done((bf16[96,512]{1,0:T(8,128)(2,1)S(1)}, bf16[96,512]{1,0:T(8,128)(2,1)S(1)}, u32[]{:S(2)}, u32[]{:S(2)}) %collective-permute-start.8) | collective-permute-done | bytes 98336 | tf_op jit(solution)/shard_map/ppermute | solution.py:578
  44.1 0.2 collective-permute-done.9.refs_1_
  44.3 0.6 %collective-permute-start.14 = (bf16[96,512]{1,0:T(8,128)(2,1)S(1)}, bf16[96,512]{1,0:T(8,128)(2,1)S(1)}, u32[]{:S(2)}, u32[]{:S(2)}) collective-permute-start(bf16[96,512]{1,0:T(8,128)(2,1)S(1)} %get-tuple-element.74), channel_id=1, source_target_pairs={{0,4},{4,0},{8,12},{12,8},{1,5},{5,1},{9,13},{13,9},{2,6},{6,2},{1... | collective-permute-start | bytes 294920 | tf_op jit(solution)/shard_map/ppermute | solution.py:550
  45.0 3.8 %collective-permute-start.15 = (bf16[96,512]{1,0:T(8,128)(2,1)S(1)}, bf16[96,512]{1,0:T(8,128)(2,1)S(1)}, u32[]{:S(2)}, u32[]{:S(2)}) collective-permute-start(bf16[96,512]{1,0:T(8,128)(2,1)S(1)} %get-tuple-element.75), channel_id=1, source_target_pairs={{0,8},{4,12},{8,0},{12,4},{1,9},{5,13},{9,1},{13,5},{2,10},{6,14},... | collective-permute-start | bytes 294920 | tf_op jit(solution)/shard_map/ppermute | solution.py:550
  48.8 0.7 %place.1 = (bf16[256,512]{1,0:T(8,128)(2,1)S(1)}, bf16[256,512]{1,0:T(8,128)(2,1)S(1)}) custom-call(bf16[104,512]{1,0:T(8,128)(2,1)S(1)} %get-tuple-element.71.refs_0_, bf16[104,512]{1,0:T(8,128)(2,1)S(1)} %collective-permute-done.10.refs_1_, bf16[104,512]{1,0:T(8,128)(2,1)S(1)} %collective-permute-done.11.refs_2_, ...), custom_call_target="tpu_custom_call" | custom-call | flops 20000000000 | tf_op jit(solution)/shard_map/place/pallas_call | solution.py:592
  49.6 0.1 collective-permute-done.14.refs_5_
  49.7 6.9 %collective-permute-done.15.refs_6_ = bf16[96,512]{1,0:T(8,128)(2,1)S(1)} collective-permute-done((bf16[96,512]{1,0:T(8,128)(2,1)S(1)}, bf16[96,512]{1,0:T(8,128)(2,1)S(1)}, u32[]{:S(2)}, u32[]{:S(2)}) %collective-permute-start.15) | collective-permute-done | bytes 98336 | tf_op jit(solution)/shard_map/ppermute | solution.py:550
  56.6 0.4 place_rest.1.rest_ref
  57.0 0.9 %join.1 = bf16[256,1024]{1,0:T(8,128)(2,1)} custom-call(bf16[256,512]{1,0:T(8,128)(2,1)S(1)} %get-tuple-element.72.mine_ref, bf16[256,512]{1,0:T(8,128)(2,1)S(1)} %collective-permute-done.13.pair_ref, bf16[256,512]{1,0:T(8,128)(2,1)S(1)} %place_rest.1.rest_ref), custom_call_target="tpu_custom_call" | custom-call | tf_op jit(solution)/shard_map/join/pallas_call | solution.py:613
  (21 shorter events, 0.3 us)
Async XLA Ops:
  0.0 16.3 %copy-start = (s32[256]{0:T(256)S(1)}, s32[256]{0:T(256)}, u32[]{:S(2)}) copy-start(s32[256]{0:T(256)} %param.8) | copy-start | bytes 3076
  0.0 11.7 %copy-start.1 = (s32[256]{0:T(256)S(1)}, s32[256]{0:T(256)}, u32[]{:S(2)}) copy-start(s32[256]{0:T(256)} %param.9) | copy-start | bytes 3076
  3.2 11.8 %collective-permute-start.1 = (bf16[272,512]{1,0:T(8,128)(2,1)S(1)}, bf16[272,512]{1,0:T(8,128)(2,1)S(1)}, u32[]{:S(2)}, u32[]{:S(2)}) collective-permute-start(bf16[272,512]{1,0:T(8,128)(2,1)S(1)} %get-tuple-element.46.refs_0_), channel_id=1, source_target_pairs={{0,4},{4,8},{8,12},{12,0},{1,5},{5,9},{9,13},{13,1},{2,6},{6,10},{... | collective-permute-start | bytes 835592 | tf_op jit(solution)/shard_map/ppermute | solution.py:440
  15.0 3.0 %collective-permute-start.2 = (bf16[272,512]{1,0:T(8,128)(2,1)S(1)}, bf16[272,512]{1,0:T(8,128)(2,1)S(1)}, u32[]{:S(2)}, u32[]{:S(2)}) collective-permute-start(bf16[272,512]{1,0:T(8,128)(2,1)S(1)} %collective-permute-done.1.refs_1_), channel_id=1, source_target_pairs={{4,8},{8,12},{5,9},{9,13},{6,10},{10,14},{7,11},{11,15},{20,24},{2... | collective-permute-start | bytes 835592 | tf_op jit(solution)/shard_map/ppermute | solution.py:466
  15.7 2.1 %collective-permute-start.3 = (bf16[264,512]{1,0:T(8,128)(2,1)S(1)}, bf16[264,512]{1,0:T(8,128)(2,1)S(1)}, u32[]{:S(2)}, u32[]{:S(2)}) collective-permute-start(bf16[264,512]{1,0:T(8,128)(2,1)S(1)} %get-tuple-element.48), channel_id=1, source_target_pairs={{0,1},{1,0},{2,3},{3,2},{4,5},{5,4},{6,7},{7,6},{8,9},{9,8},{10,11... | collective-permute-start | bytes 811016 | tf_op jit(solution)/shard_map/ppermute | solution.py:493
  15.8 2.1 %collective-permute-start.4 = (bf16[264,512]{1,0:T(8,128)(2,1)S(1)}, bf16[264,512]{1,0:T(8,128)(2,1)S(1)}, u32[]{:S(2)}, u32[]{:S(2)}) collective-permute-start(bf16[264,512]{1,0:T(8,128)(2,1)S(1)} %get-tuple-element.49), channel_id=1, source_target_pairs={{0,1},{1,0},{2,3},{3,2},{4,5},{5,4},{6,7},{7,6},{8,9},{9,8},{10,11... | collective-permute-start | bytes 811016 | tf_op jit(solution)/shard_map/ppermute | solution.py:493
  18.0 3.1 %collective-permute-start.5 = (bf16[272,512]{1,0:T(8,128)(2,1)S(1)}, bf16[272,512]{1,0:T(8,128)(2,1)S(1)}, u32[]{:S(2)}, u32[]{:S(2)}) collective-permute-start(bf16[272,512]{1,0:T(8,128)(2,1)S(1)} %collective-permute-done.2.far_ref), channel_id=1, source_target_pairs={{0,1},{1,0},{2,3},{3,2},{4,5},{5,4},{6,7},{7,6},{8,9},{9,8},{10,11... | collective-permute-start | bytes 835592 | tf_op jit(solution)/shard_map/ppermute | solution.py:506
  19.9 1.2 %collective-permute-start = (f32[32,128]{1,0:T(8,128)S(1)}, f32[32,128]{1,0:T(8,128)S(1)}, u32[]{:S(2)}, u32[]{:S(2)}) collective-permute-start(f32[32,128]{1,0:T(8,128)S(1)} %get-tuple-element.44), channel_id=1, source_target_pairs={{0,1},{1,0},{2,3},{3,2},{4,5},{5,4},{6,7},{7,6},{8,9},{9,8},{10,11... | collective-permute-start | bytes 49160 | tf_op jit(solution)/shard_map/ppermute | solution.py:492
  23.5 9.2 %collective-permute-start.6 = (bf16[256,512]{1,0:T(8,128)(2,1)S(1)}, bf16[256,512]{1,0:T(8,128)(2,1)S(1)}, u32[]{:S(2)}, u32[]{:S(2)}) collective-permute-start(bf16[256,512]{1,0:T(8,128)(2,1)S(1)} %get-tuple-element.60), channel_id=1, source_target_pairs={{0,2},{2,0},{1,3},{3,1},{4,6},{6,4},{5,7},{7,5},{8,10},{10,8},{9,1... | collective-permute-start | bytes 786440 | tf_op jit(solution)/shard_map/ppermute | solution.py:536
  28.1 14.3 %collective-permute-start.7 = (bf16[256,512]{1,0:T(8,128)(2,1)S(1)}, bf16[256,512]{1,0:T(8,128)(2,1)S(1)}, u32[]{:S(2)}, u32[]{:S(2)}) collective-permute-start(bf16[256,512]{1,0:T(8,128)(2,1)S(1)} %get-tuple-element.53), channel_id=1, source_target_pairs={{0,2},{2,0},{1,3},{3,1},{4,6},{6,4},{5,7},{7,5},{8,10},{10,8},{9,1... | collective-permute-start | bytes 786440 | tf_op jit(solution)/shard_map/ppermute | solution.py:536
  33.0 15.8 %collective-permute-start.10 = (bf16[104,512]{1,0:T(8,128)(2,1)S(1)}, bf16[104,512]{1,0:T(8,128)(2,1)S(1)}, u32[]{:S(2)}, u32[]{:S(2)}) collective-permute-start(bf16[104,512]{1,0:T(8,128)(2,1)S(1)} %get-tuple-element.62), channel_id=1, source_target_pairs={{0,4},{4,0},{8,12},{12,8},{1,5},{5,1},{9,13},{13,9},{2,6},{6,2},{1... | collective-permute-start | bytes 319496 | tf_op jit(solution)/shard_map/ppermute | solution.py:550
  37.0 11.8 %collective-permute-start.11 = (bf16[104,512]{1,0:T(8,128)(2,1)S(1)}, bf16[104,512]{1,0:T(8,128)(2,1)S(1)}, u32[]{:S(2)}, u32[]{:S(2)}) collective-permute-start(bf16[104,512]{1,0:T(8,128)(2,1)S(1)} %get-tuple-element.63), channel_id=1, source_target_pairs={{0,8},{4,12},{8,0},{12,4},{1,9},{5,13},{9,1},{13,5},{2,10},{6,14},... | collective-permute-start | bytes 319496 | tf_op jit(solution)/shard_map/ppermute | solution.py:550
  40.1 8.7 %collective-permute-start.12 = (bf16[104,512]{1,0:T(8,128)(2,1)S(1)}, bf16[104,512]{1,0:T(8,128)(2,1)S(1)}, u32[]{:S(2)}, u32[]{:S(2)}) collective-permute-start(bf16[104,512]{1,0:T(8,128)(2,1)S(1)} %get-tuple-element.64), channel_id=1, source_target_pairs={{0,12},{4,8},{8,4},{12,0},{1,13},{5,9},{9,5},{13,1},{2,14},{6,10},... | collective-permute-start | bytes 319496 | tf_op jit(solution)/shard_map/ppermute | solution.py:550
  42.8 1.4 %collective-permute-start.8 = (bf16[96,512]{1,0:T(8,128)(2,1)S(1)}, bf16[96,512]{1,0:T(8,128)(2,1)S(1)}, u32[]{:S(2)}, u32[]{:S(2)}) collective-permute-start(bf16[96,512]{1,0:T(8,128)(2,1)S(1)} %get-tuple-element.68), channel_id=1, source_target_pairs={{0,1},{1,0},{2,3},{3,2},{4,5},{5,4},{6,7},{7,6},{8,9},{9,8},{10,11... | collective-permute-start | bytes 294920 | tf_op jit(solution)/shard_map/ppermute | solution.py:578
  42.9 1.4 %collective-permute-start.9 = (bf16[96,512]{1,0:T(8,128)(2,1)S(1)}, bf16[96,512]{1,0:T(8,128)(2,1)S(1)}, u32[]{:S(2)}, u32[]{:S(2)}) collective-permute-start(bf16[96,512]{1,0:T(8,128)(2,1)S(1)} %get-tuple-element.69), channel_id=1, source_target_pairs={{0,1},{1,0},{2,3},{3,2},{4,5},{5,4},{6,7},{7,6},{8,9},{9,8},{10,11... | collective-permute-start | bytes 294920 | tf_op jit(solution)/shard_map/ppermute | solution.py:578
  44.3 5.3 %collective-permute-start.14 = (bf16[96,512]{1,0:T(8,128)(2,1)S(1)}, bf16[96,512]{1,0:T(8,128)(2,1)S(1)}, u32[]{:S(2)}, u32[]{:S(2)}) collective-permute-start(bf16[96,512]{1,0:T(8,128)(2,1)S(1)} %get-tuple-element.74), channel_id=1, source_target_pairs={{0,4},{4,0},{8,12},{12,8},{1,5},{5,1},{9,13},{13,9},{2,6},{6,2},{1... | collective-permute-start | bytes 294920 | tf_op jit(solution)/shard_map/ppermute | solution.py:550
  45.0 11.6 %collective-permute-start.15 = (bf16[96,512]{1,0:T(8,128)(2,1)S(1)}, bf16[96,512]{1,0:T(8,128)(2,1)S(1)}, u32[]{:S(2)}, u32[]{:S(2)}) collective-permute-start(bf16[96,512]{1,0:T(8,128)(2,1)S(1)} %get-tuple-element.75), channel_id=1, source_target_pairs={{0,8},{4,12},{8,0},{12,4},{1,9},{5,13},{9,1},{13,5},{2,10},{6,14},... | collective-permute-start | bytes 294920 | tf_op jit(solution)/shard_map/ppermute | solution.py:550
  48.8 7.8 %collective-permute-start.16 = (bf16[96,512]{1,0:T(8,128)(2,1)S(1)}, bf16[96,512]{1,0:T(8,128)(2,1)S(1)}, u32[]{:S(2)}, u32[]{:S(2)}) collective-permute-start(bf16[96,512]{1,0:T(8,128)(2,1)S(1)} %get-tuple-element.76), channel_id=1, source_target_pairs={{0,12},{4,8},{8,4},{12,0},{1,13},{5,9},{9,5},{13,1},{2,14},{6,10},... | collective-permute-start | bytes 294920 | tf_op jit(solution)/shard_map/ppermute | solution.py:550
  49.5 7.5 %collective-permute-start.13 = (bf16[256,512]{1,0:T(8,128)(2,1)S(1)}, bf16[256,512]{1,0:T(8,128)(2,1)S(1)}, u32[]{:S(2)}, u32[]{:S(2)}) collective-permute-start(bf16[256,512]{1,0:T(8,128)(2,1)S(1)} %get-tuple-element.73), channel_id=1, source_target_pairs={{0,1},{1,0},{2,3},{3,2},{4,5},{5,4},{6,7},{7,6},{8,9},{9,8},{10,11... | collective-permute-start | bytes 786440 | tf_op jit(solution)/shard_map/ppermute | solution.py:601

commit v8 on v7

--- a/solution.py
+++ b/solution.py
@@ -51,6 +51,8 @@
     rows, width = x_buf.shape
     kv_cols = w_buf.shape[1] // 2
     depth = width // parts
+    docs = pltpu.make_async_copy(seg_hbm, seg_ref, sem.at[3 * parts])
+    docs.start()
     copies = []
     for i in range(parts):
         at = pl.ds(i * depth, depth)
@@ -61,8 +63,6 @@
         ])
         for copy in copies[-1]:
             copy.start()
-    docs = pltpu.make_async_copy(seg_hbm, seg_ref, sem.at[3 * parts])
-    docs.start()
     first = (lax.axis_index("ctx") * 2 + lax.axis_index("rep")) * rows
     lane = lax.broadcasted_iota(jnp.int32, (1, HD), 1)
     freq = jnp.exp(lax.rem(lane, HD // 2).astype(F32) * (-2.0 * math.log(THETA) / HD))
@@ -70,13 +70,6 @@
     angle = pos * freq
     tab_ref[:, :HD] = jnp.cos(angle)
     tab_ref[:, HD:] = jnp.where(lane < HD // 2, -1.0, 1.0) * jnp.sin(angle)
-    docs.wait()
-    line = lax.broadcasted_iota(jnp.int32, (16, kv_cols), 0)
-    segs = jnp.zeros((16, kv_cols), F32)
-    for i in range(rows // kv_cols):
-        segs = jnp.where(line == i, seg_ref[:, i * kv_cols:(i + 1) * kv_cols].astype(F32), segs)
-    kv_ref[rows:, :kv_cols] = segs.astype(BF16)
-    kv_ref[rows:, kv_cols:] = jnp.zeros((16, kv_cols), BF16)
     total = None
     for i in range(parts):
         for copy in copies[i]:
@@ -87,6 +80,13 @@
     for at in range(0, kv_cols, HD):
         kv_ref[0:rows, at:at + HD] = norm_rope(total[:, at:at + HD], tab_ref[:, :HD], tab_ref[:, HD:], 1.0)
     kv_ref[0:rows, kv_cols:] = total[:, kv_cols:].astype(BF16)
+    docs.wait()
+    line = lax.broadcasted_iota(jnp.int32, (16, kv_cols), 0)
+    segs = jnp.zeros((16, kv_cols), F32)
+    for i in range(rows // kv_cols):
+        segs = jnp.where(line == i, seg_ref[:, i * kv_cols:(i + 1) * kv_cols].astype(F32), segs)
+    kv_ref[rows:, :kv_cols] = segs.astype(BF16)
+    kv_ref[rows:, kv_cols:] = jnp.zeros((16, kv_cols), BF16)
 
 
 def q_kernel(parts, x_hbm, w_hbm, tab_ref, q_ref, x_ref, w_buf, sem):

time: 58.4 us -> 58.1 us (level)
  no operation moved by 1% of the time
where the time goes in v8:
time: 58.1 us; the launch traced here: 57.7 us
  starting transfers between devices  20.8 us (36%)
  Pallas kernels  20.6 us (35%)
  waiting for transfers between devices  16.1 us (28%)
    ppermute x6, starting transfers between devices, across(): lax.ppermute(xs[k], 'ctx', [(i, i ^ k) for i in range(ctx)])  11.7 us
    ppermute x6, waiting for transfers between devices, across(): lax.ppermute(xs[k], 'ctx', [(i, i ^ k) for i in range(ctx)])  7.07 us
    pallas_call x1, Pallas kernels, local(): pl.pallas_call(functools.partial(q_kernel, parts), in_specs=[ANY, ANY, VM...  5.43 us
    pallas_call x2, Pallas kernels, project_some(): pl.pallas_call(functools.partial(project_kernel, steps), in_specs=[VMEM,...  5.36 us
    ppermute x2, waiting for transfers between devices, to_heads(): lax.ppermute(x, 'head', flip)  3.98 us
    ppermute x1, starting transfers between devices, local(): hop = [own, lax.ppermute(own, 'ctx', up)]  3.09 us
    ppermute x1, waiting for transfers between devices, local(): hop = [own, lax.ppermute(own, 'ctx', up)]  2.94 us
    pallas_call x1, Pallas kernels, local(): pl.pallas_call(functools.partial(kv_kernel, parts), in_specs=[ANY, ANY, A...  2.87 us
  transfers between devices with their start and end apart: 17, of which 7 were waited for; matrix products, arithmetic and copies ran while one was open for 0% of the time, Pallas kernels for 25%

profile of v8, /device:TPU:0, one launch (start us, length us, event | category | flops | bytes accessed | tf_op | source)
XLA Modules:
  0.0 57.7 jit_solution(16812646912126563737)
XLA Ops:
  0.0 2.9 %keys_values.1 = (bf16[272,512]{1,0:T(8,128)(2,1)S(1)}, f32[256,256]{1,0:T(8,128)S(1)}) custom-call(bf16[256,2048]{1,0:T(8,128)(2,1)} %x_hbm.3, bf16[2048,256]{1,0:T(8,128)(2,1)} %wk_hbm.1, bf16[2048,256]{1,0:T(8,128)(2,1)} %wv_hbm.1, s32[1,256]{1,0:T(1,128)} %bitcast.2), custom_call_target="tpu_custom_call" | custom-call | flops 536870912 | bytes 3145728 | tf_op jit(solution)/shard_map/keys_values/pallas_call | solution.py:424
  2.9 3.1 %collective-permute-start.1 = (bf16[272,512]{1,0:T(8,128)(2,1)S(1)}, bf16[272,512]{1,0:T(8,128)(2,1)S(1)}, u32[]{:S(2)}, u32[]{:S(2)}) collective-permute-start(bf16[272,512]{1,0:T(8,128)(2,1)S(1)} %get-tuple-element.46.refs_0_), channel_id=1, source_target_pairs={{0,4},{4,8},{8,12},{12,0},{1,5},{5,9},{9,13},{13,1},{2,6},{6,10},{... | collective-permute-start | bytes 835592 | tf_op jit(solution)/shard_map/ppermute | solution.py:440
  6.0 5.4 %queries.1.q_ref = bf16[16,256,128]{2,1,0:T(8,128)(2,1)S(1)} custom-call(bf16[256,2048]{1,0:T(8,128)(2,1)} %x_hbm.3, bf16[2048,2048]{1,0:T(8,128)(2,1)} %w_hbm.4, f32[256,256]{1,0:T(8,128)S(1)} %get-tuple-element.41.tab_ref), custom_call_target="tpu_custom_call" | custom-call | flops 2147483648 | bytes 9437184 | tf_op jit(solution)/shard_map/queries/pallas_call | solution.py:443
  11.4 0.3 routes.1
  11.7 2.9 %collective-permute-done.1.refs_1_ = bf16[272,512]{1,0:T(8,128)(2,1)S(1)} collective-permute-done((bf16[272,512]{1,0:T(8,128)(2,1)S(1)}, bf16[272,512]{1,0:T(8,128)(2,1)S(1)}, u32[]{:S(2)}, u32[]{:S(2)}) %collective-permute-start.1) | collective-permute-done | bytes 278560 | tf_op jit(solution)/shard_map/ppermute | solution.py:440
  14.6 0.7 %collective-permute-start.2 = (bf16[272,512]{1,0:T(8,128)(2,1)S(1)}, bf16[272,512]{1,0:T(8,128)(2,1)S(1)}, u32[]{:S(2)}, u32[]{:S(2)}) collective-permute-start(bf16[272,512]{1,0:T(8,128)(2,1)S(1)} %collective-permute-done.1.refs_1_), channel_id=1, source_target_pairs={{4,8},{8,12},{5,9},{9,13},{6,10},{10,14},{7,11},{11,15},{20,24},{2... | collective-permute-start | bytes 835592 | tf_op jit(solution)/shard_map/ppermute | solution.py:466
  15.4 0.5 collective-permute-start.4
  15.9 1.5 %even_attention.1.refs_2_ = f32[16,256,256]{2,1,0:T(8,128)S(1)} custom-call(s32[1,256]{1,0:T(1,128)S(1)} %bitcast.3, bf16[16,256,128]{2,1,0:T(8,128)(2,1)S(1)} %queries.1.q_ref, bf16[272,512]{1,0:T(8,128)(2,1)S(1)} %get-tuple-element.46.refs_0_, bf16[272,512]{1,0:T(8,128)(2,1)S(1)} %collective-permute-done.1.refs_1_), custom_call_target="tpu_custom_call" | custom-call | tf_op jit(solution)/shard_map/even_attention/pallas_call | solution.py:481
  17.5 0.2 odd_attention.1.near_ref
  17.7 1.9 %collective-permute-start.5 = (bf16[272,512]{1,0:T(8,128)(2,1)S(1)}, bf16[272,512]{1,0:T(8,128)(2,1)S(1)}, u32[]{:S(2)}, u32[]{:S(2)}) collective-permute-start(bf16[272,512]{1,0:T(8,128)(2,1)S(1)} %collective-permute-done.2.far_ref), channel_id=1, source_target_pairs={{0,1},{1,0},{2,3},{3,2},{4,5},{5,4},{6,7},{7,6},{8,9},{9,8},{10,11... | collective-permute-start | bytes 835592 | tf_op jit(solution)/shard_map/ppermute | solution.py:506
  19.7 1.1 %collective-permute-done.pair_slots = f32[32,128]{1,0:T(8,128)S(1)} collective-permute-done((f32[32,128]{1,0:T(8,128)S(1)}, f32[32,128]{1,0:T(8,128)S(1)}, u32[]{:S(2)}, u32[]{:S(2)}) %collective-permute-start) | collective-permute-done | bytes 16416 | tf_op jit(solution)/shard_map/ppermute | solution.py:492
  20.8 2.3 %far_attention_project.1 = (bf16[256,2048]{1,0:T(8,128)(2,1)S(1)}, bf16[256,512]{1,0:T(8,128)(2,1)S(1)}) custom-call(s32[1,256]{1,0:T(1,128)S(1)} %bitcast.5, bf16[16,256,128]{2,1,0:T(8,128)(2,1)S(1)} %queries.1.q_ref, bf16[272,512]{1,0:T(8,128)(2,1)S(1)} %collective-permute-done.2.far_ref, bf16[264,512]{1,0:T(8,128)(2,1)S(1)} %collective-permute-done.4.refs_1_.to_one, ...), custom_call_target="tpu_custom_call" | custom-call | flops 1610612736 | bytes 10485760 | tf_op jit(solution)/shard_map/far_attention_project/pallas_call | solution.py:509
  23.1 1.6 %collective-permute-start.6 = (bf16[256,512]{1,0:T(8,128)(2,1)S(1)}, bf16[256,512]{1,0:T(8,128)(2,1)S(1)}, u32[]{:S(2)}, u32[]{:S(2)}) collective-permute-start(bf16[256,512]{1,0:T(8,128)(2,1)S(1)} %get-tuple-element.60), channel_id=1, source_target_pairs={{0,2},{2,0},{1,3},{3,1},{4,6},{6,4},{5,7},{7,5},{8,10},{10,8},{9,1... | collective-permute-start | bytes 786440 | tf_op jit(solution)/shard_map/ppermute | solution.py:536
  24.7 3.1 %project.2 = (bf16[256,512]{1,0:T(8,128)(2,1)S(1)}, bf16[256,512]{1,0:T(8,128)(2,1)S(1)}) custom-call(bf16[256,2048]{1,0:T(8,128)(2,1)S(1)} %get-tuple-element.66.att_ref, bf16[2048,2048]{1,0:T(8,128)(2,1)} %w_hbm.7), custom_call_target="tpu_custom_call" | custom-call | flops 20000000000 | tf_op jit(solution)/shard_map/project/pallas_call | solution.py:522
  27.8 0.6 %collective-permute-start.7 = (bf16[256,512]{1,0:T(8,128)(2,1)S(1)}, bf16[256,512]{1,0:T(8,128)(2,1)S(1)}, u32[]{:S(2)}, u32[]{:S(2)}) collective-permute-start(bf16[256,512]{1,0:T(8,128)(2,1)S(1)} %get-tuple-element.53), channel_id=1, source_target_pairs={{0,2},{2,0},{1,3},{3,1},{4,6},{6,4},{5,7},{7,5},{8,10},{10,8},{9,1... | collective-permute-start | bytes 786440 | tf_op jit(solution)/shard_map/ppermute | solution.py:536
  28.4 4.0 %collective-permute-done.6.refs_5_ = bf16[256,512]{1,0:T(8,128)(2,1)S(1)} collective-permute-done((bf16[256,512]{1,0:T(8,128)(2,1)S(1)}, bf16[256,512]{1,0:T(8,128)(2,1)S(1)}, u32[]{:S(2)}, u32[]{:S(2)}) %collective-permute-start.6) | collective-permute-done | bytes 262176 | tf_op jit(solution)/shard_map/ppermute | solution.py:536
  32.3 0.3 add_pick.1
  32.6 3.8 %collective-permute-start.10 = (bf16[104,512]{1,0:T(8,128)(2,1)S(1)}, bf16[104,512]{1,0:T(8,128)(2,1)S(1)}, u32[]{:S(2)}, u32[]{:S(2)}) collective-permute-start(bf16[104,512]{1,0:T(8,128)(2,1)S(1)} %get-tuple-element.62), channel_id=1, source_target_pairs={{0,4},{4,0},{8,12},{12,8},{1,5},{5,1},{9,13},{13,9},{2,6},{6,2},{1... | collective-permute-start | bytes 319496 | tf_op jit(solution)/shard_map/ppermute | solution.py:550
  36.4 3.4 %collective-permute-start.11 = (bf16[104,512]{1,0:T(8,128)(2,1)S(1)}, bf16[104,512]{1,0:T(8,128)(2,1)S(1)}, u32[]{:S(2)}, u32[]{:S(2)}) collective-permute-start(bf16[104,512]{1,0:T(8,128)(2,1)S(1)} %get-tuple-element.63), channel_id=1, source_target_pairs={{0,8},{4,12},{8,0},{12,4},{1,9},{5,13},{9,1},{13,5},{2,10},{6,14},... | collective-permute-start | bytes 319496 | tf_op jit(solution)/shard_map/ppermute | solution.py:550
  39.8 2.3 %project.3.refs_0_ = bf16[256,512]{1,0:T(8,128)(2,1)S(1)} custom-call(bf16[256,2048]{1,0:T(8,128)(2,1)S(1)} %get-tuple-element.66.att_ref, bf16[2048,2048]{1,0:T(8,128)(2,1)} %w_hbm.7), custom_call_target="tpu_custom_call" | custom-call | flops 20000000000 | tf_op jit(solution)/shard_map/project/pallas_call | solution.py:522
  42.2 0.3 add_split.1
  42.5 0.2 collective-permute-start.8
  42.7 0.4 collective-permute-start.9
  43.1 0.8 %collective-permute-done.8.refs_0_ = bf16[96,512]{1,0:T(8,128)(2,1)S(1)} collective-permute-done((bf16[96,512]{1,0:T(8,128)(2,1)S(1)}, bf16[96,512]{1,0:T(8,128)(2,1)S(1)}, u32[]{:S(2)}, u32[]{:S(2)}) %collective-permute-start.8) | collective-permute-done | bytes 98336 | tf_op jit(solution)/shard_map/ppermute | solution.py:578
  43.9 0.2 collective-permute-done.9.refs_1_
  44.0 0.6 %collective-permute-start.14 = (bf16[96,512]{1,0:T(8,128)(2,1)S(1)}, bf16[96,512]{1,0:T(8,128)(2,1)S(1)}, u32[]{:S(2)}, u32[]{:S(2)}) collective-permute-start(bf16[96,512]{1,0:T(8,128)(2,1)S(1)} %get-tuple-element.74), channel_id=1, source_target_pairs={{0,4},{4,0},{8,12},{12,8},{1,5},{5,1},{9,13},{13,9},{2,6},{6,2},{1... | collective-permute-start | bytes 294920 | tf_op jit(solution)/shard_map/ppermute | solution.py:550
  44.7 3.8 %collective-permute-start.15 = (bf16[96,512]{1,0:T(8,128)(2,1)S(1)}, bf16[96,512]{1,0:T(8,128)(2,1)S(1)}, u32[]{:S(2)}, u32[]{:S(2)}) collective-permute-start(bf16[96,512]{1,0:T(8,128)(2,1)S(1)} %get-tuple-element.75), channel_id=1, source_target_pairs={{0,8},{4,12},{8,0},{12,4},{1,9},{5,13},{9,1},{13,5},{2,10},{6,14},... | collective-permute-start | bytes 294920 | tf_op jit(solution)/shard_map/ppermute | solution.py:550
  48.5 0.7 %place.1 = (bf16[256,512]{1,0:T(8,128)(2,1)S(1)}, bf16[256,512]{1,0:T(8,128)(2,1)S(1)}) custom-call(bf16[104,512]{1,0:T(8,128)(2,1)S(1)} %get-tuple-element.71.refs_0_, bf16[104,512]{1,0:T(8,128)(2,1)S(1)} %collective-permute-done.10.refs_1_, bf16[104,512]{1,0:T(8,128)(2,1)S(1)} %collective-permute-done.11.refs_2_, ...), custom_call_target="tpu_custom_call" | custom-call | flops 20000000000 | tf_op jit(solution)/shard_map/place/pallas_call | solution.py:592
  49.3 2.5 %collective-permute-done.14.refs_5_ = bf16[96,512]{1,0:T(8,128)(2,1)S(1)} collective-permute-done((bf16[96,512]{1,0:T(8,128)(2,1)S(1)}, bf16[96,512]{1,0:T(8,128)(2,1)S(1)}, u32[]{:S(2)}, u32[]{:S(2)}) %collective-permute-start.14) | collective-permute-done | bytes 98336 | tf_op jit(solution)/shard_map/ppermute | solution.py:550
  51.8 4.5 %collective-permute-done.15.refs_6_ = bf16[96,512]{1,0:T(8,128)(2,1)S(1)} collective-permute-done((bf16[96,512]{1,0:T(8,128)(2,1)S(1)}, bf16[96,512]{1,0:T(8,128)(2,1)S(1)}, u32[]{:S(2)}, u32[]{:S(2)}) %collective-permute-start.15) | collective-permute-done | bytes 98336 | tf_op jit(solution)/shard_map/ppermute | solution.py:550
  56.4 0.4 place_rest.1.rest_ref
  56.8 0.9 %join.1 = bf16[256,1024]{1,0:T(8,128)(2,1)} custom-call(bf16[256,512]{1,0:T(8,128)(2,1)S(1)} %get-tuple-element.72.mine_ref, bf16[256,512]{1,0:T(8,128)(2,1)S(1)} %collective-permute-done.13.pair_ref, bf16[256,512]{1,0:T(8,128)(2,1)S(1)} %place_rest.1.rest_ref), custom_call_target="tpu_custom_call" | custom-call | tf_op jit(solution)/shard_map/join/pallas_call | solution.py:613
  (21 shorter events, 0.3 us)
Async XLA Ops:
  0.0 15.9 %copy-start = (s32[256]{0:T(256)S(1)}, s32[256]{0:T(256)}, u32[]{:S(2)}) copy-start(s32[256]{0:T(256)} %param.8) | copy-start | bytes 3076
  0.0 11.4 %copy-start.1 = (s32[256]{0:T(256)S(1)}, s32[256]{0:T(256)}, u32[]{:S(2)}) copy-start(s32[256]{0:T(256)} %param.9) | copy-start | bytes 3076
  2.9 11.8 %collective-permute-start.1 = (bf16[272,512]{1,0:T(8,128)(2,1)S(1)}, bf16[272,512]{1,0:T(8,128)(2,1)S(1)}, u32[]{:S(2)}, u32[]{:S(2)}) collective-permute-start(bf16[272,512]{1,0:T(8,128)(2,1)S(1)} %get-tuple-element.46.refs_0_), channel_id=1, source_target_pairs={{0,4},{4,8},{8,12},{12,0},{1,5},{5,9},{9,13},{13,1},{2,6},{6,10},{... | collective-permute-start | bytes 835592 | tf_op jit(solution)/shard_map/ppermute | solution.py:440
  14.6 3.0 %collective-permute-start.2 = (bf16[272,512]{1,0:T(8,128)(2,1)S(1)}, bf16[272,512]{1,0:T(8,128)(2,1)S(1)}, u32[]{:S(2)}, u32[]{:S(2)}) collective-permute-start(bf16[272,512]{1,0:T(8,128)(2,1)S(1)} %collective-permute-done.1.refs_1_), channel_id=1, source_target_pairs={{4,8},{8,12},{5,9},{9,13},{6,10},{10,14},{7,11},{11,15},{20,24},{2... | collective-permute-start | bytes 835592 | tf_op jit(solution)/shard_map/ppermute | solution.py:466
  15.4 2.1 %collective-permute-start.3 = (bf16[264,512]{1,0:T(8,128)(2,1)S(1)}, bf16[264,512]{1,0:T(8,128)(2,1)S(1)}, u32[]{:S(2)}, u32[]{:S(2)}) collective-permute-start(bf16[264,512]{1,0:T(8,128)(2,1)S(1)} %get-tuple-element.48), channel_id=1, source_target_pairs={{0,1},{1,0},{2,3},{3,2},{4,5},{5,4},{6,7},{7,6},{8,9},{9,8},{10,11... | collective-permute-start | bytes 811016 | tf_op jit(solution)/shard_map/ppermute | solution.py:493
  15.4 2.1 %collective-permute-start.4 = (bf16[264,512]{1,0:T(8,128)(2,1)S(1)}, bf16[264,512]{1,0:T(8,128)(2,1)S(1)}, u32[]{:S(2)}, u32[]{:S(2)}) collective-permute-start(bf16[264,512]{1,0:T(8,128)(2,1)S(1)} %get-tuple-element.49), channel_id=1, source_target_pairs={{0,1},{1,0},{2,3},{3,2},{4,5},{5,4},{6,7},{7,6},{8,9},{9,8},{10,11... | collective-permute-start | bytes 811016 | tf_op jit(solution)/shard_map/ppermute | solution.py:493
  17.7 3.1 %collective-permute-start.5 = (bf16[272,512]{1,0:T(8,128)(2,1)S(1)}, bf16[272,512]{1,0:T(8,128)(2,1)S(1)}, u32[]{:S(2)}, u32[]{:S(2)}) collective-permute-start(bf16[272,512]{1,0:T(8,128)(2,1)S(1)} %collective-permute-done.2.far_ref), channel_id=1, source_target_pairs={{0,1},{1,0},{2,3},{3,2},{4,5},{5,4},{6,7},{7,6},{8,9},{9,8},{10,11... | collective-permute-start | bytes 835592 | tf_op jit(solution)/shard_map/ppermute | solution.py:506
  19.6 1.2 %collective-permute-start = (f32[32,128]{1,0:T(8,128)S(1)}, f32[32,128]{1,0:T(8,128)S(1)}, u32[]{:S(2)}, u32[]{:S(2)}) collective-permute-start(f32[32,128]{1,0:T(8,128)S(1)} %get-tuple-element.44), channel_id=1, source_target_pairs={{0,1},{1,0},{2,3},{3,2},{4,5},{5,4},{6,7},{7,6},{8,9},{9,8},{10,11... | collective-permute-start | bytes 49160 | tf_op jit(solution)/shard_map/ppermute | solution.py:492
  23.1 9.2 %collective-permute-start.6 = (bf16[256,512]{1,0:T(8,128)(2,1)S(1)}, bf16[256,512]{1,0:T(8,128)(2,1)S(1)}, u32[]{:S(2)}, u32[]{:S(2)}) collective-permute-start(bf16[256,512]{1,0:T(8,128)(2,1)S(1)} %get-tuple-element.60), channel_id=1, source_target_pairs={{0,2},{2,0},{1,3},{3,1},{4,6},{6,4},{5,7},{7,5},{8,10},{10,8},{9,1... | collective-permute-start | bytes 786440 | tf_op jit(solution)/shard_map/ppermute | solution.py:536
  27.8 14.4 %collective-permute-start.7 = (bf16[256,512]{1,0:T(8,128)(2,1)S(1)}, bf16[256,512]{1,0:T(8,128)(2,1)S(1)}, u32[]{:S(2)}, u32[]{:S(2)}) collective-permute-start(bf16[256,512]{1,0:T(8,128)(2,1)S(1)} %get-tuple-element.53), channel_id=1, source_target_pairs={{0,2},{2,0},{1,3},{3,1},{4,6},{6,4},{5,7},{7,5},{8,10},{10,8},{9,1... | collective-permute-start | bytes 786440 | tf_op jit(solution)/shard_map/ppermute | solution.py:536
  32.6 15.9 %collective-permute-start.10 = (bf16[104,512]{1,0:T(8,128)(2,1)S(1)}, bf16[104,512]{1,0:T(8,128)(2,1)S(1)}, u32[]{:S(2)}, u32[]{:S(2)}) collective-permute-start(bf16[104,512]{1,0:T(8,128)(2,1)S(1)} %get-tuple-element.62), channel_id=1, source_target_pairs={{0,4},{4,0},{8,12},{12,8},{1,5},{5,1},{9,13},{13,9},{2,6},{6,2},{1... | collective-permute-start | bytes 319496 | tf_op jit(solution)/shard_map/ppermute | solution.py:550
  36.4 12.1 %collective-permute-start.11 = (bf16[104,512]{1,0:T(8,128)(2,1)S(1)}, bf16[104,512]{1,0:T(8,128)(2,1)S(1)}, u32[]{:S(2)}, u32[]{:S(2)}) collective-permute-start(bf16[104,512]{1,0:T(8,128)(2,1)S(1)} %get-tuple-element.63), channel_id=1, source_target_pairs={{0,8},{4,12},{8,0},{12,4},{1,9},{5,13},{9,1},{13,5},{2,10},{6,14},... | collective-permute-start | bytes 319496 | tf_op jit(solution)/shard_map/ppermute | solution.py:550
  39.8 8.7 %collective-permute-start.12 = (bf16[104,512]{1,0:T(8,128)(2,1)S(1)}, bf16[104,512]{1,0:T(8,128)(2,1)S(1)}, u32[]{:S(2)}, u32[]{:S(2)}) collective-permute-start(bf16[104,512]{1,0:T(8,128)(2,1)S(1)} %get-tuple-element.64), channel_id=1, source_target_pairs={{0,12},{4,8},{8,4},{12,0},{1,13},{5,9},{9,5},{13,1},{2,14},{6,10},... | collective-permute-start | bytes 319496 | tf_op jit(solution)/shard_map/ppermute | solution.py:550
  42.5 1.4 %collective-permute-start.8 = (bf16[96,512]{1,0:T(8,128)(2,1)S(1)}, bf16[96,512]{1,0:T(8,128)(2,1)S(1)}, u32[]{:S(2)}, u32[]{:S(2)}) collective-permute-start(bf16[96,512]{1,0:T(8,128)(2,1)S(1)} %get-tuple-element.68), channel_id=1, source_target_pairs={{0,1},{1,0},{2,3},{3,2},{4,5},{5,4},{6,7},{7,6},{8,9},{9,8},{10,11... | collective-permute-start | bytes 294920 | tf_op jit(solution)/shard_map/ppermute | solution.py:578
  42.7 1.3 %collective-permute-start.9 = (bf16[96,512]{1,0:T(8,128)(2,1)S(1)}, bf16[96,512]{1,0:T(8,128)(2,1)S(1)}, u32[]{:S(2)}, u32[]{:S(2)}) collective-permute-start(bf16[96,512]{1,0:T(8,128)(2,1)S(1)} %get-tuple-element.69), channel_id=1, source_target_pairs={{0,1},{1,0},{2,3},{3,2},{4,5},{5,4},{6,7},{7,6},{8,9},{9,8},{10,11... | collective-permute-start | bytes 294920 | tf_op jit(solution)/shard_map/ppermute | solution.py:578
  44.0 7.8 %collective-permute-start.14 = (bf16[96,512]{1,0:T(8,128)(2,1)S(1)}, bf16[96,512]{1,0:T(8,128)(2,1)S(1)}, u32[]{:S(2)}, u32[]{:S(2)}) collective-permute-start(bf16[96,512]{1,0:T(8,128)(2,1)S(1)} %get-tuple-element.74), channel_id=1, source_target_pairs={{0,4},{4,0},{8,12},{12,8},{1,5},{5,1},{9,13},{13,9},{2,6},{6,2},{1... | collective-permute-start | bytes 294920 | tf_op jit(solution)/shard_map/ppermute | solution.py:550
  44.7 11.7 %collective-permute-start.15 = (bf16[96,512]{1,0:T(8,128)(2,1)S(1)}, bf16[96,512]{1,0:T(8,128)(2,1)S(1)}, u32[]{:S(2)}, u32[]{:S(2)}) collective-permute-start(bf16[96,512]{1,0:T(8,128)(2,1)S(1)} %get-tuple-element.75), channel_id=1, source_target_pairs={{0,8},{4,12},{8,0},{12,4},{1,9},{5,13},{9,1},{13,5},{2,10},{6,14},... | collective-permute-start | bytes 294920 | tf_op jit(solution)/shard_map/ppermute | solution.py:550
  48.5 7.8 %collective-permute-start.16 = (bf16[96,512]{1,0:T(8,128)(2,1)S(1)}, bf16[96,512]{1,0:T(8,128)(2,1)S(1)}, u32[]{:S(2)}, u32[]{:S(2)}) collective-permute-start(bf16[96,512]{1,0:T(8,128)(2,1)S(1)} %get-tuple-element.76), channel_id=1, source_target_pairs={{0,12},{4,8},{8,4},{12,0},{1,13},{5,9},{9,5},{13,1},{2,14},{6,10},... | collective-permute-start | bytes 294920 | tf_op jit(solution)/shard_map/ppermute | solution.py:550
  49.2 7.6 %collective-permute-start.13 = (bf16[256,512]{1,0:T(8,128)(2,1)S(1)}, bf16[256,512]{1,0:T(8,128)(2,1)S(1)}, u32[]{:S(2)}, u32[]{:S(2)}) collective-permute-start(bf16[256,512]{1,0:T(8,128)(2,1)S(1)} %get-tuple-element.73), channel_id=1, source_target_pairs={{0,1},{1,0},{2,3},{3,2},{4,5},{5,4},{6,7},{7,6},{8,9},{9,8},{10,11... | collective-permute-start | bytes 786440 | tf_op jit(solution)/shard_map/ppermute | solution.py:601
